TPU v7x, 32 devices: a whole 2x2x4 slice. The times are simulated.
32 devices in a mesh: dp: 8 (over z, y), tensor: 4 (over x, core).
Axes of the slice: x: 2, y: 2, z: 4, core: 2. Of those that a mesh axis runs over, the one named last changes fastest.
Arguments:
- tokens: bfloat16 [8192, 1024], P(('dp', 'tensor')), may hold values from -6 to 6
- segment_ids: int32 [8, 1024], P('dp'), may hold values from 0 to 5, as said below
- positions: int32 [8, 1024], P('dp'), may hold values from 0 to 1023, as said below
- w_query: bfloat16 [1024, 2048], P('dp', 'tensor'), may hold values from -0.1875 to 0.1875
- key_projection: bfloat16 [1024, 1024], P('dp', 'tensor'), may hold values from -0.1875 to 0.1875
- value_projection: bfloat16 [1024, 1024], P('dp', 'tensor'), may hold values from -0.1875 to 0.1875
- w_out: bfloat16 [2048, 1024], P('tensor', 'dp'), may hold values from -0.5 to 0.5
- w_gate: bfloat16 [1024, 3072], P('dp', 'tensor'), may hold values from -0.1875 to 0.1875
- w_up: bfloat16 [1024, 3072], P('dp', 'tensor'), may hold values from -0.1875 to 0.1875
- w_down: bfloat16 [3072, 1024], P('tensor', 'dp'), may hold values from -0.109375 to 0.109375
- gain_attn: bfloat16 [1024], P('dp'), may hold values from 0.5 to 1.5
- gain_mlp: bfloat16 [1024], P('dp'), may hold values from 0.5 to 1.5
- gain_query: bfloat16 [128], P('dp'), may hold values from 0.5 to 1.5
- gain_key: bfloat16 [128], P('dp'), may hold values from 0.5 to 1.5
- cotangent: bfloat16 [8192, 1024], P(('dp', 'tensor')), may hold values from -6 to 6
Outputs:
- activations: bfloat16 [8192, 1024], P(('dp', 'tensor'))
- d_tokens: float32 [8192, 1024], P(('dp', 'tensor'))
- grad_query: float32 [1024, 2048], P('dp', 'tensor')
- grad_key: float32 [1024, 1024], P('dp', 'tensor')
- grad_value: float32 [1024, 1024], P('dp', 'tensor')
- grad_out: float32 [2048, 1024], P('tensor', 'dp')
- grad_gate: float32 [1024, 3072], P('dp', 'tensor')
- grad_up: float32 [1024, 3072], P('dp', 'tensor')
- grad_down: float32 [3072, 1024], P('tensor', 'dp')
- grad_gain_attn: float32 [1024], P('dp')
- grad_gain_mlp: float32 [1024], P('dp')
- grad_gain_query: float32 [128], P('dp')
- grad_gain_key: float32 [128], P('dp')
Inputs may be any that keep to these rules, and one draw needn't show every extreme that they name: `segment_ids`: within each sequence the document number starts at 0 and rises by one at each new document; a document holds 200 to 2000 tokens (never more than 1024), except the last of a sequence, which may be cut short at the sequence's end. The largest number is reached in every draw. `positions`: the offset of each token from the first token of its document.
All inputs are finite; a program needn't handle non-finite values.
Results may differ from a plain program's by a relative error of at most 0.02.
Values may be sent and summed in bfloat16 or wider, within the bound.
No kernel may reach another device: no remote copies, remote signals or barrier semaphores. Data moves between devices by JAX's collectives and lax.ppermute only.
A program may use at most 128 MiB of HBM per device.

v0:
```python
import jax
import jax.numpy as jnp
from jax import lax
from jax.sharding import PartitionSpec as P

HEAD_SIZE = 128


epsilon = 1e-06
rope_base = 1000000.0
masked_score = -1e30


def rms_scale(values, row_gain):
    return (
        values * lax.rsqrt(jnp.mean(values * values, axis=-1, keepdims=True) + epsilon) * row_gain
    )


def rotate(values, cosine, sine):
    middle = values.shape[-1] // 2
    front_half = values[..., :middle]
    back_half = values[..., middle:]
    return jnp.concatenate(
        [front_half * cosine - back_half * sine, back_half * cosine + front_half * sine], axis=-1
    )


def rope_tables(offsets, width):
    frequency = rope_base ** (-(2.0 * jnp.arange(width // 2, dtype=jnp.float32)) / width)
    angles = offsets.astype(jnp.float32)[:, None] * frequency[None, :]
    return (jnp.cos(angles)[:, None, :], jnp.sin(angles)[:, None, :])


def swish_product(gate_in, up_in):
    return jax.nn.silu(gate_in) * up_in


def dot_rows(left, right):
    return lax.dot_general(
        left, right, (((0,), (0,)), ((), ())), preferred_element_type=jnp.float32
    )


def dot_back(left, right):
    return lax.dot_general(
        left, right, (((1,), (1,)), ((), ())), preferred_element_type=jnp.float32
    )


def row_slice(values, row_start, row_count):
    return lax.dynamic_slice_in_dim(values, row_start, row_count, 0)


def masked_scores(q_block, keys, seg_block, segments, row_start, score_scale):
    scores = (
        jnp.einsum("qkgd,skd->kgqs", q_block, keys, preferred_element_type=jnp.float32)
        * score_scale
    )
    row_ids = row_start + jnp.arange(q_block.shape[0], dtype=jnp.int32)
    col_ids = jnp.arange(keys.shape[0], dtype=jnp.int32)
    allowed = (seg_block[:, None] == segments[None, :]) & (col_ids[None, :] <= row_ids[:, None])
    return jnp.where(allowed, scores, masked_score)


def body(
    tokens,
    segment_ids,
    positions,
    w_query,
    key_projection,
    value_projection,
    w_out,
    w_gate,
    w_up,
    w_down,
    gain_attn,
    gain_mlp,
    gain_query,
    gain_key,
    cotangent,
):
    local_rows = tokens.shape[0]
    full_set = (
        lax.all_gather(w_query, "dp", axis=0, tiled=True),
        lax.all_gather(key_projection, "dp", axis=0, tiled=True),
        lax.all_gather(value_projection, "dp", axis=0, tiled=True),
        lax.all_gather(w_out, "dp", axis=1, tiled=True),
        lax.all_gather(w_gate, "dp", axis=0, tiled=True),
        lax.all_gather(w_up, "dp", axis=0, tiled=True),
        lax.all_gather(w_down, "dp", axis=1, tiled=True),
        lax.all_gather(gain_attn, "dp", axis=0, tiled=True),
        lax.all_gather(gain_mlp, "dp", axis=0, tiled=True),
        lax.all_gather(gain_query, "dp", axis=0, tiled=True),
        lax.all_gather(gain_key, "dp", axis=0, tiled=True),
    )
    query_mat, key_mat, value_mat, out_mat, gate_mat, up_mat, down_mat = full_set[:7]
    attn_norm_gain = full_set[7].astype(jnp.float32)
    mlp_norm_gain = full_set[8].astype(jnp.float32)
    query_norm_gain = full_set[9].astype(jnp.float32)
    key_norm_gain = full_set[10].astype(jnp.float32)
    segments = segment_ids[0]
    offsets = positions[0]
    seq_len = segments.shape[0]
    q_heads = query_mat.shape[1] // HEAD_SIZE
    kv_heads = key_mat.shape[1] // HEAD_SIZE
    query_group = q_heads // kv_heads
    block = min(512, seq_len)
    blocks = seq_len // block
    score_scale = HEAD_SIZE ** (-0.5)
    inputs = tokens.astype(jnp.float32)
    normed_local = rms_scale(inputs, attn_norm_gain).astype(jnp.bfloat16)
    normed_attn = lax.all_gather(normed_local, "tensor", axis=0, tiled=True)
    q_raw = jnp.dot(normed_attn, query_mat, preferred_element_type=jnp.float32).reshape(
        seq_len, q_heads, HEAD_SIZE
    )
    key_unrotated = jnp.dot(normed_attn, key_mat, preferred_element_type=jnp.float32).reshape(
        seq_len, kv_heads, HEAD_SIZE
    )
    value_projected = jnp.dot(normed_attn, value_mat, preferred_element_type=jnp.float32)
    cosine, sine = rope_tables(offsets, HEAD_SIZE)

    def prepare(q_in, k_in, gain_for_q, gain_for_k):
        return (
            rotate(rms_scale(q_in, gain_for_q), cosine, sine),
            rotate(rms_scale(k_in, gain_for_k), cosine, sine),
        )

    (q_rot, k_rot), prepare_back = jax.vjp(
        prepare, q_raw, key_unrotated, query_norm_gain, key_norm_gain
    )
    queries = q_rot.astype(jnp.bfloat16).reshape(seq_len, kv_heads, query_group, HEAD_SIZE)
    keys = k_rot.astype(jnp.bfloat16)
    values = value_projected.astype(jnp.bfloat16).reshape(seq_len, kv_heads, HEAD_SIZE)

    def forward_block(block_index):
        row_start = block_index * block
        q_block = row_slice(queries, row_start, block)
        seg_block = row_slice(segments, row_start, block)
        scores = masked_scores(q_block, keys, seg_block, segments, row_start, score_scale)
        row_peak = jnp.max(scores, axis=-1, keepdims=True)
        expd = jnp.exp(scores - row_peak)
        row_total = jnp.sum(expd, axis=-1, keepdims=True)
        attn_probs = (expd / row_total).astype(jnp.bfloat16)
        attended = jnp.einsum(
            "kgqs,skd->qkgd", attn_probs, values, preferred_element_type=jnp.float32
        )
        return (attended.astype(jnp.bfloat16), (row_peak + jnp.log(row_total))[..., 0])

    mixed_blocks, log_totals = lax.map(forward_block, jnp.arange(blocks, dtype=jnp.int32))
    mixed = mixed_blocks.reshape(seq_len, q_heads * HEAD_SIZE)
    attn_branch = lax.psum_scatter(
        jnp.dot(
            row_slice(mixed, jnp.int32(0), lax.axis_size("tensor") * local_rows),
            out_mat,
            preferred_element_type=jnp.float32,
        ),
        "tensor",
        scatter_dimension=0,
        tiled=True,
    )
    hidden = inputs + attn_branch
    normed_mlp_local = rms_scale(hidden, mlp_norm_gain).astype(jnp.bfloat16)
    normed_mlp = lax.all_gather(normed_mlp_local, "tensor", axis=0, tiled=True)
    gate_use, up_use, down_use = (gate_mat, up_mat, down_mat)
    gate = jnp.dot(normed_mlp, gate_use, preferred_element_type=jnp.float32)
    up_proj = jnp.dot(normed_mlp, up_use, preferred_element_type=jnp.float32)
    act = swish_product(gate, up_proj).astype(jnp.bfloat16)
    mlp_branch = lax.psum_scatter(
        jnp.dot(
            row_slice(act, jnp.int32(0), lax.axis_size("tensor") * local_rows),
            down_use,
            preferred_element_type=jnp.float32,
        ).astype(jnp.bfloat16),
        "tensor",
        scatter_dimension=0,
        tiled=True,
    ).astype(jnp.float32)
    activations = (hidden + mlp_branch).astype(jnp.bfloat16)
    back_set = (
        lax.all_gather(w_query, "dp", axis=0, tiled=True),
        lax.all_gather(key_projection, "dp", axis=0, tiled=True),
        lax.all_gather(value_projection, "dp", axis=0, tiled=True),
        lax.all_gather(w_out, "dp", axis=1, tiled=True),
        lax.all_gather(w_gate, "dp", axis=0, tiled=True),
        lax.all_gather(w_up, "dp", axis=0, tiled=True),
        lax.all_gather(w_down, "dp", axis=1, tiled=True),
        lax.all_gather(gain_attn, "dp", axis=0, tiled=True),
        lax.all_gather(gain_mlp, "dp", axis=0, tiled=True),
        lax.all_gather(gain_query, "dp", axis=0, tiled=True),
        lax.all_gather(gain_key, "dp", axis=0, tiled=True),
    )
    query_back, key_back, value_back, out_back = (
        back_set[0],
        back_set[1],
        back_set[2],
        back_set[3],
    )
    upstream = cotangent.astype(jnp.float32)
    grad_rows = lax.all_gather(cotangent, "tensor", axis=0, tiled=True)
    gate_back, up_back, down_back = (back_set[4], back_set[5], back_set[6])
    d_act = dot_back(grad_rows, down_back)
    grad_down = dot_rows(act, grad_rows)
    swish_values, swish_back = jax.vjp(swish_product, gate, up_proj)
    d_gate, d_up = swish_back(d_act)
    d_gate_low = d_gate.astype(jnp.bfloat16)
    d_up_low = d_up.astype(jnp.bfloat16)
    grad_gate = dot_rows(normed_mlp, d_gate_low)
    grad_up = dot_rows(normed_mlp, d_up_low)
    row_start = jnp.int32(0)
    d_normed_mlp = lax.psum_scatter(
        dot_back(row_slice(d_gate_low, row_start, lax.axis_size("tensor") * local_rows), gate_back)
        + dot_back(row_slice(d_up_low, row_start, lax.axis_size("tensor") * local_rows), up_back),
        "tensor",
        scatter_dimension=0,
        tiled=True,
    )
    norm_values, norm_mlp_back = jax.vjp(rms_scale, hidden, mlp_norm_gain)
    d_hidden_part, d_mlp_gain = norm_mlp_back(d_normed_mlp)
    d_hidden = upstream + d_hidden_part
    branch_low = d_hidden.astype(jnp.bfloat16)
    branch_rows = lax.all_gather(branch_low, "tensor", axis=0, tiled=True)
    grad_out = dot_rows(mixed, branch_rows)
    d_mixed = (
        dot_back(branch_rows, out_back)
        .astype(jnp.bfloat16)
        .reshape(seq_len, kv_heads, query_group, HEAD_SIZE)
    )

    def backward_block(totals, block_items):
        key_grad, value_grad = totals
        block_index, log_total = block_items
        row_start = block_index * block
        q_block = row_slice(queries, row_start, block)
        seg_block = row_slice(segments, row_start, block)
        grad_block = row_slice(d_mixed, row_start, block)
        scores = masked_scores(q_block, keys, seg_block, segments, row_start, score_scale)
        attn_probs = jnp.exp(scores - log_total[..., None])
        probs_low = attn_probs.astype(jnp.bfloat16)
        value_grad = value_grad + jnp.einsum(
            "kgqs,qkgd->skd", probs_low, grad_block, preferred_element_type=jnp.float32
        )
        d_probs = jnp.einsum(
            "qkgd,skd->kgqs", grad_block, values, preferred_element_type=jnp.float32
        )
        d_scores = attn_probs * (d_probs - jnp.sum(attn_probs * d_probs, axis=-1, keepdims=True))
        d_scores_low = d_scores.astype(jnp.bfloat16)
        d_q_block = (
            jnp.einsum("kgqs,skd->qkgd", d_scores_low, keys, preferred_element_type=jnp.float32)
            * score_scale
        )
        key_grad = (
            key_grad
            + jnp.einsum(
                "kgqs,qkgd->skd", d_scores_low, q_block, preferred_element_type=jnp.float32
            )
            * score_scale
        )
        return ((key_grad, value_grad), d_q_block)

    zero_keys = jnp.zeros((seq_len, kv_heads, HEAD_SIZE), jnp.float32)
    (d_keys, d_values), d_q_blocks = lax.scan(
        backward_block, (zero_keys, zero_keys), (jnp.arange(blocks, dtype=jnp.int32), log_totals)
    )
    d_queries = d_q_blocks.reshape(seq_len, q_heads, HEAD_SIZE)
    d_q_raw, d_k_raw, d_query_gain, d_key_gain = prepare_back((d_queries, d_keys))
    dq_low = d_q_raw.reshape(seq_len, q_heads * HEAD_SIZE).astype(jnp.bfloat16)
    dk_low = d_k_raw.reshape(seq_len, kv_heads * HEAD_SIZE).astype(jnp.bfloat16)
    dv_low = d_values.reshape(seq_len, kv_heads * HEAD_SIZE).astype(jnp.bfloat16)
    grad_query = dot_rows(normed_attn, dq_low)
    grad_key = dot_rows(normed_attn, dk_low)
    grad_value = dot_rows(normed_attn, dv_low)
    row_start = jnp.int32(0)
    part_query = dot_back(
        row_slice(dq_low, row_start, lax.axis_size("tensor") * local_rows), query_back
    )
    part_key = dot_back(
        row_slice(dk_low, row_start, lax.axis_size("tensor") * local_rows), key_back
    )
    part_value = dot_back(
        row_slice(dv_low, row_start, lax.axis_size("tensor") * local_rows), value_back
    )
    d_normed_attn = lax.psum_scatter(
        (part_query + part_key + part_value).astype(jnp.bfloat16),
        "tensor",
        scatter_dimension=0,
        tiled=True,
    ).astype(jnp.float32)
    norm_attn_values, norm_attn_back = jax.vjp(rms_scale, inputs, attn_norm_gain)
    d_inputs_part, d_attn_gain = norm_attn_back(d_normed_attn)
    d_tokens = d_hidden + d_inputs_part
    gain_totals = lax.psum((d_attn_gain, d_mlp_gain, d_query_gain, d_key_gain), "tensor")
    shards = (
        lax.psum_scatter(
            grad_query.astype(jnp.bfloat16), "dp", scatter_dimension=0, tiled=True
        ).astype(jnp.float32),
        lax.psum_scatter(
            grad_key.astype(jnp.bfloat16), "dp", scatter_dimension=0, tiled=True
        ).astype(jnp.float32),
        lax.psum_scatter(
            grad_value.astype(jnp.bfloat16), "dp", scatter_dimension=0, tiled=True
        ).astype(jnp.float32),
        lax.psum_scatter(
            grad_out.astype(jnp.bfloat16), "dp", scatter_dimension=1, tiled=True
        ).astype(jnp.float32),
        lax.psum_scatter(
            grad_gate.astype(jnp.bfloat16), "dp", scatter_dimension=0, tiled=True
        ).astype(jnp.float32),
        lax.psum_scatter(
            grad_up.astype(jnp.bfloat16), "dp", scatter_dimension=0, tiled=True
        ).astype(jnp.float32),
        lax.psum_scatter(
            grad_down.astype(jnp.bfloat16), "dp", scatter_dimension=1, tiled=True
        ).astype(jnp.float32),
        lax.psum_scatter(
            gain_totals[0].astype(jnp.bfloat16), "dp", scatter_dimension=0, tiled=True
        ).astype(jnp.float32),
        lax.psum_scatter(
            gain_totals[1].astype(jnp.bfloat16), "dp", scatter_dimension=0, tiled=True
        ).astype(jnp.float32),
        lax.psum_scatter(
            gain_totals[2].astype(jnp.bfloat16), "dp", scatter_dimension=0, tiled=True
        ).astype(jnp.float32),
        lax.psum_scatter(
            gain_totals[3].astype(jnp.bfloat16), "dp", scatter_dimension=0, tiled=True
        ).astype(jnp.float32),
    )
    return (
        activations,
        d_tokens,
        shards[0],
        shards[1],
        shards[2],
        shards[3],
        shards[4],
        shards[5],
        shards[6],
        shards[7],
        shards[8],
        shards[9],
        shards[10],
    )


def solution(mesh):
    return jax.shard_map(
        body,
        mesh=mesh,
        in_specs=(
            P(("dp", "tensor"), None),
            P("dp", None),
            P("dp", None),
            P("dp", "tensor"),
            P("dp", "tensor"),
            P("dp", "tensor"),
            P("tensor", "dp"),
            P("dp", "tensor"),
            P("dp", "tensor"),
            P("tensor", "dp"),
            P("dp"),
            P("dp"),
            P("dp"),
            P("dp"),
            P(("dp", "tensor"), None),
        ),
        out_specs=(
            P(("dp", "tensor"), None),
            P(("dp", "tensor"), None),
            P("dp", "tensor"),
            P("dp", "tensor"),
            P("dp", "tensor"),
            P("tensor", "dp"),
            P("dp", "tensor"),
            P("dp", "tensor"),
            P("tensor", "dp"),
            P("dp"),
            P("dp"),
            P("dp"),
            P("dp"),
        ),
        check_vma=False,
    )
```

profile of v0, /device:TPU:12, one launch (start us, length us, event | category | flops | bytes accessed | tf_op | source)
XLA Modules:
  0.0 1021.4 jit_solution(532979325443604231)
XLA Ops:
  9.0 14.4 %all-gather = bf16[8,1,128]{2,1,0:T(2,128)(2,1)S(1)} all-gather(bf16[1,1,128]{2,1,0:T(2,128)(2,1)} %bitcast.260), channel_id=1, replica_groups=mesh['dp'=8,'tensor'=4] {'dp'}, dimensions={0}, use_global_device_ids=true | all-gather | bytes 2304 | tf_op jit(solution)/shard_map/all_gather | solution.py:92
  28.9 21.4 %all-reduce.12 = (bf16[128]{0:T(256)(128)(2,1)S(1)}, bf16[128]{0:T(256)(128)(2,1)S(1)}) all-reduce(bf16[128]{0:T(256)(128)(2,1)S(1)} %dynamic-update-slice, bf16[128]{0:T(256)(128)(2,1)S(1)} %dynamic-update-slice.1), channel_id=1, replica_groups=mesh['dp'=8,'tensor'=4] {'dp'}, use_global_device_ids=true, to_apply=%add.4 | all-reduce | flops 256 | bytes 1024
  53.3 29.6 %all_gather.56 = bf16[1024,256]{1,0:T(8,128)(2,1)S(1)} all-gather(bf16[128,256]{1,0:T(8,128)(2,1)S(1)} %copy-done.50), channel_id=1, replica_groups=mesh['dp'=8,'tensor'=4] {'dp'}, dimensions={0}, use_global_device_ids=true | all-gather | bytes 589824 | tf_op jit(solution)/shard_map/all_gather | solution.py:86
  83.0 31.9 %all_gather.58 = bf16[1024,256]{1,0:T(8,128)(2,1)S(1)} all-gather(bf16[128,256]{1,0:T(8,128)(2,1)S(1)} %copy-done.51), channel_id=1, replica_groups=mesh['dp'=8,'tensor'=4] {'dp'}, dimensions={0}, use_global_device_ids=true | all-gather | bytes 589824 | tf_op jit(solution)/shard_map/all_gather | solution.py:87
  133.1 20.3 %while.27 = (s32[]{:T(128)}, bf16[2,512,2,2,128]{4,3,2,1,0:T(2,128)(2,1)S(1)}, f32[2,2,2,512]{3,2,1,0:T(2,128)S(1)}, s32[2]{0:T(128)S(1)}, s32[1024]{0:T(1024)S(...) while((s32[]{:T(128)}, ...), condition=%wide.region_6.7_spmd, body=%wide.region_3.6_spmd.sunk | while | flops 1100741120 | bytes 30488788 | solution.py:150
  161.4 19.9 %all-gather.1 = bf16[8,1,128]{2,1,0:T(2,128)(2,1)S(1)} all-gather(bf16[1,1,128]{2,1,0:T(2,128)(2,1)S(1)} %bitcast.261), channel_id=1, replica_groups=mesh['dp'=8,'tensor'=4] {'dp'}, dimensions={0}, use_global_device_ids=true | all-gather | bytes 2304 | tf_op jit(solution)/shard_map/all_gather | solution.py:93
  181.3 27.8 %reduce-scatter.16.cloned.1.call-done = f32[256,1024]{1,0:T(8,128)} async-done(((f32[1024,1024]{1,0:T(8,128)}), f32[256,1024]{1,0:T(8,128)}) %reduce-scatter.16.cloned.1.call-update) | async-done | bytes 1048592 | tf_op jit(solution)/shard_map/reduce_scatter | solution.py:152
  214.2 40.2 %all-gather.22.cloned.1.call-done = bf16[1024,768]{1,0:T(8,128)(2,1)} async-done(((bf16[128,768]{1,0:T(8,128)(2,1)}), bf16[1024,768]{1,0:T(8,128)(2,1)}) %all-gather.22.cloned.1.call-update) | async-done | bytes 1572880 | tf_op jit(solution)/shard_map/all_gather | solution.py:90
  254.4 23.9 %all-gather.18.cloned.1.call-done = bf16[1024,1024]{1,0:T(8,128)(2,1)} async-done(((bf16[256,1024]{1,0:T(8,128)(2,1)}), bf16[1024,1024]{1,0:T(8,128)(2,1)}) %all-gather.18.cloned.1.call-update) | async-done | bytes 2097168 | tf_op jit(solution)/shard_map/all_gather | solution.py:164
  283.8 40.0 %all-gather.20.cloned.1.call-done = bf16[1024,768]{1,0:T(8,128)(2,1)} async-done(((bf16[128,768]{1,0:T(8,128)(2,1)}), bf16[1024,768]{1,0:T(8,128)(2,1)}) %all-gather.20.cloned.1.call-update) | async-done | bytes 1572880 | tf_op jit(solution)/shard_map/all_gather | solution.py:89
  329.2 38.1 %all-gather.24.cloned.1.call-done = bf16[768,1024]{1,0:T(8,128)(2,1)} async-done(((bf16[768,128]{1,0:T(8,128)(2,1)}), bf16[768,1024]{1,0:T(8,128)(2,1)}) %all-gather.24.cloned.1.call-update) | async-done | bytes 1572880 | tf_op jit(solution)/shard_map/all_gather | solution.py:91
  367.4 24.5 %all-gather.26.cloned.1.call-done = bf16[1024,1024]{1,0:T(8,128)(2,1)} async-done(((bf16[256,1024]{1,0:T(8,128)(2,1)}), bf16[1024,1024]{1,0:T(8,128)(2,1)}) %all-gather.26.cloned.1.call-update) | async-done | bytes 2097168 | tf_op jit(solution)/shard_map/all_gather | solution.py:200
  391.9 8.0 multiply_convert_fusion
  406.4 44.7 %reduce-scatter.20.cloned.1.call-done = f32[256,1024]{1,0:T(8,128)} async-done(((f32[1024,1024]{1,0:T(8,128)}), f32[256,1024]{1,0:T(8,128)}) %reduce-scatter.20.cloned.1.call-update) | async-done | bytes 1048592 | tf_op jit(solution)/shard_map/reduce_scatter | solution.py:211
  481.9 35.8 %while.28 = (s32[]{:T(128)}, f32[1024,2,128]{0,2,1:T(8,128)S(1)}, f32[1024,2,128]{0,2,1:T(8,128)}, f32[2,512,2,2,128]{4,1,0,3,2:T(8,128)}, s32[2]{0:T(128)S(1)},...) while((s32[]{:T(128)}, f32[1024,2,128]{0,2,1:T(8,128)S(1)}, ...), condition=%wide.region_14.15_spmd.clone, body=%wide.region_12.14_spmd.clone.sunk | while | flops 2718956032 | bytes 94968144 | solution.py:262
  557.3 56.7 %reduce-scatter.32.cloned.1.call-done = bf16[128,768]{1,0:T(8,128)(2,1)} async-done(((bf16[1024,768]{1,0:T(8,128)(2,1)}), bf16[128,768]{1,0:T(8,128)(2,1)}) %reduce-scatter.32.cloned.1.call-update) | async-done | bytes 196624 | tf_op jit(solution)/shard_map/reduce_scatter | solution.py:309
  615.7 66.1 %reduce-scatter.30.cloned.1.call-done = bf16[128,768]{1,0:T(8,128)(2,1)} async-done(((bf16[1024,768]{1,0:T(8,128)(2,1)}), bf16[128,768]{1,0:T(8,128)(2,1)}) %reduce-scatter.30.cloned.1.call-update) | async-done | bytes 196624 | tf_op jit(solution)/shard_map/reduce_scatter | solution.py:306
  683.5 63.3 %reduce-scatter.28.cloned.1.call-done = bf16[128,256]{1,0:T(8,128)(2,1)} async-done(((bf16[1024,256]{1,0:T(8,128)(2,1)}), bf16[128,256]{1,0:T(8,128)(2,1)}) %reduce-scatter.28.cloned.1.call-update) | async-done | bytes 65552 | tf_op jit(solution)/shard_map/reduce_scatter | solution.py:300
  748.4 63.3 %reduce-scatter.26.cloned.1.call-done = bf16[128,256]{1,0:T(8,128)(2,1)} async-done(((bf16[1024,256]{1,0:T(8,128)(2,1)}), bf16[128,256]{1,0:T(8,128)(2,1)}) %reduce-scatter.26.cloned.1.call-update) | async-done | bytes 65552 | tf_op jit(solution)/shard_map/reduce_scatter | solution.py:297
  813.2 64.9 %reduce-scatter.34.cloned.1.call-done = bf16[128,512]{1,0:T(8,128)(2,1)} async-done(((bf16[1024,512]{1,0:T(8,128)(2,1)}), bf16[128,512]{1,0:T(8,128)(2,1)}) %reduce-scatter.34.cloned.1.call-update) | async-done | bytes 131088
  879.9 65.1 %reduce-scatter.24.cloned.1.call-done = bf16[128,512]{1,0:T(8,128)(2,1)} async-done(((bf16[1024,512]{1,0:T(8,128)(2,1)}), bf16[128,512]{1,0:T(8,128)(2,1)}) %reduce-scatter.24.cloned.1.call-update) | async-done | bytes 131088 | tf_op jit(solution)/shard_map/reduce_scatter | solution.py:294
  946.6 31.2 %reduce-scatter.22.cloned.1.call-done = bf16[256,1024]{1,0:T(8,128)(2,1)} async-done(((bf16[1024,1024]{1,0:T(8,128)(2,1)}), bf16[256,1024]{1,0:T(8,128)(2,1)}) %reduce-scatter.22.cloned.1.call-update) | async-done | bytes 524304 | tf_op jit(solution)/shard_map/reduce_scatter | solution.py:283
  979.4 10.3 %all-reduce.10 = (bf16[1024]{0:T(1024)(128)(2,1)S(1)}, bf16[1024]{0:T(1024)(128)(2,1)S(1)}, bf16[128]{0:T(256)(128)(2,1)S(1)}, bf16[128]{0:T(256)(128)(2,1)S(1)}) all-reduce(f32[1024]{0:T(1024)S(1)} %get-tuple-element.280, f32[1024]{0:T(1024)S(1)} %copy-done.56, ...), channel_id=1, replica_groups=mesh['dp'=8,'tensor'=4] {'tensor'}, use_global_device_ids=true, to_apply=%region_27.28 | all-reduce | flops 2304 | bytes 13824 | tf_op jit(solution)/shard_map/psum | solution.py:292
  989.7 15.3 %all-reduce.11 = (bf16[1024]{0:T(1024)(128)(2,1)S(1)}, bf16[1024]{0:T(1024)(128)(2,1)S(1)}, bf16[128]{0:T(256)(128)(2,1)S(1)}, bf16[128]{0:T(256)(128)(2,1)S(1)}) all-reduce(bf16[1024]{0:T(1024)(128)(2,1)S(1)} %get-tuple-element.324, bf16[1024]{0:T(1024)(128)(2,1)S(1)} %get-tuple-element.325, ...), channel_id=13, replica_groups=mesh['dp'=8,'tensor'=4] {'dp'}, use_global_device_ids=true, to_apply=%region_28.29.clone | all-reduce | flops 2304 | bytes 9216
  (334 shorter events, 200.2 us)
Async XLA Ops:
  7.2 107.6 %all-gather.12.cloned.1.call-start = ((), (), s32[]{:S(2)}) async-start(), calls=%async_computation.11 | async-start | bytes 2621440 | tf_op jit(solution)/shard_map/all_gather | solution.py:113
  25.5 97.9 %all-gather.14.cloned.1.call-start = ((), (), s32[]{:S(2)}) async-start(), calls=%async_computation.12 | async-start | bytes 1179648 | tf_op jit(solution)/shard_map/all_gather | solution.py:85
  26.3 129.6 %all-gather.16.cloned.1.call-start = ((), (), s32[]{:S(2)}) async-start(), calls=%async_computation.13 | async-start | bytes 1179648 | tf_op jit(solution)/shard_map/all_gather | solution.py:88
  27.0 182.1 %reduce-scatter.16.cloned.1.call-start = ((), (), s32[]{:S(2)}) async-start(), calls=%async_computation.14 | async-start | bytes 5242880 | tf_op jit(solution)/shard_map/reduce_scatter | solution.py:152
  160.8 93.6 %all-gather.22.cloned.1.call-start = ((), (), s32[]{:S(2)}) async-start(), calls=%async_computation.17 | async-start | bytes 1769472 | tf_op jit(solution)/shard_map/all_gather | solution.py:90
  161.4 117.0 %all-gather.18.cloned.1.call-start = ((), (), s32[]{:S(2)}) async-start(), calls=%async_computation.15 | async-start | bytes 2621440 | tf_op jit(solution)/shard_map/all_gather | solution.py:164
  211.9 111.9 %all-gather.20.cloned.1.call-start = ((), (), s32[]{:S(2)}) async-start(), calls=%async_computation.16 | async-start | bytes 1769472 | tf_op jit(solution)/shard_map/all_gather | solution.py:89
  212.7 154.7 %all-gather.24.cloned.1.call-start = ((), (), s32[]{:S(2)}) async-start(), calls=%async_computation.18 | async-start | bytes 1769472 | tf_op jit(solution)/shard_map/all_gather | solution.py:91
  213.4 178.5 %all-gather.26.cloned.1.call-start = ((), (), s32[]{:S(2)}) async-start(), calls=%async_computation.20 | async-start | bytes 2621440 | tf_op jit(solution)/shard_map/all_gather | solution.py:200
  214.1 236.9 %reduce-scatter.20.cloned.1.call-start = ((), (), s32[]{:S(2)}) async-start(), calls=%async_computation.21 | async-start | bytes 5242880 | tf_op jit(solution)/shard_map/reduce_scatter | solution.py:211
  406.4 71.4 %all-gather.28.cloned.1.call-start = ((), (), s32[]{:S(2)}) async-start(), calls=%async_computation.22 | async-start | bytes 2621440 | tf_op jit(solution)/shard_map/all_gather | solution.py:222
  455.0 100.3 %reduce-scatter.36.cloned.1.call-start = ((), (), s32[]{:S(2)}) async-start(), calls=%async_computation.30 | async-start | bytes 1769472
  462.8 151.2 %reduce-scatter.32.cloned.1.call-start = ((), (), s32[]{:S(2)}) async-start(), calls=%async_computation.28 | async-start | bytes 1769472 | tf_op jit(solution)/shard_map/reduce_scatter | solution.py:309
  468.2 213.6 %reduce-scatter.30.cloned.1.call-start = ((), (), s32[]{:S(2)}) async-start(), calls=%async_computation.27 | async-start | bytes 1769472 | tf_op jit(solution)/shard_map/reduce_scatter | solution.py:306
  473.4 273.4 %reduce-scatter.28.cloned.1.call-start = ((), (), s32[]{:S(2)}) async-start(), calls=%async_computation.26 | async-start | bytes 589824 | tf_op jit(solution)/shard_map/reduce_scatter | solution.py:300
  522.4 289.3 %reduce-scatter.26.cloned.1.call-start = ((), (), s32[]{:S(2)}) async-start(), calls=%async_computation.25 | async-start | bytes 589824 | tf_op jit(solution)/shard_map/reduce_scatter | solution.py:297
  527.4 350.7 %reduce-scatter.34.cloned.1.call-start = ((), (), s32[]{:S(2)}) async-start(), calls=%async_computation.29 | async-start | bytes 1179648
  532.6 412.4 %reduce-scatter.24.cloned.1.call-start = ((), (), s32[]{:S(2)}) async-start(), calls=%async_computation.24 | async-start | bytes 1179648 | tf_op jit(solution)/shard_map/reduce_scatter | solution.py:294
  542.9 435.0 %reduce-scatter.22.cloned.1.call-start = ((), (), s32[]{:S(2)}) async-start(), calls=%async_computation.23 | async-start | bytes 2621440 | tf_op jit(solution)/shard_map/reduce_scatter | solution.py:283
  548.0 463.4 %reduce-scatter.18.cloned.1.call-start = ((), (), s32[]{:S(2)}) async-start(), calls=%async_computation.19 | async-start | bytes 2621440 | tf_op jit(solution)/shard_map/reduce_scatter | solution.py:169
  556.5 455.0 %copy-start.3 = (f32[256,1024]{1,0:T(8,128)S(1)}, f32[256,1024]{1,0:T(8,128)}, u32[]{:S(2)}) copy-start(f32[256,1024]{1,0:T(8,128)} %copy-done.2) | copy-start | bytes 3145732
  556.5 455.0 %copy-start.8 = (f32[256,1024]{1,0:T(8,128)S(1)}, f32[256,1024]{1,0:T(8,128)}, u32[]{:S(2)}) copy-start(f32[256,1024]{1,0:T(8,128)} %reduce-scatter.20.cloned.1.call-done) | copy-start | bytes 3145732
  556.5 455.0 %copy-start.20 = (bf16[256,1024]{1,0:T(8,128)(2,1)S(1)}, bf16[256,1024]{1,0:T(8,128)(2,1)}, u32[]{:S(2)}) copy-start(bf16[256,1024]{1,0:T(8,128)(2,1)} %param.33) | copy-start | bytes 1572868
  556.5 454.9 %copy-start.45 = (f32[8,1,128]{2,1,0:T(1,128)S(1)}, f32[8,1,128]{2,1,0:T(1,128)}, u32[]{:S(2)}) copy-start(f32[8,1,128]{2,1,0:T(1,128)} %copy-done.44) | copy-start | bytes 12292
  (76 other events, 4520.9 us)
Sparse Core Ops, SparseCore 0:
  25.7 26.2 all-gather.11
  54.0 42.2 all-gather.13
  98.4 39.7 all-gather.15
  160.9 48.1 reduce-scatter.15
  211.1 43.2 all-gather.21
  256.4 21.8 all-gather.17
  280.5 43.2 all-gather.19
  325.8 41.5 all-gather.23
  368.9 22.9 all-gather.25
  406.5 44.5 reduce-scatter.19
  455.2 22.5 all-gather.27
  481.0 65.0 reduce-scatter.35
  549.6 64.3 reduce-scatter.31
  617.3 64.5 reduce-scatter.29
  685.0 61.8 reduce-scatter.27
  750.1 61.5 reduce-scatter.25
  814.9 63.1 reduce-scatter.33
  881.9 63.0 reduce-scatter.23
  947.5 30.2 reduce-scatter.21
  980.2 31.1 reduce-scatter.17
where the time goes:
time: 1030 us; the launch traced here: 1020 us
  waiting for transfers between devices  664 us (64%)
  blocking collectives  143 us (14%)
  matrix products  111 us (11%)
  other arithmetic  47.5 us (5%)
  local copies, waits for them, and re-layouts  34.5 us (3%)
  between operations  17.6 us (2%)
    unnamed x22, waiting for transfers between devices  69.1 us
    reduce_scatter x1, waiting for transfers between devices, body(): lax.psum_scatter(grad_gate.astype(jnp.bfloat16), 'dp', scatter_dimension=...  66.1 us
    reduce_scatter x1, waiting for transfers between devices, body(): lax.psum_scatter(grad_query.astype(jnp.bfloat16), 'dp', scatter_dimension...  65.1 us
    reduce_scatter x1, waiting for transfers between devices, body(): lax.psum_scatter(grad_value.astype(jnp.bfloat16), 'dp', scatter_dimension...  63.3 us
    reduce_scatter x1, waiting for transfers between devices, body(): lax.psum_scatter(grad_key.astype(jnp.bfloat16), 'dp', scatter_dimension=0...  63.3 us
    reduce_scatter x1, waiting for transfers between devices, body(): lax.psum_scatter(grad_up.astype(jnp.bfloat16), 'dp', scatter_dimension=0,...  56.7 us
    reduce_scatter x1, waiting for transfers between devices, body(): lax.psum_scatter(dot_back(row_slice(d_gate_low, row_start, lax.axis_size(...  44.7 us
    all_gather x1, waiting for transfers between devices, body(): lax.all_gather(w_up, 'dp', axis=0, tiled=True)  40.2 us
  transfers between devices with their start and end apart: 20, of which 16 were waited for; matrix products, arithmetic and copies ran while one was open for 15% of the time, Pallas kernels for 0%

commit v1 on v0

v1 whole, which is shorter than its diff:
```python
import functools

import jax
import jax.numpy as jnp
from jax import lax
from jax.experimental import pallas as pl
from jax.experimental.pallas import tpu as pltpu
from jax.sharding import PartitionSpec as P

HEAD = 128
EPS = 1e-06
ROPE_BASE = 1000000.0
SCALE = HEAD ** (-0.5)
EXP2_SCALE = SCALE * 1.4426950408889634
F32 = jnp.float32
BF16 = jnp.bfloat16
VMEM_LIMIT = 60 * 1024 * 1024


def mm(a, b, ca=1, cb=0):
    return lax.dot_general(a, b, (((ca,), (cb,)), ((), ())), preferred_element_type=F32)


def call(kernel, grid, in_specs, out_specs, out_shape, flops, nbytes, scratch=()):
    return pl.pallas_call(
        kernel,
        out_shape=out_shape,
        grid_spec=pltpu.PrefetchScalarGridSpec(
            num_scalar_prefetch=1,
            grid=grid,
            in_specs=in_specs,
            out_specs=out_specs,
            scratch_shapes=list(scratch),
        ),
        compiler_params=pltpu.CompilerParams(
            dimension_semantics=("arbitrary",) * len(grid), vmem_limit_bytes=VMEM_LIMIT
        ),
        cost_estimate=pl.CostEstimate(flops=flops, bytes_accessed=nbytes, transcendentals=0),
    )


def whole(shape):
    return pl.BlockSpec(shape, lambda i, t: (0,) * len(shape))


def rows_at(rows, cols):
    return pl.BlockSpec((rows, cols), lambda i, t: (i, 0))


def rows_xor(rows, cols):
    return pl.BlockSpec((rows, cols), lambda i, t: (lax.bitwise_xor(i, t[0]), 0))


def qkv_kernel(kv_heads, group, t, x, gain, w, cos, sin, gq, gk, normed, packed, raw):
    u = x[...].astype(F32)
    r = lax.rsqrt(jnp.mean(u * u, axis=1, keepdims=True) + EPS)
    low = (u * r * gain[...]).astype(BF16)
    normed[...] = low
    y = mm(low, w[...])
    c = cos[...]
    s = sin[...]
    for h in range(kv_heads):
        base = h * (group + 2) * HEAD
        kept = h * (group + 1) * HEAD
        for j in range(group + 1):
            v = y[:, base + j * HEAD : base + (j + 1) * HEAD]
            raw[:, kept + j * HEAD : kept + (j + 1) * HEAD] = v
            scale = gq[...] if j < group else gk[...]
            v = v * lax.rsqrt(jnp.mean(v * v, axis=1, keepdims=True) + EPS) * scale
            v = v * c + pltpu.roll(v, HEAD // 2, 1) * s
            packed[:, base + j * HEAD : base + (j + 1) * HEAD] = v.astype(BF16)
        end = base + (group + 1) * HEAD
        packed[:, end : end + HEAD] = y[:, end : end + HEAD].astype(BF16)


def qkv_call(t, x, gain, w, cos, sin, gq, gk, rows, kv_heads, group):
    n, width = x.shape
    cols = w.shape[1]
    kept = kv_heads * (group + 1) * HEAD
    return call(
        functools.partial(qkv_kernel, kv_heads, group),
        (n // rows,),
        [
            rows_at(rows, width),
            whole(gain.shape),
            whole(w.shape),
            rows_xor(rows, HEAD),
            rows_xor(rows, HEAD),
            whole(gq.shape),
            whole(gk.shape),
        ],
        [rows_at(rows, width), rows_xor(rows, cols), rows_xor(rows, kept)],
        [
            jax.ShapeDtypeStruct((n, width), BF16),
            jax.ShapeDtypeStruct((n, cols), BF16),
            jax.ShapeDtypeStruct((n, kept), F32),
        ],
        2 * n * width * cols,
        n * width * 4 + width * cols * 2 + n * cols * 5,
    )(t, x, gain, w, cos, sin, gq, gk)


def weights_of(q, k, same, causal):
    e = jnp.exp2(mm(k, q, 1, 1) * EXP2_SCALE)
    keep = same if causal is None else same & causal
    return jnp.where(keep, e, 0.0)


def attn_forward_kernel(rows, blocks, group, t, packed, seg_col, seg_row, mixed, inv):
    causal = lax.broadcasted_iota(jnp.int32, (rows, rows), 0) <= lax.broadcasted_iota(
        jnp.int32, (rows, rows), 1
    )
    kc = group * HEAD
    for i in range(blocks):
        lo = i * rows
        at = pl.multiple_of(lax.bitwise_xor(i, t[0]) * rows, rows)
        sq = seg_row[:, lo : lo + rows]
        for j in range(group):
            q = packed[lo : lo + rows, j * HEAD : (j + 1) * HEAD]
            parts = []
            total = jnp.zeros((1, rows), F32)
            for b in range(i + 1):
                k = packed[b * rows : (b + 1) * rows, kc : kc + HEAD]
                same = seg_col[b * rows : (b + 1) * rows, :] == sq
                e = weights_of(q, k, same, causal if b == i else None)
                total = total + jnp.sum(e, axis=0, keepdims=True)
                parts.append(e)
            rec = 1.0 / total
            inv[0, j : j + 1, lo : lo + rows] = rec
            out = jnp.zeros((rows, HEAD), F32)
            for b in range(i + 1):
                v = packed[b * rows : (b + 1) * rows, kc + HEAD : kc + 2 * HEAD]
                out = out + mm((parts[b] * rec).astype(BF16), v, 0, 0)
            mixed[pl.ds(at, rows), j * HEAD : (j + 1) * HEAD] = out.astype(BF16)


def attn_forward(t, packed, seg_col, seg_row, rows, kv_heads, group):
    n = packed.shape[0]
    return call(
        functools.partial(attn_forward_kernel, rows, n // rows, group),
        (kv_heads,),
        [
            pl.BlockSpec((n, (group + 2) * HEAD), lambda h, t: (0, h)),
            whole(seg_col.shape),
            whole(seg_row.shape),
        ],
        [
            pl.BlockSpec((n, group * HEAD), lambda h, t: (0, h)),
            pl.BlockSpec((1, 8, n), lambda h, t: (h, 0, 0)),
        ],
        [
            jax.ShapeDtypeStruct((n, kv_heads * group * HEAD), BF16),
            jax.ShapeDtypeStruct((kv_heads, 8, n), F32),
        ],
        kv_heads * group * n * n * HEAD * 4,
        n * kv_heads * (group + 1) * HEAD * 4,
    )(t, packed, seg_col, seg_row)


def head_back(e, u, cos, sin, gain):
    e = e * cos - pltpu.roll(e, HEAD // 2, 1) * sin
    r = lax.rsqrt(jnp.mean(u * u, axis=1, keepdims=True) + EPS)
    ur = u * r
    dgain = jnp.sum(e * ur, axis=0, keepdims=True)
    ec = e * gain
    du = r * (ec - ur * jnp.mean(ur * ec, axis=1, keepdims=True))
    return du, dgain


def attn_backward_kernel(
    rows, blocks, group, t, packed, seg_col, seg_row, inv, dmix, raw, cos, sin, gq, gk, dpacked, dgain, dk, dv
):
    causal = lax.broadcasted_iota(jnp.int32, (rows, rows), 0) <= lax.broadcasted_iota(
        jnp.int32, (rows, rows), 1
    )
    kc = group * HEAD
    dk[...] = jnp.zeros_like(dk)
    dv[...] = jnp.zeros_like(dv)
    dgain[...] = jnp.zeros_like(dgain)
    for i in range(blocks):
        lo = i * rows
        at = pl.multiple_of(lax.bitwise_xor(i, t[0]) * rows, rows)
        sq = seg_row[:, lo : lo + rows]
        for j in range(group):
            q = packed[lo : lo + rows, j * HEAD : (j + 1) * HEAD]
            do = dmix[pl.ds(at, rows), j * HEAD : (j + 1) * HEAD]
            rec = inv[0, j : j + 1, lo : lo + rows]
            probs = []
            dprobs = []
            delta = jnp.zeros((1, rows), F32)
            for b in range(i + 1):
                here = slice(b * rows, (b + 1) * rows)
                k = packed[here, kc : kc + HEAD]
                v = packed[here, kc + HEAD : kc + 2 * HEAD]
                same = seg_col[here, :] == sq
                p = weights_of(q, k, same, causal if b == i else None) * rec
                dp = mm(v, do, 1, 1)
                delta = delta + jnp.sum(p * dp, axis=0, keepdims=True)
                dv[here, :] += mm(p.astype(BF16), do)
                probs.append(p)
                dprobs.append(dp)
            dq = jnp.zeros((rows, HEAD), F32)
            for b in range(i + 1):
                here = slice(b * rows, (b + 1) * rows)
                k = packed[here, kc : kc + HEAD]
                ds = (probs[b] * (dprobs[b] - delta)).astype(BF16)
                dk[here, :] += mm(ds, q)
                dq = dq + mm(ds, k, 0, 0)
            du, dg = head_back(
                dq * SCALE,
                raw[lo : lo + rows, j * HEAD : (j + 1) * HEAD],
                cos[lo : lo + rows, :],
                sin[lo : lo + rows, :],
                gq[...],
            )
            dgain[0, 0:1, :] += dg
            dpacked[pl.ds(at, rows), j * HEAD : (j + 1) * HEAD] = du.astype(BF16)
    for i in range(blocks):
        here = slice(i * rows, (i + 1) * rows)
        at = pl.multiple_of(lax.bitwise_xor(i, t[0]) * rows, rows)
        du, dg = head_back(
            dk[here, :] * SCALE, raw[here, kc : kc + HEAD], cos[here, :], sin[here, :], gk[...]
        )
        dgain[0, 1:2, :] += dg
        dpacked[pl.ds(at, rows), kc : kc + HEAD] = du.astype(BF16)
        dpacked[pl.ds(at, rows), kc + HEAD : kc + 2 * HEAD] = dv[here, :].astype(BF16)


def attn_backward(t, packed, seg_col, seg_row, inv, dmix, raw, cos, sin, gq, gk, rows, kv_heads, group):
    n = packed.shape[0]
    by_head = lambda width: pl.BlockSpec((n, width), lambda h, t: (0, h))
    return call(
        functools.partial(attn_backward_kernel, rows, n // rows, group),
        (kv_heads,),
        [
            by_head((group + 2) * HEAD),
            whole(seg_col.shape),
            whole(seg_row.shape),
            pl.BlockSpec((1, 8, n), lambda h, t: (h, 0, 0)),
            by_head(group * HEAD),
            by_head((group + 1) * HEAD),
            whole(cos.shape),
            whole(sin.shape),
            whole(gq.shape),
            whole(gk.shape),
        ],
        [by_head((group + 2) * HEAD), pl.BlockSpec((1, 8, HEAD), lambda h, t: (h, 0, 0))],
        [
            jax.ShapeDtypeStruct(packed.shape, BF16),
            jax.ShapeDtypeStruct((kv_heads, 8, HEAD), F32),
        ],
        kv_heads * group * n * n * HEAD * 10,
        n * kv_heads * (group + 1) * HEAD * 14,
        [pltpu.VMEM((n, HEAD), F32), pltpu.VMEM((n, HEAD), F32)],
    )(t, packed, seg_col, seg_row, inv, dmix, raw, cos, sin, gq, gk)


def mlp_kernel(ff, t, x, g, w, wd, act, dgu, dx, out):
    y = mm(x[...], w[...])
    gate = y[:, :ff]
    up = y[:, ff:]
    sig = 1.0 / (1.0 + jnp.exp(-gate))
    silu = gate * sig
    a = (silu * up).astype(BF16)
    act[...] = a
    da = mm(g[...], wd[...])
    dgu[:, :ff] = (da * up * sig * (1.0 + gate * (1.0 - sig))).astype(BF16)
    dgu[:, ff:] = (da * silu).astype(BF16)
    dx[...] = mm(dgu[...], w[...], 1, 1).astype(BF16)
    out[...] = mm(a, wd[...], 1, 1).astype(BF16)


def mlp_call(t, x, g, w, wd, rows):
    n, width = x.shape
    ff = wd.shape[1]
    return call(
        functools.partial(mlp_kernel, ff),
        (n // rows,),
        [rows_at(rows, width), rows_at(rows, width), whole(w.shape), whole(wd.shape)],
        [rows_at(rows, ff), rows_at(rows, 2 * ff), rows_at(rows, width), rows_at(rows, width)],
        [
            jax.ShapeDtypeStruct((n, ff), BF16),
            jax.ShapeDtypeStruct((n, 2 * ff), BF16),
            jax.ShapeDtypeStruct((n, width), BF16),
            jax.ShapeDtypeStruct((n, width), BF16),
        ],
        2 * n * width * ff * 6,
        n * width * 8 + width * ff * 6 + n * ff * 6,
    )(t, x, g, w, wd)


def xor_pairs(size, bits):
    return [(i, i ^ bits) for i in range(size)]


class Links:
    def __init__(self, dp, tensor):
        self.dp, self.tensor = dp, tensor
        self.direct = (dp, tensor) == (8, 4)
        self.d = lax.axis_index("dp")
        self.t = lax.axis_index("tensor")

    def over_dp(self, x, bits):
        return lax.ppermute(x, "dp", xor_pairs(self.dp, bits))

    def over_tensor(self, x, bits):
        return lax.ppermute(x, "tensor", xor_pairs(self.tensor, bits))

    def row_offset(self):
        return (self.t if self.direct else jnp.int32(0)).reshape(1)

    def columns_in(self, x):
        if not self.direct:
            return x
        n = x.shape[1] // 8
        order = [2 * p if p < 4 else 2 * (p - 4) + 1 for p in range(8)]
        return jnp.concatenate(
            [lax.dynamic_slice_in_dim(x, lax.bitwise_xor(self.d, k) * n, n, 1) for k in order], axis=1
        )

    def columns_out(self, x):
        if not self.direct:
            return x
        n = x.shape[1] // 8
        blocks = []
        for b in range(8):
            k = lax.bitwise_xor(self.d, b)
            blocks.append(lax.dynamic_slice_in_dim(x, ((k >> 1) + 4 * (k & 1)) * n, n, 1))
        return jnp.concatenate(blocks, axis=1)

    def gather_dp(self, x):
        if not self.direct:
            return lax.all_gather(x, "dp", axis=0, tiled=True)
        own = [x] + [self.over_dp(x, 2 * z) for z in (1, 2, 3)]
        return jnp.concatenate(own + [self.over_dp(b, 1) for b in own], axis=0)

    def scatter_dp(self, left, right):
        if not self.direct:
            return lax.psum_scatter(
                mm(left, right, 0, 0).astype(BF16), "dp", scatter_dimension=0, tiled=True
            ).astype(F32)
        half = left.shape[1] // 2
        quarter = half // 4
        got = self.over_dp(mm(left[:, half:], right, 0, 0).astype(BF16), 1)
        keep = lax.optimization_barrier(mm(left[:, :half], right, 0, 0).astype(BF16))
        total = None
        parts = []
        for z in range(4):
            here = slice(z * quarter, (z + 1) * quarter)
            s = keep[here].astype(F32) + got[here].astype(F32)
            parts.append(s if z == 0 else self.over_dp(s.astype(BF16), 2 * z).astype(F32))
        return parts[0] + parts[1] + parts[2] + parts[3]

    def gather_tensor(self, x):
        if not self.direct:
            return lax.all_gather(x, "tensor", axis=0, tiled=True)
        far = self.over_tensor(x, 2)
        return jnp.concatenate([x, self.over_tensor(x, 1), far, self.over_tensor(far, 1)], axis=0)

    def scatter_tensor(self, x):
        if not self.direct:
            return lax.psum_scatter(x, "tensor", scatter_dimension=0, tiled=True).astype(F32)
        n = x.shape[0] // 4
        block = lambda k: x[k * n : (k + 1) * n]
        far = block(2).astype(F32) + self.over_tensor(block(3), 1).astype(F32)
        near = block(0).astype(F32) + self.over_tensor(block(1), 1).astype(F32)
        return near + self.over_tensor(far.astype(BF16), 2).astype(F32)

    def total(self, x):
        if not self.direct:
            return lax.psum(x, ("dp", "tensor"))
        x = x + self.over_tensor(x, 1)
        x = x + self.over_tensor(x, 2)
        x = x + self.over_dp(x, 1)
        return x + self.over_dp(x, 2) + self.over_dp(x, 4) + self.over_dp(x, 6)

    def gather_gains(self, *gains):
        if not self.direct:
            return [lax.all_gather(g, "dp", axis=0, tiled=True) for g in gains]
        sizes = [g.shape[0] for g in gains]
        flat = jnp.concatenate(gains)[None, :]
        own = [flat] + [self.over_dp(flat, 2 * z) for z in (1, 2, 3)]
        near = jnp.concatenate(own, axis=0)
        table = jnp.concatenate([near, self.over_dp(near, 1)], axis=0)
        out, at = [], 0
        for index, size in enumerate(sizes):
            part = table[:, at : at + size]
            if index >= 2:
                rows = []
                for b in range(8):
                    k = lax.bitwise_xor(self.d, b)
                    rows.append(lax.dynamic_slice_in_dim(part, (k >> 1) + 4 * (k & 1), 1, 0))
                part = jnp.concatenate(rows, axis=0)
            out.append(part.reshape(-1))
            at += size
        return out


def norm_back(e, u, gain):
    r = lax.rsqrt(jnp.mean(u * u, axis=1, keepdims=True) + EPS)
    ur = u * r
    ec = e * gain
    return r * (ec - ur * jnp.mean(ur * ec, axis=1, keepdims=True)), jnp.sum(e * ur, axis=0)


def rope_tables(offsets):
    frequency = ROPE_BASE ** (-(2.0 * jnp.arange(HEAD // 2, dtype=F32)) / HEAD)
    angles = offsets.astype(F32)[:, None] * frequency[None, :]
    cos, sin = jnp.cos(angles), jnp.sin(angles)
    return jnp.concatenate([cos, cos], axis=1), jnp.concatenate([-sin, sin], axis=1)


def pack_heads(wq, wk, wv, group):
    parts = []
    for h in range(wk.shape[1] // HEAD):
        parts += [
            wq[:, h * group * HEAD : (h + 1) * group * HEAD],
            wk[:, h * HEAD : (h + 1) * HEAD],
            wv[:, h * HEAD : (h + 1) * HEAD],
        ]
    return jnp.concatenate(parts, axis=1)


def unpack_heads(w, kv_heads, group):
    q, k, v = [], [], []
    for h in range(kv_heads):
        base = h * (group + 2) * HEAD
        mid = base + group * HEAD
        q.append(w[:, base:mid])
        k.append(w[:, mid : mid + HEAD])
        v.append(w[:, mid + HEAD : mid + 2 * HEAD])
    join = lambda parts: jnp.concatenate(parts, axis=1)
    return join(q), join(k), join(v)


def body(
    dp,
    tensor,
    tokens,
    segment_ids,
    positions,
    w_query,
    key_projection,
    value_projection,
    w_out,
    w_gate,
    w_up,
    w_down,
    gain_attn,
    gain_mlp,
    gain_query,
    gain_key,
    cotangent,
):
    links = Links(dp, tensor)
    rows = tokens.shape[0]
    kv_heads = key_projection.shape[1] // HEAD
    group = w_query.shape[1] // key_projection.shape[1]
    t = links.row_offset()

    w_qkv = links.gather_dp(pack_heads(w_query, key_projection, value_projection, group))
    w_o = links.gather_dp(w_out.T)
    w_gu = links.gather_dp(jnp.concatenate([w_gate, w_up], axis=1))
    w_d = links.gather_dp(w_down.T)
    g_attn, g_mlp, g_q, g_k = [
        g.astype(F32)[None, :] for g in links.gather_gains(gain_attn, gain_mlp, gain_query, gain_key)
    ]

    x_low = links.columns_in(tokens)
    cot_low = links.columns_in(cotangent)
    x_rows = links.gather_tensor(x_low)
    cot_rows = links.gather_tensor(cot_low)
    cos, sin = rope_tables(positions[0])
    seg_row = segment_ids
    seg_col = segment_ids.reshape(-1, 1)

    normed, packed, raw = qkv_call(
        t, x_rows, g_attn, w_qkv, cos, sin, g_q, g_k, rows, kv_heads, group
    )
    mixed, inv = attn_forward(t, packed, seg_col, seg_row, rows, kv_heads, group)
    branch = links.scatter_tensor(mm(mixed, w_o, 1, 1).astype(BF16))
    x = x_low.astype(F32)
    hidden = x + branch
    r = lax.rsqrt(jnp.mean(hidden * hidden, axis=1, keepdims=True) + EPS)
    normed_mlp = links.gather_tensor((hidden * r * g_mlp).astype(BF16))
    act, d_gu, d_norm, mlp_out = mlp_call(t, normed_mlp, cot_rows, w_gu, w_d, rows)
    d_norm_mlp = links.scatter_tensor(d_norm)
    d_part, d_gain_mlp = norm_back(d_norm_mlp, hidden, g_mlp)
    d_hidden = cot_low.astype(F32) + d_part
    branch_rows = links.gather_tensor(d_hidden.astype(BF16))
    activations = (hidden + links.scatter_tensor(mlp_out)).astype(BF16)

    grad_down = links.scatter_dp(cot_rows, act)
    grad_gu = links.scatter_dp(normed_mlp, d_gu)
    d_mixed = mm(branch_rows, w_o).astype(BF16)
    grad_out = links.scatter_dp(branch_rows, mixed)
    d_packed, d_gain_heads = attn_backward(
        t, packed, seg_col, seg_row, inv, d_mixed, raw, cos, sin, g_q, g_k, rows, kv_heads, group
    )
    grad_qkv = links.scatter_dp(normed, d_packed)
    d_norm_attn = links.scatter_tensor(mm(d_packed, w_qkv, 1, 1).astype(BF16))
    d_part, d_gain_attn = norm_back(d_norm_attn, x, g_attn)
    d_tokens = d_hidden + d_part

    head_gains = jnp.sum(d_gain_heads, axis=0)
    sums = links.total(
        jnp.concatenate(
            [
                links.columns_out(d_gain_attn[None, :]).reshape(-1, HEAD),
                links.columns_out(d_gain_mlp[None, :]).reshape(-1, HEAD),
                head_gains[:2],
            ],
            axis=0,
        )
    )
    width = tokens.shape[1]
    model_rows = width // HEAD
    n = width // dp
    m = HEAD // dp
    sum_attn = sums[:model_rows].reshape(-1)
    sum_mlp = sums[model_rows : 2 * model_rows].reshape(-1)
    shard = lambda v, size: lax.dynamic_slice_in_dim(v, links.d * size, size, 0)
    grad_query, grad_key, grad_value = unpack_heads(grad_qkv, kv_heads, group)
    ff = w_gate.shape[1]
    return (
        links.columns_out(activations),
        links.columns_out(d_tokens),
        grad_query,
        grad_key,
        grad_value,
        grad_out.T,
        grad_gu[:, :ff],
        grad_gu[:, ff:],
        grad_down.T,
        shard(sum_attn, n),
        shard(sum_mlp, n),
        shard(sums[2 * model_rows], m),
        shard(sums[2 * model_rows + 1], m),
    )


def solution(mesh):
    tokens = P(("dp", "tensor"), None)
    by_rows = P("dp", "tensor")
    by_columns = P("tensor", "dp")
    sequence = P("dp", None)
    gain = P("dp")
    return jax.shard_map(
        functools.partial(body, mesh.shape["dp"], mesh.shape["tensor"]),
        mesh=mesh,
        in_specs=(
            tokens,
            sequence,
            sequence,
            by_rows,
            by_rows,
            by_rows,
            by_columns,
            by_rows,
            by_rows,
            by_columns,
            gain,
            gain,
            gain,
            gain,
            tokens,
        ),
        out_specs=(
            tokens,
            tokens,
            by_rows,
            by_rows,
            by_rows,
            by_columns,
            by_rows,
            by_rows,
            by_columns,
            gain,
            gain,
            gain,
            gain,
        ),
        check_vma=False,
    )
```

time: 1030 us -> 433 us (0.42)
  the two profiles are of different devices: /device:TPU:12 before, /device:TPU:0 now
where the time goes in v1:
time: 433 us; the launch traced here: 426 us
  waiting for transfers between devices  180 us (42%)
  starting transfers between devices  80.8 us (19%)
  local copies, waits for them, and re-layouts  54.6 us (13%)
  Pallas kernels  50.7 us (12%)
  other arithmetic  32.8 us (8%)
  matrix products  26.1 us (6%)
    ppermute x52, waiting for transfers between devices, over_dp(): return lax.ppermute(x, 'dp', xor_pairs(self.dp, bits))  161 us
    ppermute x52, starting transfers between devices, over_dp(): return lax.ppermute(x, 'dp', xor_pairs(self.dp, bits))  67.1 us
    unnamed x139, local copies, waits for them, and re-layouts  40.8 us
    dot_general x11, matrix products, mm(): lax.dot_general(a, b, (((ca,), (cb,)), ((), ())), preferred_element_type=...  26.1 us
    ppermute x26, waiting for transfers between devices, over_tensor(): return lax.ppermute(x, 'tensor', xor_pairs(self.tensor, bits))  18.2 us
    pallas_call x1, Pallas kernels, attn_backward(): call(functools.partial(attn_backward_kernel, rows, n // rows, group), (kv...  18 us
    pallas_call x1, Pallas kernels, mlp_call(): call(functools.partial(mlp_kernel, ff), (n // rows,), [rows_at(rows, widt...  15.7 us
    ppermute x26, starting transfers between devices, over_tensor(): return lax.ppermute(x, 'tensor', xor_pairs(self.tensor, bits))  13.7 us
  transfers between devices with their start and end apart: 78, of which 33 were waited for; matrix products, arithmetic and copies ran while one was open for 20% of the time, Pallas kernels for 4%

profile of v1, /device:TPU:0, one launch (start us, length us, event | category | flops | bytes accessed | tf_op | source)
XLA Modules:
  0.0 426.3 jit_solution(981204315018577703)
XLA Ops:
  1.5 5.1 %collective-permute-start.5 = (bf16[1,288]{1,0:T(2,128)(2,1)S(1)}, bf16[1,288]{1,0:T(2,128)(2,1)S(1)}, u32[]{:S(2)}, u32[]{:S(2)}) collective-permute-start(bf16[1,288]{1,0:T(2,128)(2,1)S(1)} %broadcast_in_dim.2), channel_id=1, source_target_pairs={{0,24},{4,28},{8,16},{12,20},{16,8},{20,12},{24,0},{28,4},{1,25},{... | collective-permute-start | bytes 1736 | tf_op jit(solution)/shard_map/ppermute | solution.py:304
  74.2 10.1 %collective-permute-done.8 = bf16[128,1024]{1,0:T(8,128)(2,1)S(1)} collective-permute-done((bf16[128,1024]{1,0:T(8,128)(2,1)}, bf16[128,1024]{1,0:T(8,128)(2,1)S(1)}, u32[]{:S(2)}, u32[]{:S(2)}) %collective-permute-start.8) | collective-permute-done | bytes 262176 | tf_op jit(solution)/shard_map/ppermute | solution.py:304
  87.4 5.6 %collective-permute-done.18 = bf16[128,512]{0,1:T(8,128)(2,1)S(1)} collective-permute-done((bf16[128,512]{0,1:T(8,128)(2,1)S(1)}, bf16[128,512]{0,1:T(8,128)(2,1)S(1)}, u32[]{:S(2)}, u32[]{:S(2)}) %collective-permute-start.18) | collective-permute-done | bytes 131104 | tf_op jit(solution)/shard_map/ppermute | solution.py:304
  107.5 5.3 %collective-permute-done.13 = bf16[128,1024]{1,0:T(8,128)(2,1)S(1)} collective-permute-done((bf16[128,1024]{1,0:T(8,128)(2,1)S(1)}, bf16[128,1024]{1,0:T(8,128)(2,1)S(1)}, u32[]{:S(2)}, u32[]{:S(2)}) %collective-permute-start.13) | collective-permute-done | bytes 262176 | tf_op jit(solution)/shard_map/ppermute | solution.py:304
  119.6 8.1 %shard_map.246 = (bf16[1024,1024]{1,0:T(8,128)(2,1)}, bf16[1024,1024]{1,0:T(8,128)(2,1)}, f32[1024,768]{1,0:T(8,128)}) custom-call(s32[1]{0:T(128)} %bitcast.t, bf16[1024,1024]{1,0:T(8,128)(2,1)} %pad_maximum_fusion.x, f32[1,1024]{1,0:T(1,128)} %bitcast.88, bf16[1024,1024]{1,0:T(8,128)(2,1)} %copy-done.25, f32[1024,128]{1,0:T(8,128)} %get-tuple-element.139.cos, ...), custom_call_target="tpu_custom_call" | custom-call | flops 2147483648 | bytes 11534336 | tf_op jit(solution)/shard_map/pallas_call | solution.py:80
  127.7 8.8 %shard_map.247 = (bf16[1024,512]{1,0:T(8,128)(2,1)}, f32[2,8,1024]{2,1,0:T(8,128)}) custom-call(s32[1]{0:T(128)} %bitcast.t, bf16[1024,1024]{1,0:T(8,128)(2,1)} %get-tuple-element.24.packed, s32[1024,1]{1,0:T(8,128)} %copy.33.seg_col, s32[1,1024]{1,0:T(1,128)} %seg_row.3), custom_call_target="tpu_custom_call" | custom-call | flops 2147483648 | bytes 3145728 | tf_op jit(solution)/shard_map/pallas_call | solution.py:139
  159.8 7.8 %collective-permute-done.23 = bf16[256,1024]{1,0:T(8,128)(2,1)S(1)} collective-permute-done((bf16[256,1024]{1,0:T(8,128)(2,1)S(1)}, bf16[256,1024]{1,0:T(8,128)(2,1)S(1)}, u32[]{:S(2)}, u32[]{:S(2)}) %collective-permute-start.23) | collective-permute-done | bytes 524320 | tf_op jit(solution)/shard_map/ppermute | solution.py:307
  171.6 10.3 %collective-permute-done.34 = bf16[128,1536]{1,0:T(8,128)(2,1)S(1)} collective-permute-done((bf16[128,1536]{1,0:T(8,128)(2,1)}, bf16[128,1536]{1,0:T(8,128)(2,1)S(1)}, u32[]{:S(2)}, u32[]{:S(2)}) %collective-permute-start.34) | collective-permute-done | bytes 393248 | tf_op jit(solution)/shard_map/ppermute | solution.py:304
  183.9 5.9 %collective-permute-done.36 = bf16[128,1536]{1,0:T(8,128)(2,1)S(1)} collective-permute-done((bf16[128,1536]{1,0:T(8,128)(2,1)S(1)}, bf16[128,1536]{1,0:T(8,128)(2,1)S(1)}, u32[]{:S(2)}, u32[]{:S(2)}) %collective-permute-start.36) | collective-permute-done | bytes 393248 | tf_op jit(solution)/shard_map/ppermute | solution.py:304
  193.7 15.7 %shard_map.248 = (bf16[1024,768]{1,0:T(8,128)(2,1)}, bf16[1024,1536]{1,0:T(8,128)(2,1)}, bf16[1024,1024]{1,0:T(8,128)(2,1)}, bf16[1024,1024]{1,0:T(8,128)(2,1)}) custom-call(s32[1]{0:T(128)} %bitcast.t, bf16[1024,1024]{1,0:T(8,128)(2,1)} %pad_maximum_fusion.1.x, bf16[1024,1024]{1,0:T(8,128)(2,1)} %pad_maximum_fusion.2.g, ...), custom_call_target="tpu_custom_call" | custom-call | flops 9663676416 | bytes 17825792 | tf_op jit(solution)/shard_map/pallas_call | solution.py:276
  209.5 5.4 %convolution_convert_fusion = bf16[512,1536]{1,0:T(8,128)(2,1)} fusion(bf16[1024,1536]{1,0:T(8,128)(2,1)} %get-tuple-element.32, bf16[1024,1024]{1,0:T(8,128)(2,1)} %pad_maximum_fusion.1.x), kind=kOutput, calls=%fused_computation | convolution fusion | flops 1611399168 | bytes 5767168 | tf_op jit(solution)/shard_map/dot_general | solution.py:21
  226.1 12.0 %collective-permute-done.68 = bf16[512,768]{1,0:T(8,128)(2,1)S(1)} collective-permute-done((bf16[512,768]{1,0:T(8,128)(2,1)S(1)}, bf16[512,768]{1,0:T(8,128)(2,1)S(1)}, u32[]{:S(2)}, u32[]{:S(2)}) %collective-permute-start.68) | collective-permute-done | bytes 786464 | tf_op jit(solution)/shard_map/ppermute | solution.py:304
  245.5 6.3 %collective-permute-done.71 = bf16[128,768]{1,0:T(8,128)(2,1)S(1)} collective-permute-done((bf16[128,768]{1,0:T(8,128)(2,1)S(1)}, bf16[128,768]{1,0:T(8,128)(2,1)S(1)}, u32[]{:S(2)}, u32[]{:S(2)}) %collective-permute-start.71) | collective-permute-done | bytes 196640 | tf_op jit(solution)/shard_map/ppermute | solution.py:304
  253.3 4.8 %collective-permute-done.70 = bf16[128,768]{1,0:T(8,128)(2,1)S(1)} collective-permute-done((bf16[128,768]{1,0:T(8,128)(2,1)S(1)}, bf16[128,768]{1,0:T(8,128)(2,1)S(1)}, u32[]{:S(2)}, u32[]{:S(2)}) %collective-permute-start.70) | collective-permute-done | bytes 196640 | tf_op jit(solution)/shard_map/ppermute | solution.py:304
  262.6 7.8 %collective-permute-done.46 = bf16[256,1024]{1,0:T(8,128)(2,1)} collective-permute-done((bf16[256,1024]{1,0:T(8,128)(2,1)}, bf16[256,1024]{1,0:T(8,128)(2,1)}, u32[]{:S(2)}, u32[]{:S(2)}) %collective-permute-start.46) | collective-permute-done | bytes 524320 | tf_op jit(solution)/shard_map/ppermute | solution.py:307
  275.2 8.8 %collective-permute-done.64 = bf16[512,1536]{1,0:T(8,128)(2,1)} collective-permute-done((bf16[512,1536]{1,0:T(8,128)(2,1)}, bf16[512,1536]{1,0:T(8,128)(2,1)}, u32[]{:S(2)}, u32[]{:S(2)}) %collective-permute-start.64) | collective-permute-done | bytes 1572896 | tf_op jit(solution)/shard_map/ppermute | solution.py:304
  289.8 6.1 %collective-permute-done.65 = bf16[128,1536]{1,0:T(8,128)(2,1)S(1)} collective-permute-done((bf16[128,1536]{1,0:T(8,128)(2,1)S(1)}, bf16[128,1536]{1,0:T(8,128)(2,1)S(1)}, u32[]{:S(2)}, u32[]{:S(2)}) %collective-permute-start.65) | collective-permute-done | bytes 393248 | tf_op jit(solution)/shard_map/ppermute | solution.py:304
  295.9 11.6 %collective-permute-done.67 = bf16[128,1536]{1,0:T(8,128)(2,1)S(1)} collective-permute-done((bf16[128,1536]{1,0:T(8,128)(2,1)S(1)}, bf16[128,1536]{1,0:T(8,128)(2,1)S(1)}, u32[]{:S(2)}, u32[]{:S(2)}) %collective-permute-start.67) | collective-permute-done | bytes 393248 | tf_op jit(solution)/shard_map/ppermute | solution.py:304
  307.4 13.8 %collective-permute-done.66 = bf16[128,1536]{1,0:T(8,128)(2,1)S(1)} collective-permute-done((bf16[128,1536]{1,0:T(8,128)(2,1)S(1)}, bf16[128,1536]{1,0:T(8,128)(2,1)S(1)}, u32[]{:S(2)}, u32[]{:S(2)}) %collective-permute-start.66) | collective-permute-done | bytes 393248 | tf_op jit(solution)/shard_map/ppermute | solution.py:304
  329.2 18.0 %shard_map.249 = (bf16[1024,1024]{1,0:T(8,128)(2,1)}, f32[2,8,128]{2,1,0:T(8,128)}) custom-call(s32[1]{0:T(128)} %bitcast.t, bf16[1024,1024]{1,0:T(8,128)(2,1)} %get-tuple-element.24.packed, s32[1024,1]{1,0:T(8,128)} %copy.33.seg_col, s32[1,1024]{1,0:T(1,128)} %seg_row.3, f32[2,8,1024]{2,1,0:T(8,128)} %get-tuple-element.28.inv, ...), custom_call_target="tpu_custom_call" | custom-call | flops 5368709120 | bytes 11010048 | tf_op jit(solution)/shard_map/pallas_call | solution.py:232
  357.5 5.2 %collective-permute-done.60 = bf16[512,512]{1,0:T(8,128)(2,1)S(1)} collective-permute-done((bf16[512,512]{1,0:T(8,128)(2,1)S(1)}, bf16[512,512]{1,0:T(8,128)(2,1)S(1)}, u32[]{:S(2)}, u32[]{:S(2)}) %collective-permute-start.60) | collective-permute-done | bytes 524320 | tf_op jit(solution)/shard_map/ppermute | solution.py:304
  389.5 6.1 %collective-permute-done.74 = f32[18,128]{1,0:T(8,128)S(1)} collective-permute-done((f32[18,128]{1,0:T(8,128)S(1)}, f32[18,128]{1,0:T(8,128)S(1)}, u32[]{:S(2)}, u32[]{:S(2)}) %collective-permute-start.74) | collective-permute-done | bytes 9248 | tf_op jit(solution)/shard_map/ppermute | solution.py:304
  409.3 4.8 %collective-permute-done.59 = bf16[128,1024]{1,0:T(8,128)(2,1)S(1)} collective-permute-done((bf16[128,1024]{1,0:T(8,128)(2,1)S(1)}, bf16[128,1024]{1,0:T(8,128)(2,1)S(1)}, u32[]{:S(2)}, u32[]{:S(2)}) %collective-permute-start.59) | collective-permute-done | bytes 262176 | tf_op jit(solution)/shard_map/ppermute | solution.py:304
  414.1 8.7 %collective-permute-done.58 = bf16[128,1024]{1,0:T(8,128)(2,1)S(1)} collective-permute-done((bf16[128,1024]{1,0:T(8,128)(2,1)S(1)}, bf16[128,1024]{1,0:T(8,128)(2,1)S(1)}, u32[]{:S(2)}, u32[]{:S(2)}) %collective-permute-start.58) | collective-permute-done | bytes 262176 | tf_op jit(solution)/shard_map/ppermute | solution.py:304
  (363 shorter events, 222.5 us)
Async XLA Ops:
  1.5 36.4 %collective-permute-start.5 = (bf16[1,288]{1,0:T(2,128)(2,1)S(1)}, bf16[1,288]{1,0:T(2,128)(2,1)S(1)}, u32[]{:S(2)}, u32[]{:S(2)}) collective-permute-start(bf16[1,288]{1,0:T(2,128)(2,1)S(1)} %broadcast_in_dim.2), channel_id=1, source_target_pairs={{0,24},{4,28},{8,16},{12,20},{16,8},{20,12},{24,0},{28,4},{1,25},{... | collective-permute-start | bytes 1736 | tf_op jit(solution)/shard_map/ppermute | solution.py:304
  6.6 31.3 %collective-permute-start.4 = (bf16[1,288]{1,0:T(2,128)(2,1)S(1)}, bf16[1,288]{1,0:T(2,128)(2,1)S(1)}, u32[]{:S(2)}, u32[]{:S(2)}) collective-permute-start(bf16[1,288]{1,0:T(2,128)(2,1)S(1)} %broadcast_in_dim.2), channel_id=1, source_target_pairs={{0,16},{4,20},{8,24},{12,28},{16,0},{20,4},{24,8},{28,12},{1,17},{... | collective-permute-start | bytes 1736 | tf_op jit(solution)/shard_map/ppermute | solution.py:304
  6.6 32.1 %collective-permute-start.3 = (bf16[1,288]{1,0:T(2,128)(2,1)S(1)}, bf16[1,288]{1,0:T(2,128)(2,1)S(1)}, u32[]{:S(2)}, u32[]{:S(2)}) collective-permute-start(bf16[1,288]{1,0:T(2,128)(2,1)S(1)} %broadcast_in_dim.2), channel_id=1, source_target_pairs={{0,8},{4,12},{8,0},{12,4},{16,24},{20,28},{24,16},{28,20},{1,9},{5... | collective-permute-start | bytes 1736 | tf_op jit(solution)/shard_map/ppermute | solution.py:304
  7.3 44.0 %collective-permute-start.17 = (bf16[128,512]{0,1:T(8,128)(2,1)}, bf16[128,512]{0,1:T(8,128)(2,1)S(1)}, u32[]{:S(2)}, u32[]{:S(2)}) collective-permute-start(bf16[128,512]{0,1:T(8,128)(2,1)} %bitcast.78), channel_id=1, source_target_pairs={{0,4},{4,0},{8,12},{12,8},{16,20},{20,16},{24,28},{28,24},{1,5},{5... | collective-permute-start | bytes 393224 | tf_op jit(solution)/shard_map/ppermute | solution.py:304
  8.9 41.0 %collective-permute-start.16 = (bf16[128,512]{0,1:T(8,128)(2,1)}, bf16[128,512]{0,1:T(8,128)(2,1)S(1)}, u32[]{:S(2)}, u32[]{:S(2)}) collective-permute-start(bf16[128,512]{0,1:T(8,128)(2,1)} %bitcast.79), channel_id=1, source_target_pairs={{0,24},{4,28},{8,16},{12,20},{16,8},{20,12},{24,0},{28,4},{1,25},{... | collective-permute-start | bytes 393224 | tf_op jit(solution)/shard_map/ppermute | solution.py:304
  42.4 25.2 %collective-permute-start.40 = (bf16[128,768]{1,0:T(8,128)(2,1)S(1)}, bf16[128,768]{1,0:T(8,128)(2,1)S(1)}, u32[]{:S(2)}, u32[]{:S(2)}) collective-permute-start(bf16[128,768]{1,0:T(8,128)(2,1)S(1)} %bitcast.74), channel_id=1, source_target_pairs={{0,4},{4,0},{8,12},{12,8},{16,20},{20,16},{24,28},{28,24},{1,5},{5... | collective-permute-start | bytes 589832 | tf_op jit(solution)/shard_map/ppermute | solution.py:304
  51.3 45.8 %collective-permute-start.1 = (bf16[256,1024]{1,0:T(8,128)(2,1)S(1)}, bf16[256,1024]{1,0:T(8,128)(2,1)S(1)}, u32[]{:S(2)}, u32[]{:S(2)}) collective-permute-start(bf16[256,1024]{1,0:T(8,128)(2,1)S(1)} %constant_dynamic-update-slice_fusion), channel_id=1, source_target_pairs={{0,2},{1,3},{2,0},{3,1},{4,6},{5,7},{6,4},{7,5},{8,10},{9,11},{10,... | collective-permute-start | bytes 1572872 | tf_op jit(solution)/shard_map/ppermute | solution.py:307
  58.0 57.1 %collective-permute-start = (bf16[256,1024]{1,0:T(8,128)(2,1)S(1)}, bf16[256,1024]{1,0:T(8,128)(2,1)S(1)}, u32[]{:S(2)}, u32[]{:S(2)}) collective-permute-start(bf16[256,1024]{1,0:T(8,128)(2,1)S(1)} %constant_dynamic-update-slice_fusion), channel_id=1, source_target_pairs={{0,1},{1,0},{2,3},{3,2},{4,5},{5,4},{6,7},{7,6},{8,9},{9,8},{10,11... | collective-permute-start | bytes 1572872 | tf_op jit(solution)/shard_map/ppermute | solution.py:307
  101.6 55.4 %collective-permute-start.33 = (bf16[128,1536]{1,0:T(8,128)(2,1)}, bf16[128,1536]{1,0:T(8,128)(2,1)S(1)}, u32[]{:S(2)}, u32[]{:S(2)}) collective-permute-start(bf16[128,1536]{1,0:T(8,128)(2,1)} %get-tuple-element.99), channel_id=1, source_target_pairs={{0,4},{4,0},{8,12},{12,8},{16,20},{20,16},{24,28},{28,24},{1,5},{5... | collective-permute-start | bytes 1179656 | tf_op jit(solution)/shard_map/ppermute | solution.py:304
  107.2 49.0 %collective-permute-start.32 = (bf16[128,1536]{1,0:T(8,128)(2,1)}, bf16[128,1536]{1,0:T(8,128)(2,1)S(1)}, u32[]{:S(2)}, u32[]{:S(2)}) collective-permute-start(bf16[128,1536]{1,0:T(8,128)(2,1)} %get-tuple-element.99), channel_id=1, source_target_pairs={{0,24},{4,28},{8,16},{12,20},{16,8},{20,12},{24,0},{28,4},{1,25},{... | collective-permute-start | bytes 1179656 | tf_op jit(solution)/shard_map/ppermute | solution.py:304
  112.9 28.4 %collective-permute-start.31 = (bf16[128,1536]{1,0:T(8,128)(2,1)}, bf16[128,1536]{1,0:T(8,128)(2,1)}, u32[]{:S(2)}, u32[]{:S(2)}) collective-permute-start(bf16[128,1536]{1,0:T(8,128)(2,1)} %get-tuple-element.99), channel_id=1, source_target_pairs={{0,16},{4,20},{8,24},{12,28},{16,0},{20,4},{24,8},{28,12},{1,17},{... | collective-permute-start | bytes 1179656 | tf_op jit(solution)/shard_map/ppermute | solution.py:304
  115.1 24.2 %collective-permute-start.30 = (bf16[128,1536]{1,0:T(8,128)(2,1)}, bf16[128,1536]{1,0:T(8,128)(2,1)}, u32[]{:S(2)}, u32[]{:S(2)}) collective-permute-start(bf16[128,1536]{1,0:T(8,128)(2,1)} %get-tuple-element.99), channel_id=1, source_target_pairs={{0,8},{4,12},{8,0},{12,4},{16,24},{20,28},{24,16},{28,20},{1,9},{5... | collective-permute-start | bytes 1179656 | tf_op jit(solution)/shard_map/ppermute | solution.py:304
  116.5 54.2 %collective-permute-start.28 = (bf16[256,1024]{1,0:T(8,128)(2,1)S(1)}, bf16[256,1024]{1,0:T(8,128)(2,1)S(1)}, u32[]{:S(2)}, u32[]{:S(2)}) collective-permute-start(bf16[256,1024]{1,0:T(8,128)(2,1)S(1)} %constant_dynamic-update-slice_fusion.35), channel_id=1, source_target_pairs={{0,2},{1,3},{2,0},{3,1},{4,6},{5,7},{6,4},{7,5},{8,10},{9,11},{10,... | collective-permute-start | bytes 1572872 | tf_op jit(solution)/shard_map/ppermute | solution.py:307
  156.2 34.4 %collective-permute-start.27 = (bf16[256,1024]{1,0:T(8,128)(2,1)S(1)}, bf16[256,1024]{1,0:T(8,128)(2,1)S(1)}, u32[]{:S(2)}, u32[]{:S(2)}) collective-permute-start(bf16[256,1024]{1,0:T(8,128)(2,1)S(1)} %constant_dynamic-update-slice_fusion.35), channel_id=1, source_target_pairs={{0,1},{1,0},{2,3},{3,2},{4,5},{5,4},{6,7},{7,6},{8,9},{9,8},{10,11... | collective-permute-start | bytes 1572872 | tf_op jit(solution)/shard_map/ppermute | solution.py:307
  159.0 23.6 %collective-permute-start.35 = (bf16[128,1536]{1,0:T(8,128)(2,1)}, bf16[128,1536]{1,0:T(8,128)(2,1)S(1)}, u32[]{:S(2)}, u32[]{:S(2)}) collective-permute-start(bf16[128,1536]{1,0:T(8,128)(2,1)} %collective-permute-done.31), channel_id=1, source_target_pairs={{0,4},{4,0},{8,12},{12,8},{16,20},{20,16},{24,28},{28,24},{1,5},{5... | collective-permute-start | bytes 1179656 | tf_op jit(solution)/shard_map/ppermute | solution.py:304
  223.5 37.2 %collective-permute-start.47 = (bf16[256,1024]{1,0:T(8,128)(2,1)}, bf16[256,1024]{1,0:T(8,128)(2,1)S(1)}, u32[]{:S(2)}, u32[]{:S(2)}) collective-permute-start(bf16[256,1024]{1,0:T(8,128)(2,1)} %get-tuple-element.77), channel_id=1, source_target_pairs={{0,1},{1,0},{2,3},{3,2},{4,5},{5,4},{6,7},{7,6},{8,9},{9,8},{10,11... | collective-permute-start | bytes 1572872 | tf_op jit(solution)/shard_map/ppermute | solution.py:307
  224.6 36.1 %collective-permute-start.49 = (bf16[256,1024]{1,0:T(8,128)(2,1)}, bf16[256,1024]{1,0:T(8,128)(2,1)S(1)}, u32[]{:S(2)}, u32[]{:S(2)}) collective-permute-start(bf16[256,1024]{1,0:T(8,128)(2,1)} %add_convert_fusion.1), channel_id=1, source_target_pairs={{0,2},{1,3},{2,0},{3,1},{4,6},{5,7},{6,4},{7,5},{8,10},{9,11},{10,... | collective-permute-start | bytes 1572872 | tf_op jit(solution)/shard_map/ppermute | solution.py:307
  251.8 32.1 %collective-permute-start.64 = (bf16[512,1536]{1,0:T(8,128)(2,1)}, bf16[512,1536]{1,0:T(8,128)(2,1)}, u32[]{:S(2)}, u32[]{:S(2)}) collective-permute-start(bf16[512,1536]{1,0:T(8,128)(2,1)} %convolution_convert_fusion), channel_id=1, source_target_pairs={{0,4},{4,0},{8,12},{12,8},{16,20},{20,16},{24,28},{28,24},{1,5},{5... | collective-permute-start | bytes 4718600 | tf_op jit(solution)/shard_map/ppermute | solution.py:304
  274.5 49.0 %collective-permute-start.50 = (bf16[256,1024]{1,0:T(8,128)(2,1)S(1)}, bf16[256,1024]{1,0:T(8,128)(2,1)S(1)}, u32[]{:S(2)}, u32[]{:S(2)}) collective-permute-start(bf16[256,1024]{1,0:T(8,128)(2,1)S(1)} %get-tuple-element.65), channel_id=1, source_target_pairs={{0,1},{1,0},{2,3},{3,2},{4,5},{5,4},{6,7},{7,6},{8,9},{9,8},{10,11... | collective-permute-start | bytes 1572872 | tf_op jit(solution)/shard_map/ppermute | solution.py:307
  285.6 21.8 %collective-permute-start.67 = (bf16[128,1536]{1,0:T(8,128)(2,1)S(1)}, bf16[128,1536]{1,0:T(8,128)(2,1)S(1)}, u32[]{:S(2)}, u32[]{:S(2)}) collective-permute-start(bf16[128,1536]{1,0:T(8,128)(2,1)S(1)} %get-tuple-element.70), channel_id=1, source_target_pairs={{0,24},{4,28},{8,16},{12,20},{16,8},{20,12},{24,0},{28,4},{1,25},{... | collective-permute-start | bytes 1179656 | tf_op jit(solution)/shard_map/ppermute | solution.py:304
  289.0 32.3 %collective-permute-start.66 = (bf16[128,1536]{1,0:T(8,128)(2,1)S(1)}, bf16[128,1536]{1,0:T(8,128)(2,1)S(1)}, u32[]{:S(2)}, u32[]{:S(2)}) collective-permute-start(bf16[128,1536]{1,0:T(8,128)(2,1)S(1)} %get-tuple-element.71), channel_id=1, source_target_pairs={{0,16},{4,20},{8,24},{12,28},{16,0},{20,4},{24,8},{28,12},{1,17},{... | collective-permute-start | bytes 1179656 | tf_op jit(solution)/shard_map/ppermute | solution.py:304
  289.7 33.7 %collective-permute-start.52 = (bf16[256,1024]{1,0:T(8,128)(2,1)S(1)}, bf16[256,1024]{1,0:T(8,128)(2,1)S(1)}, u32[]{:S(2)}, u32[]{:S(2)}) collective-permute-start(bf16[256,1024]{1,0:T(8,128)(2,1)S(1)} %collective-permute-done.51), channel_id=1, source_target_pairs={{0,1},{1,0},{2,3},{3,2},{4,5},{5,4},{6,7},{7,6},{8,9},{9,8},{10,11... | collective-permute-start | bytes 1572872 | tf_op jit(solution)/shard_map/ppermute | solution.py:307
  354.7 24.5 %collective-permute-start.53 = (bf16[256,1024]{1,0:T(8,128)(2,1)}, bf16[256,1024]{1,0:T(8,128)(2,1)S(1)}, u32[]{:S(2)}, u32[]{:S(2)}) collective-permute-start(bf16[256,1024]{1,0:T(8,128)(2,1)} %get-tuple-element.75), channel_id=1, source_target_pairs={{0,1},{1,0},{2,3},{3,2},{4,5},{5,4},{6,7},{7,6},{8,9},{9,8},{10,11... | collective-permute-start | bytes 1572872 | tf_op jit(solution)/shard_map/ppermute | solution.py:307
  373.8 26.2 %collective-permute-start.56 = (bf16[512,1024]{1,0:T(8,128)(2,1)}, bf16[512,1024]{1,0:T(8,128)(2,1)}, u32[]{:S(2)}, u32[]{:S(2)}) collective-permute-start(bf16[512,1024]{1,0:T(8,128)(2,1)} %convolution_convert_fusion.4), channel_id=1, source_target_pairs={{0,4},{4,0},{8,12},{12,8},{16,20},{20,16},{24,28},{28,24},{1,5},{5... | collective-permute-start | bytes 3145736 | tf_op jit(solution)/shard_map/ppermute | solution.py:304
  (84 other events, 985.2 us)

commit v2 on v1

v2 whole, which is shorter than its diff:
```python
import functools

import jax
import jax.numpy as jnp
from jax import lax
from jax.experimental import pallas as pl
from jax.experimental.pallas import tpu as pltpu
from jax.sharding import PartitionSpec as P

HEAD = 128
EPS = 1e-06
ROPE_BASE = 1000000.0
SCALE = HEAD ** (-0.5)
EXP2_SCALE = SCALE * 1.4426950408889634
F32 = jnp.float32
BF16 = jnp.bfloat16
VMEM_LIMIT = 60 * 1024 * 1024
ORDER = (0, 2, 4, 6, 1, 3, 5, 7)
GAIN_ROWS = 16
ROW_STEPS = 1


def mm(a, b, ca=1, cb=0):
    return lax.dot_general(a, b, (((ca,), (cb,)), ((), ())), preferred_element_type=F32)


def shape_of(shape, dtype=BF16):
    return jax.ShapeDtypeStruct(shape, dtype)


def call(kernel, grid, in_specs, out_specs, out_shape, flops, scratch=()):
    return pl.pallas_call(
        kernel,
        out_shape=out_shape,
        grid_spec=pltpu.PrefetchScalarGridSpec(
            num_scalar_prefetch=1,
            grid=grid,
            in_specs=in_specs,
            out_specs=out_specs,
            scratch_shapes=list(scratch),
        ),
        compiler_params=pltpu.CompilerParams(
            dimension_semantics=("arbitrary",) * len(grid), vmem_limit_bytes=VMEM_LIMIT
        ),
        cost_estimate=pl.CostEstimate(flops=1, bytes_accessed=1, transcendentals=0),
    )


def tie(x, *after):
    return lax.optimization_barrier((x, after))[0]


def whole(shape):
    return pl.BlockSpec(shape, lambda i, t: (0,) * len(shape))


def part_at(shape, index):
    return pl.BlockSpec(shape, lambda i, t: (0, index))


def rows_at(rows, cols):
    return pl.BlockSpec((rows, cols), lambda i, t: (i, 0))


def rows_xor(rows, cols):
    return pl.BlockSpec((rows, cols), lambda i, t: (lax.bitwise_xor(i, t[0]), 0))


def model_block(t, p):
    return pl.multiple_of(lax.bitwise_xor(t[1], ORDER[p]) * HEAD, HEAD)


def pack_attn_kernel(kv_heads, group, t, wq, wk, wv, wo, g_attn, g_mlp, g_query, g_key, out):
    n = wq.shape[0]
    for h in range(kv_heads):
        base = h * (group + 2) * HEAD
        mid = base + group * HEAD
        out[:n, base:mid] = wq[:, h * group * HEAD : (h + 1) * group * HEAD]
        out[:n, mid : mid + HEAD] = wk[:, h * HEAD : (h + 1) * HEAD]
        out[:n, mid + HEAD : mid + 2 * HEAD] = wv[:, h * HEAD : (h + 1) * HEAD]
    out[:n, kv_heads * (group + 2) * HEAD :] = wo[...].T
    out[n:, :] = jnp.zeros((GAIN_ROWS, out.shape[1]), BF16)
    m = g_query.shape[1]
    place = lax.broadcasted_iota(jnp.int32, (m, HEAD), 0) + t[1] * m == lax.broadcasted_iota(
        jnp.int32, (m, HEAD), 1
    )
    place = jnp.where(place, 1.0, 0.0).astype(BF16)
    rows = (g_attn[...].astype(F32), g_mlp[...].astype(F32), mm(g_query[...], place), mm(g_key[...], place))
    at = lax.broadcasted_iota(jnp.int32, (GAIN_ROWS, HEAD), 0)
    tile = jnp.zeros((GAIN_ROWS, HEAD), F32)
    for k, row in enumerate(rows):
        tile = jnp.where(at == k, row, tile)
    out[n:, :HEAD] = tile.astype(BF16)


def pack_attn(t, wq, wk, wv, wo, gains, kv_heads, group):
    n = wq.shape[0]
    cols = kv_heads * (group + 2) * HEAD + wo.shape[0]
    args = (wq, wk, wv, wo, *[g[None, :] for g in gains])
    return call(
        functools.partial(pack_attn_kernel, kv_heads, group),
        (1,),
        [whole(a.shape) for a in args],
        whole((n + GAIN_ROWS, cols)),
        shape_of((n + GAIN_ROWS, cols)),
        n * cols,
    )(t, *args)


def pack_rows_kernel(t, x, g, out):
    width = x.shape[1]
    for p in range(width // HEAD):
        at = model_block(t, p)
        out[:, p * HEAD : (p + 1) * HEAD] = x[:, pl.ds(at, HEAD)]
        out[:, width + p * HEAD : width + (p + 1) * HEAD] = g[:, pl.ds(at, HEAD)]


def pack_rows(t, x, g):
    n, width = x.shape
    return call(
        pack_rows_kernel,
        (1,),
        [whole(x.shape), whole(g.shape)],
        whole((n, 2 * width)),
        shape_of((n, 2 * width)),
        n * width,
    )(t, x, g)


def pack_mlp_kernel(t, wg, wu, wd, out):
    ff = wg.shape[1]
    out[:, :ff] = wg[...]
    out[:, ff : 2 * ff] = wu[...]
    out[:, 2 * ff :] = wd[...].T


def pack_mlp(t, wg, wu, wd):
    shape = (wg.shape[0], 3 * wg.shape[1])
    args = (wg, wu, wd)
    return call(
        pack_mlp_kernel,
        (1,),
        [whole(a.shape) for a in args],
        whole(shape),
        shape_of(shape),
        shape[0] * shape[1],
    )(t, *args)


def join(blocks, out):
    n = out.shape[0] // len(blocks)
    for p, b in enumerate(blocks):
        out[p * n : (p + 1) * n, :] = b[:n, :]


def qkv_kernel(nx, nw, packed_gains, kv_heads, group, t, *refs):
    xs, ws = refs[:nx], refs[nx : nx + nw]
    gains_in, cos, sin, normed, packed, raw, gains, w, x = refs[nx + nw :]
    i = pl.program_id(0)

    @pl.when(i == 0)
    def _():
        join(ws, w)
        if packed_gains:
            n = w.shape[0] // nw
            gains[...] = jnp.zeros_like(gains)
            heads = jnp.zeros((GAIN_ROWS, HEAD), F32)
            for p, b in enumerate(ws):
                tile = b[n:, :HEAD].astype(F32)
                gains[0:2, p * n : (p + 1) * n] = tile[0:2]
                heads = heads + tile
            gains[2:4, :HEAD] = heads[2:4]
        else:
            gains[...] = gains_in[...]

    for k in range(nx):

        @pl.when(i == k)
        def _(k=k):
            x[...] = xs[k][...]

    u = x[...].astype(F32)
    r = lax.rsqrt(jnp.mean(u * u, axis=1, keepdims=True) + EPS)
    low = (u * r * gains[0:1, :]).astype(BF16)
    normed[...] = low
    y = mm(low, w[...])
    c = cos[...]
    s = sin[...]
    gq = gains[2:3, :HEAD]
    gk = gains[3:4, :HEAD]
    for h in range(kv_heads):
        base = h * (group + 2) * HEAD
        kept = h * (group + 1) * HEAD
        for j in range(group + 1):
            v = y[:, base + j * HEAD : base + (j + 1) * HEAD]
            raw[:, kept + j * HEAD : kept + (j + 1) * HEAD] = v
            scale = gq if j < group else gk
            v = v * lax.rsqrt(jnp.mean(v * v, axis=1, keepdims=True) + EPS) * scale
            v = v * c + pltpu.roll(v, HEAD // 2, 1) * s
            packed[:, base + j * HEAD : base + (j + 1) * HEAD] = v.astype(BF16)
        end = base + (group + 1) * HEAD
        packed[:, end : end + HEAD] = y[:, end : end + HEAD].astype(BF16)


def qkv_call(t, xs, ws, gains, packed_gains, cos, sin, width, kv_heads, group):
    rows = xs[0].shape[0]
    n = rows * len(xs)
    cols = kv_heads * (group + 2) * HEAD
    kept = kv_heads * (group + 1) * HEAD
    return call(
        functools.partial(qkv_kernel, len(xs), len(ws), packed_gains, kv_heads, group),
        (len(xs),),
        [part_at((rows, width), 0) for _ in xs]
        + [part_at((w.shape[0], cols), 0) for w in ws]
        + [whole(gains.shape), rows_xor(rows, HEAD), rows_xor(rows, HEAD)],
        [rows_at(rows, width), rows_xor(rows, cols), rows_xor(rows, kept), whole((8, width))],
        [
            shape_of((n, width)),
            shape_of((n, cols)),
            shape_of((n, kept), F32),
            shape_of((8, width), F32),
        ],
        2 * n * width * cols,
        [pltpu.VMEM((width, cols), BF16), pltpu.VMEM((rows, width), BF16)],
    )(t, *xs, *ws, gains, cos, sin)


def weights_of(q, k, same, causal):
    e = jnp.exp2(mm(k, q, 1, 1) * EXP2_SCALE)
    keep = same if causal is None else same & causal
    return jnp.where(keep, e, 0.0)


def accumulate(part, acc):
    h = pl.program_id(0)

    @pl.when(h == 0)
    def _():
        acc[...] = part

    @pl.when(h > 0)
    def _():
        acc[...] += part


def split_rows(rows, acc, keep, send):
    for k in range(acc.shape[0] // rows):
        out = send if k % 2 else keep
        at = (k // 2) * rows
        out[at : at + rows, :] = acc[k * rows : (k + 1) * rows, :].astype(BF16)


def attn_forward_kernel(rows, blocks, group, kv_heads, nw, t, packed, seg_col, seg_row, *refs):
    ws = refs[:nw]
    mixed, inv, keep, send, w, acc = refs[nw:]
    causal = lax.broadcasted_iota(jnp.int32, (rows, rows), 0) <= lax.broadcasted_iota(
        jnp.int32, (rows, rows), 1
    )
    kc = group * HEAD
    join(ws, w)
    for i in range(blocks):
        lo = i * rows
        at = pl.multiple_of(lax.bitwise_xor(i, t[0]) * rows, rows)
        sq = seg_row[:, lo : lo + rows]
        for j in range(group):
            q = packed[lo : lo + rows, j * HEAD : (j + 1) * HEAD]
            parts = []
            total = jnp.zeros((1, rows), F32)
            for b in range(i + 1):
                k = packed[b * rows : (b + 1) * rows, kc : kc + HEAD]
                same = seg_col[b * rows : (b + 1) * rows, :] == sq
                e = weights_of(q, k, same, causal if b == i else None)
                total = total + jnp.sum(e, axis=0, keepdims=True)
                parts.append(e)
            rec = 1.0 / total
            inv[0, j : j + 1, lo : lo + rows] = rec
            out = jnp.zeros((rows, HEAD), F32)
            for b in range(i + 1):
                v = packed[b * rows : (b + 1) * rows, kc + HEAD : kc + 2 * HEAD]
                out = out + mm((parts[b] * rec).astype(BF16), v, 0, 0)
            mixed[pl.ds(at, rows), j * HEAD : (j + 1) * HEAD] = out.astype(BF16)
    accumulate(mm(mixed[...], w[...], 1, 1), acc)

    @pl.when(pl.program_id(0) == kv_heads - 1)
    def _():
        split_rows(rows, acc, keep, send)


def by_head(n, width, first=0):
    return pl.BlockSpec((n, width), lambda h, t: (0, first + h))


def attn_forward(t, packed, seg_col, seg_row, w_o, first, rows, width, kv_heads, group):
    n = packed.shape[0]
    q_cols = group * HEAD
    return call(
        functools.partial(attn_forward_kernel, rows, n // rows, group, kv_heads, len(w_o)),
        (kv_heads,),
        [by_head(n, q_cols + 2 * HEAD), whole(seg_col.shape), whole(seg_row.shape)]
        + [by_head(w.shape[0], q_cols, first) for w in w_o],
        [
            by_head(n, q_cols),
            pl.BlockSpec((1, 8, n), lambda h, t: (h, 0, 0)),
            whole((n // 2, width)),
            whole((n // 2, width)),
        ],
        [
            shape_of((n, kv_heads * q_cols)),
            shape_of((kv_heads, 8, n), F32),
            shape_of((n // 2, width)),
            shape_of((n // 2, width)),
        ],
        kv_heads * group * n * n * HEAD * 4,
        [pltpu.VMEM((width, q_cols), BF16), pltpu.VMEM((n, width), F32)],
    )(t, packed, seg_col, seg_row, *w_o)


def head_back(e, u, cos, sin, gain):
    e = e * cos - pltpu.roll(e, HEAD // 2, 1) * sin
    r = lax.rsqrt(jnp.mean(u * u, axis=1, keepdims=True) + EPS)
    ur = u * r
    dgain = jnp.sum(e * ur, axis=0, keepdims=True)
    ec = e * gain
    du = r * (ec - ur * jnp.mean(ur * ec, axis=1, keepdims=True))
    return du, dgain


def attn_backward_kernel(rows, blocks, group, kv_heads, nw, t, *refs):
    packed, seg_col, seg_row, inv, raw, cos, sin, gains = refs[:8]
    refs = refs[8:]
    branch, refs = refs[:blocks], refs[blocks:]
    xs, refs = refs[:blocks], refs[blocks:]
    w_os, refs = refs[:nw], refs[nw:]
    w_qkvs, refs = refs[:nw], refs[nw:]
    dpacked, dgain, keep, send, dgain_x, dk, dv, dmix, w_o, w_qkv, acc = refs
    causal = lax.broadcasted_iota(jnp.int32, (rows, rows), 0) <= lax.broadcasted_iota(
        jnp.int32, (rows, rows), 1
    )
    kc = group * HEAD
    gq = gains[2:3, :HEAD]
    gk = gains[3:4, :HEAD]
    join(w_os, w_o)
    join(w_qkvs, w_qkv)
    for k in range(blocks):
        dmix[k * rows : (k + 1) * rows, :] = mm(branch[k][...], w_o[...]).astype(BF16)
    dk[...] = jnp.zeros_like(dk)
    dv[...] = jnp.zeros_like(dv)
    dgain[...] = jnp.zeros_like(dgain)
    for i in range(blocks):
        lo = i * rows
        at = pl.multiple_of(lax.bitwise_xor(i, t[0]) * rows, rows)
        sq = seg_row[:, lo : lo + rows]
        for j in range(group):
            q = packed[lo : lo + rows, j * HEAD : (j + 1) * HEAD]
            do = dmix[pl.ds(at, rows), j * HEAD : (j + 1) * HEAD]
            rec = inv[0, j : j + 1, lo : lo + rows]
            probs = []
            dprobs = []
            delta = jnp.zeros((1, rows), F32)
            for b in range(i + 1):
                here = slice(b * rows, (b + 1) * rows)
                k = packed[here, kc : kc + HEAD]
                v = packed[here, kc + HEAD : kc + 2 * HEAD]
                same = seg_col[here, :] == sq
                p = weights_of(q, k, same, causal if b == i else None) * rec
                dp = mm(v, do, 1, 1)
                delta = delta + jnp.sum(p * dp, axis=0, keepdims=True)
                dv[here, :] += mm(p.astype(BF16), do)
                probs.append(p)
                dprobs.append(dp)
            dq = jnp.zeros((rows, HEAD), F32)
            for b in range(i + 1):
                here = slice(b * rows, (b + 1) * rows)
                k = packed[here, kc : kc + HEAD]
                ds = (probs[b] * (dprobs[b] - delta)).astype(BF16)
                dk[here, :] += mm(ds, q)
                dq = dq + mm(ds, k, 0, 0)
            du, dg = head_back(
                dq * SCALE,
                raw[lo : lo + rows, j * HEAD : (j + 1) * HEAD],
                cos[lo : lo + rows, :],
                sin[lo : lo + rows, :],
                gq,
            )
            dgain[0, 0:1, :] += dg
            dpacked[pl.ds(at, rows), j * HEAD : (j + 1) * HEAD] = du.astype(BF16)
    for i in range(blocks):
        here = slice(i * rows, (i + 1) * rows)
        at = pl.multiple_of(lax.bitwise_xor(i, t[0]) * rows, rows)
        du, dg = head_back(
            dk[here, :] * SCALE, raw[here, kc : kc + HEAD], cos[here, :], sin[here, :], gk
        )
        dgain[0, 1:2, :] += dg
        dpacked[pl.ds(at, rows), kc : kc + HEAD] = du.astype(BF16)
        dpacked[pl.ds(at, rows), kc + HEAD : kc + 2 * HEAD] = dv[here, :].astype(BF16)
    accumulate(mm(dpacked[...], w_qkv[...], 1, 1), acc)

    @pl.when(pl.program_id(0) == kv_heads - 1)
    def _():
        total = jnp.zeros((1, acc.shape[1]), F32)
        for k in range(blocks):
            u = xs[k][...].astype(F32)
            ur = u * lax.rsqrt(jnp.mean(u * u, axis=1, keepdims=True) + EPS)
            total = total + jnp.sum(acc[k * rows : (k + 1) * rows, :] * ur, axis=0, keepdims=True)
        dgain_x[...] = jnp.broadcast_to(total, dgain_x.shape)
        split_rows(rows, acc, keep, send)


def attn_backward(
    t, packed, seg_col, seg_row, inv, raw, cos, sin, gains, branch, xs, w_o, first, w_qkv, width, kv_heads, group
):
    n = packed.shape[0]
    rows = xs[0].shape[0]
    q_cols = group * HEAD
    cols = q_cols + 2 * HEAD
    return call(
        functools.partial(attn_backward_kernel, rows, n // rows, group, kv_heads, len(w_o)),
        (kv_heads,),
        [
            by_head(n, cols),
            whole(seg_col.shape),
            whole(seg_row.shape),
            pl.BlockSpec((1, 8, n), lambda h, t: (h, 0, 0)),
            by_head(n, q_cols + HEAD),
            whole(cos.shape),
            whole(sin.shape),
            whole(gains.shape),
        ]
        + [whole(b.shape) for b in branch]
        + [part_at((rows, width), 0) for _ in xs]
        + [by_head(w.shape[0], q_cols, first) for w in w_o]
        + [by_head(w.shape[0], cols) for w in w_qkv],
        [
            by_head(n, cols),
            pl.BlockSpec((1, 8, HEAD), lambda h, t: (h, 0, 0)),
            whole((n // 2, width)),
            whole((n // 2, width)),
            whole((8, width)),
        ],
        [
            shape_of(packed.shape),
            shape_of((kv_heads, 8, HEAD), F32),
            shape_of((n // 2, width)),
            shape_of((n // 2, width)),
            shape_of((8, width), F32),
        ],
        kv_heads * group * n * n * HEAD * 10,
        [
            pltpu.VMEM((n, HEAD), F32),
            pltpu.VMEM((n, HEAD), F32),
            pltpu.VMEM((n, q_cols), BF16),
            pltpu.VMEM((width, q_cols), BF16),
            pltpu.VMEM((width, cols), BF16),
            pltpu.VMEM((n, width), F32),
        ],
    )(t, packed, seg_col, seg_row, inv, raw, cos, sin, gains, *branch, *xs, *w_o, *w_qkv)


def join_in_order(t, reorder, block, out):
    if not reorder:
        out[...] = block[...]
        return
    for p in range(out.shape[0] // HEAD):
        out[p * HEAD : (p + 1) * HEAD, :] = block[pl.ds(model_block(t, p), HEAD), :]


def mlp_kernel(ff, nx, reorder, t, *refs):
    xs, refs = refs[:nx], refs[nx:]
    gs, refs = refs[:nx], refs[nx:]
    w_gu, w_d, *refs = refs
    act, dgu, x_out, g_out, dx_keep, dx_send, out_keep, out_send, w, wd, x, g = refs
    i = pl.program_id(0)

    @pl.when(i == 0)
    def _():
        join_in_order(t, reorder, w_gu, w)
        join_in_order(t, reorder, w_d, wd)

    for k in range(nx):

        @pl.when(i == k)
        def _(k=k):
            x[...] = xs[k][...]
            g[...] = gs[k][...]
            store_columns(t, reorder, xs[k][...], x_out)
            g_out[...] = gs[k][...]

    y = mm(x[...], w[...])
    gate = y[:, :ff]
    up = y[:, ff:]
    sig = 1.0 / (1.0 + jnp.exp(-gate))
    silu = gate * sig
    a = (silu * up).astype(BF16)
    act[...] = a
    da = mm(g[...], wd[...])
    dgu[:, :ff] = (da * up * sig * (1.0 + gate * (1.0 - sig))).astype(BF16)
    dgu[:, ff:] = (da * silu).astype(BF16)
    dx = mm(dgu[...], w[...], 1, 1).astype(BF16)
    out = mm(a, wd[...], 1, 1).astype(BF16)

    @pl.when(lax.rem(i, 2) == 0)
    def _():
        dx_keep[...] = dx
        out_keep[...] = out

    @pl.when(lax.rem(i, 2) == 1)
    def _():
        dx_send[...] = dx
        out_send[...] = out


def mlp_call(t, reorder, xs, gs, g_index, w_gu, w_d, d_index, ff, width):
    rows = xs[0].shape[0]
    n = rows * len(xs)
    halves = pl.BlockSpec((rows, width), lambda i, t: (lax.div(i, 2), 0))
    return call(
        functools.partial(mlp_kernel, ff, len(xs), reorder),
        (len(xs),),
        [whole(x.shape) for x in xs]
        + [part_at((rows, width), g_index) for _ in gs]
        + [part_at((width, 2 * ff), 0), part_at((width, ff), d_index)],
        [rows_at(rows, ff), rows_at(rows, 2 * ff)] + [rows_at(rows, width)] * 2 + [halves] * 4,
        [shape_of((n, ff)), shape_of((n, 2 * ff))]
        + [shape_of((n, width))] * 2
        + [shape_of((n // 2, width))] * 4,
        2 * n * width * ff * 6,
        [
            pltpu.VMEM((width, 2 * ff), BF16),
            pltpu.VMEM((width, ff), BF16),
            pltpu.VMEM((rows, width), BF16),
            pltpu.VMEM((rows, width), BF16),
        ],
    )(t, *xs, *gs, w_gu, w_d)


def sum_of(parts):
    total = parts[0][...].astype(F32)
    for p in parts[1:]:
        total = total + p[...].astype(F32)
    return total


def hidden_kernel(n_parts, t, *refs):
    parts = refs[:n_parts]
    x, gains, hidden, normed = refs[n_parts:]
    h = x[...].astype(F32) + sum_of(parts)
    hidden[...] = h
    r = lax.rsqrt(jnp.mean(h * h, axis=1, keepdims=True) + EPS)
    normed[...] = (h * r * gains[1:2, :]).astype(BF16)


def row_tile(rows, width, index=0):
    return pl.BlockSpec((rows // ROW_STEPS, width), lambda i, t: (i, index))


def hidden_call(t, parts, x, gains, rows, width):
    spec = row_tile(rows, width)
    return call(
        functools.partial(hidden_kernel, len(parts)),
        (ROW_STEPS,),
        [spec for _ in parts] + [spec, whole(gains.shape)],
        [spec, spec],
        [shape_of((rows, width), F32), shape_of((rows, width))],
        rows * width * 8,
    )(t, *parts, x, gains)


def norm_back(e, u, gain):
    r = lax.rsqrt(jnp.mean(u * u, axis=1, keepdims=True) + EPS)
    ur = u * r
    ec = e * gain
    return r * (ec - ur * jnp.mean(ur * ec, axis=1, keepdims=True)), jnp.sum(e * ur, axis=0, keepdims=True)


def d_hidden_kernel(n_parts, t, *refs):
    parts = refs[:n_parts]
    hidden, g, gains, d_hidden, branch, d_gain = refs[n_parts:]
    du, dg = norm_back(sum_of(parts), hidden[...], gains[1:2, :])
    d = g[...].astype(F32) + du
    d_hidden[...] = d
    branch[...] = d.astype(BF16)
    accumulate(jnp.broadcast_to(dg, d_gain.shape), d_gain)


def d_hidden_call(t, parts, hidden, g, g_index, gains, rows, width):
    spec = row_tile(rows, width)
    return call(
        functools.partial(d_hidden_kernel, len(parts)),
        (ROW_STEPS,),
        [spec for _ in parts] + [spec, row_tile(rows, width, g_index), whole(gains.shape)],
        [spec, spec, whole((8, width))],
        [shape_of((rows, width), F32), shape_of((rows, width)), shape_of((8, width), F32)],
        rows * width * 12,
    )(t, *parts, hidden, g, gains)


def store_columns(t, reorder, value, out):
    if not reorder:
        out[...] = value
        return
    for p in range(value.shape[1] // HEAD):
        out[:, pl.ds(model_block(t, p), HEAD)] = value[:, p * HEAD : (p + 1) * HEAD]


def activations_kernel(n_parts, reorder, t, *refs):
    parts = refs[:n_parts]
    hidden, out = refs[n_parts:]
    store_columns(t, reorder, (hidden[...] + sum_of(parts)).astype(BF16), out)


def activations_call(t, reorder, parts, hidden, rows, width):
    spec = row_tile(rows, width)
    return call(
        functools.partial(activations_kernel, len(parts), reorder),
        (ROW_STEPS,),
        [spec for _ in parts] + [spec],
        spec,
        shape_of((rows, width)),
        rows * width * 2,
    )(t, *parts, hidden)


def d_tokens_kernel(n_parts, reorder, t, *refs):
    parts = refs[:n_parts]
    x, d_hidden, gains, out = refs[n_parts:]
    du, _ = norm_back(sum_of(parts), x[...].astype(F32), gains[0:1, :])
    store_columns(t, reorder, d_hidden[...] + du, out)


def d_tokens_call(t, reorder, parts, x, d_hidden, gains, rows, width):
    spec = row_tile(rows, width)
    return call(
        functools.partial(d_tokens_kernel, len(parts), reorder),
        (ROW_STEPS,),
        [spec for _ in parts] + [spec, spec, whole(gains.shape)],
        spec,
        shape_of((rows, width), F32),
        rows * width * 12,
    )(t, *parts, x, d_hidden, gains)


def outer_half(left, right, half):
    m = left.shape[1] // 2
    return mm(left[:, half * m : (half + 1) * m], right, 0, 0).astype(BF16)


def shard_of(parts):
    total = parts[0].astype(F32)
    for p in parts[1:]:
        total = total + p.astype(F32)
    return total


def unpack_heads(kv_heads, group, w):
    q, k, v = [], [], []
    for h in range(kv_heads):
        base = h * (group + 2) * HEAD
        mid = base + group * HEAD
        q.append(w[:, base:mid])
        k.append(w[:, mid : mid + HEAD])
        v.append(w[:, mid + HEAD : mid + 2 * HEAD])
    join = lambda parts: jnp.concatenate(parts, axis=1)
    return join(q), join(k), join(v)


def gain_rows_kernel(t, d_attn, d_mlp, d_heads, out):
    heads = jnp.sum(d_heads[...], axis=0)
    at = lax.broadcasted_iota(jnp.int32, (GAIN_ROWS, 4 * HEAD), 0)
    for p in range(d_attn.shape[1] // HEAD):
        here = slice(p * HEAD, (p + 1) * HEAD)
        row = jnp.concatenate([d_attn[0:1, here], d_mlp[0:1, here], heads[0:1], heads[1:2]], axis=1)
        rows = slice(p * GAIN_ROWS, (p + 1) * GAIN_ROWS)
        out[rows, : 4 * HEAD] = jnp.where(at == 0, row, 0.0).astype(BF16)
        out[rows, 4 * HEAD :] = jnp.zeros((GAIN_ROWS, out.shape[1] - 4 * HEAD), BF16)


def gain_rows(t, d_attn, d_mlp, d_heads, cols):
    args = (d_attn, d_mlp, d_heads)
    rows = d_attn.shape[1] // HEAD * GAIN_ROWS
    return call(
        gain_rows_kernel,
        (1,),
        [whole(a.shape) for a in args],
        whole((rows, cols)),
        shape_of((rows, cols)),
        rows * HEAD,
    )(t, *args)


def pair_sum_kernel(t, keep, rows, got, *outs):
    n = keep.shape[0] // len(outs)
    for z, out in enumerate(outs):
        here = slice(z * n, (z + 1) * n)
        low = slice(z * GAIN_ROWS, (z + 1) * GAIN_ROWS)
        there = slice(keep.shape[0] + z * GAIN_ROWS, keep.shape[0] + (z + 1) * GAIN_ROWS)
        out[:n, :] = (keep[here, :].astype(F32) + got[here, :].astype(F32)).astype(out.dtype)
        out[n:, :] = (rows[low, :].astype(F32) + got[there, :].astype(F32)).astype(out.dtype)


def pair_sum(t, keep, rows, got, parts):
    m, cols = keep.shape
    n = m // parts + GAIN_ROWS
    return call(
        pair_sum_kernel,
        (1,),
        [whole(keep.shape), whole(rows.shape), whole(got.shape)],
        [whole((n, cols)) for _ in range(parts)],
        [shape_of((n, cols), F32 if z == 0 else BF16) for z in range(parts)],
        m * cols,
    )(t, keep, rows, got)


def xor_pairs(size, bits):
    return [(i, i ^ bits) for i in range(size)]


class Links:
    def __init__(self, dp, tensor):
        self.dp, self.tensor = dp, tensor
        self.direct = (dp, tensor) == (8, 4)
        self.d = lax.axis_index("dp")
        self.t = lax.axis_index("tensor")

    def over_dp(self, x, bits):
        return lax.ppermute(x, "dp", xor_pairs(self.dp, bits))

    def over_tensor(self, x, bits):
        return lax.ppermute(x, "tensor", xor_pairs(self.tensor, bits))

    def offsets(self):
        if self.direct:
            return jnp.stack([self.t, self.d])
        return jnp.zeros((2,), jnp.int32)

    def gather_dp(self, x):
        if not self.direct:
            return [lax.all_gather(x, "dp", axis=0, tiled=True)]
        own = self.gather_z(x)
        return own + [self.over_dp(b, 1) for b in own]

    def gather_z(self, x):
        return [x] + [self.over_dp(x, 2 * z) for z in (1, 2, 3)]

    def send_half(self, left, right):
        send = outer_half(left, right, 1)
        if self.direct:
            send = self.over_dp(send, 1)
        return send, outer_half(left, right, 0)

    def send_quarters(self, got, keep):
        if not self.direct:
            both = jnp.concatenate([keep, got], axis=0)
            return [lax.psum_scatter(both, "dp", scatter_dimension=0, tiled=True)]
        n = keep.shape[0] // 4
        part = lambda z: keep[z * n : (z + 1) * n].astype(F32) + got[z * n : (z + 1) * n].astype(F32)
        return [part(0)] + [self.over_dp(part(z).astype(BF16), 2 * z) for z in (1, 2, 3)]

    def gather_tensor(self, x, *after):
        if not self.direct:
            full = lax.all_gather(x, "tensor", axis=0, tiled=True)
            return jnp.split(full, self.tensor, axis=0)
        far = self.over_tensor(x, 2)
        return [x, self.over_tensor(x, 1), far, self.over_tensor(tie(far, *after) if after else far, 1)]

    def scatter_tensor(self, keep, send):
        rows = 2 * keep.shape[0] // self.tensor
        if not self.direct:
            blocks = []
            for k in range(self.tensor // 2):
                blocks += [keep[k * rows : (k + 1) * rows], send[k * rows : (k + 1) * rows]]
            full = jnp.concatenate(blocks, axis=0)
            return [lax.psum_scatter(full, "tensor", scatter_dimension=0, tiled=True)]
        got = self.over_tensor(send, 1)
        far = keep[rows:].astype(F32) + got[rows:].astype(F32)
        return [keep, got, self.over_tensor(far.astype(BF16), 2)]


def rope_tables(offsets):
    frequency = ROPE_BASE ** (-(2.0 * jnp.arange(HEAD // 2, dtype=F32)) / HEAD)
    angles = offsets.astype(F32)[:, None] * frequency[None, :]
    cos, sin = jnp.cos(angles), jnp.sin(angles)
    return jnp.concatenate([cos, cos], axis=1), jnp.concatenate([-sin, sin], axis=1)


def pack_heads(wq, wk, wv, group):
    parts = []
    for h in range(wk.shape[1] // HEAD):
        parts += [
            wq[:, h * group * HEAD : (h + 1) * group * HEAD],
            wk[:, h * HEAD : (h + 1) * HEAD],
            wv[:, h * HEAD : (h + 1) * HEAD],
        ]
    return jnp.concatenate(parts, axis=1)


def body(
    dp,
    tensor,
    tokens,
    segment_ids,
    positions,
    w_query,
    key_projection,
    value_projection,
    w_out,
    w_gate,
    w_up,
    w_down,
    gain_attn,
    gain_mlp,
    gain_query,
    gain_key,
    cotangent,
):
    links = Links(dp, tensor)
    direct = links.direct
    rows, width = tokens.shape
    kv_heads = key_projection.shape[1] // HEAD
    group = w_query.shape[1] // key_projection.shape[1]
    q_cols = group * HEAD
    ff = w_gate.shape[1]
    head_part = HEAD // dp
    t = links.offsets()

    if direct:
        w_attn = pack_attn(
            t,
            w_query,
            key_projection,
            value_projection,
            w_out,
            (gain_attn, gain_mlp, gain_query, gain_key),
            kv_heads,
            group,
        )
        both = pack_rows(t, tie(tokens, w_attn), cotangent)
        w_mlp = pack_mlp(t, tie(w_gate, both), w_up, w_down)
        attn_near = links.gather_z(w_attn)
        attn_far = links.over_dp(w_attn, 1)
        beside = links.over_tensor(both, 1)
        far = links.over_tensor(both, 2)
        across = tie(far, attn_far, attn_near[1], attn_near[2])
        rows_all = [both, beside, far, links.over_tensor(across, 1)]
        w_mlp = tie(w_mlp, (far, attn_far, attn_near[1], attn_near[2]))
        w_attn = attn_near + [attn_far] + [links.over_dp(b, 1) for b in attn_near[1:]]
        w_qkv, w_o, o_index = w_attn, w_attn, kv_heads * (group + 2) * HEAD // q_cols
        w_gu = w_d = lax.all_gather(w_mlp, "dp", axis=0, tiled=True)
        d_index = 2
        gains = jnp.zeros((8, width), F32)
    else:
        w_qkv = links.gather_dp(pack_heads(w_query, key_projection, value_projection, group))
        w_o = links.gather_dp(w_out.T)
        w_gu = links.gather_dp(jnp.concatenate([w_gate, w_up], axis=1))[0]
        w_d = links.gather_dp(w_down.T)[0]
        d_index, o_index = 0, 0
        row = lambda g: jnp.pad(g, (0, width - g.shape[0]))[None, :].astype(F32)
        whole_gain = lambda g: row(lax.all_gather(g, "dp", axis=0, tiled=True))
        gains = jnp.concatenate(
            [whole_gain(g) for g in (gain_attn, gain_mlp, gain_query, gain_key)]
            + [jnp.zeros((4, width), F32)],
            axis=0,
        )
        rows_all = links.gather_tensor(jnp.concatenate([tokens, cotangent], axis=1))
    own = rows_all[0] if direct else jnp.concatenate([tokens, cotangent], axis=1)

    cos, sin = rope_tables(positions[0])
    seg_row = segment_ids
    seg_col = segment_ids.reshape(-1, 1)

    normed, packed, raw, gains = qkv_call(
        t, rows_all, w_qkv, gains, direct, cos, sin, width, kv_heads, group
    )
    mixed, inv, keep, send = attn_forward(
        t, packed, seg_col, seg_row, w_o, o_index, rows, width, kv_heads, group
    )
    parts = links.scatter_tensor(keep, send)
    hidden, normed_mlp = hidden_call(t, parts, own, gains, rows, width)
    normed_mlp = links.gather_tensor(normed_mlp)
    act, d_gu, normed_mlp, cot, dx_keep, dx_send, out_keep, out_send = mlp_call(
        t, direct, normed_mlp, rows_all, 1, w_gu, w_d, d_index, ff, width
    )
    parts = links.scatter_tensor(dx_keep, dx_send)
    gu_sum = mm(normed_mlp, tie(d_gu, parts[:2]), 0, 0).astype(BF16)
    gu = lax.psum_scatter(gu_sum, "dp", scatter_dimension=0, tiled=True)
    d_hidden, branch, d_gain_mlp = d_hidden_call(
        t, tie(parts, gu_sum), hidden, own, 1, gains, rows, width
    )
    down = links.send_half(cot, tie(act, branch))
    branch = links.gather_tensor(branch, down[1])
    out_parts = links.scatter_tensor(out_keep, tie(out_send, branch))
    out = links.send_half(jnp.concatenate(branch, axis=0), mixed)
    d_packed, d_gain_heads, keep, send, d_gain_attn = tie(
        attn_backward(
            t, packed, seg_col, seg_row, inv, raw, cos, sin, gains, branch, rows_all, w_o, o_index, w_qkv,
            width, kv_heads, group,
        ),
        out[0],
        down[0],
        out_parts,
    )
    if direct:
        tails = gain_rows(t, d_gain_attn, d_gain_mlp, d_gain_heads, d_packed.shape[1])
        half = tails.shape[0] // 2
        send_qkv = jnp.concatenate([outer_half(normed, d_packed, 1), tails[half:]], axis=0)
        got = links.over_dp(send_qkv, 1)
        parts = links.scatter_tensor(keep, send)
        out, down = tie((out, down), parts[:2])
        out = links.send_quarters(*out)
        down = links.send_quarters(*down)
        qkv = pair_sum(t, outer_half(normed, d_packed, 0), tails[:half], tie(got, out[1:], down[1:], gu), 4)
        qkv = [qkv[0]] + [links.over_dp(qkv[z], 2 * z) for z in (1, 2, 3)]
    else:
        qkv = links.send_quarters(*links.send_half(normed, d_packed))
        out = links.send_quarters(*out)
        down = links.send_quarters(*down)
        parts = links.scatter_tensor(keep, send)
    d_tokens = d_tokens_call(t, direct, parts, own, d_hidden, gains, rows, width)
    activations = activations_call(t, direct, out_parts, hidden, rows, width)
    grad_down = shard_of(down).T
    grad_gate, grad_up = gu[:, :ff].astype(F32), gu[:, ff:].astype(F32)
    grad_out = shard_of(out).T
    n = width // dp
    qkv = shard_of(qkv)
    grad_query, grad_key, grad_value = unpack_heads(kv_heads, group, qkv[:n])
    if direct:
        sums = qkv[n : n + 1, : 4 * HEAD]
        sums = sums + links.over_tensor(sums, 1)
        sums = (sums + links.over_tensor(sums, 2)).reshape(4, HEAD)
        sum_attn, sum_mlp, sum_query, sum_key = sums[0], sums[1], sums[2], sums[3]
    else:
        heads = jnp.sum(d_gain_heads, axis=0)
        sum_attn, sum_mlp, sum_query, sum_key = lax.psum(
            (d_gain_attn[0], d_gain_mlp[0], heads[0], heads[1]), ("dp", "tensor")
        )
        sum_attn = lax.dynamic_slice_in_dim(sum_attn, links.d * n, n, 0)
        sum_mlp = lax.dynamic_slice_in_dim(sum_mlp, links.d * n, n, 0)
    shard = lambda v: lax.dynamic_slice_in_dim(v, links.d * head_part, head_part, 0)
    return (
        activations,
        d_tokens,
        grad_query,
        grad_key,
        grad_value,
        grad_out,
        grad_gate,
        grad_up,
        grad_down,
        sum_attn,
        sum_mlp,
        shard(sum_query),
        shard(sum_key),
    )


def solution(mesh):
    tokens = P(("dp", "tensor"), None)
    by_rows = P("dp", "tensor")
    by_columns = P("tensor", "dp")
    sequence = P("dp", None)
    gain = P("dp")
    return jax.shard_map(
        functools.partial(body, mesh.shape["dp"], mesh.shape["tensor"]),
        mesh=mesh,
        in_specs=(
            tokens,
            sequence,
            sequence,
            by_rows,
            by_rows,
            by_rows,
            by_columns,
            by_rows,
            by_rows,
            by_columns,
            gain,
            gain,
            gain,
            gain,
            tokens,
        ),
        out_specs=(
            tokens,
            tokens,
            by_rows,
            by_rows,
            by_rows,
            by_columns,
            by_rows,
            by_rows,
            by_columns,
            gain,
            gain,
            gain,
            gain,
        ),
        check_vma=False,
    )
```

time: 433 us -> 359 us (0.83)
  the two profiles are of different devices: /device:TPU:0 before, /device:TPU:12 now
where the time goes in v2:
time: 359 us; the launch traced here: 355 us
  waiting for transfers between devices  154 us (43%)
  Pallas kernels  98.9 us (28%)
  starting transfers between devices  34.1 us (9%)
  matrix products  21.8 us (6%)
  other arithmetic  17.3 us (5%)
  between operations  14.7 us (4%)
  local copies, waits for them, and re-layouts  13.7 us (4%)
    ppermute x19, waiting for transfers between devices, over_dp(): return lax.ppermute(x, 'dp', xor_pairs(self.dp, bits))  96 us
    ppermute x19, waiting for transfers between devices, over_tensor(): return lax.ppermute(x, 'tensor', xor_pairs(self.tensor, bits))  58.5 us
    pallas_call x1, Pallas kernels, attn_backward(): call(functools.partial(attn_backward_kernel, rows, n // rows, group, kv_h...  25.8 us
    dot_general x7, matrix products, mm(): lax.dot_general(a, b, (((ca,), (cb,)), ((), ())), preferred_element_type=...  21.8 us
    ppermute x19, starting transfers between devices, over_dp(): return lax.ppermute(x, 'dp', xor_pairs(self.dp, bits))  21.1 us
    pallas_call x1, Pallas kernels, mlp_call(): call(functools.partial(mlp_kernel, ff, len(xs), reorder), (len(xs),), [wh...  20.5 us
    ppermute x19, starting transfers between devices, over_tensor(): return lax.ppermute(x, 'tensor', xor_pairs(self.tensor, bits))  12.9 us
    pallas_call x1, Pallas kernels, attn_forward(): call(functools.partial(attn_forward_kernel, rows, n // rows, group, kv_he...  12.7 us
  transfers between devices with their start and end apart: 40, of which 23 were waited for; matrix products, arithmetic and copies ran while one was open for 10% of the time, Pallas kernels for 20%

profile of v2, /device:TPU:12, one launch (start us, length us, event | category | flops | bytes accessed | tf_op | source)
XLA Modules:
  0.0 355.0 jit_solution(14907712162463227597)
XLA Ops:
  10.4 3.3 shard_map.247.refs_0_.refs_3_.refs_4_.refs_12_
  21.4 14.9 %collective-permute-done.4.refs_6_.refs_2_.refs_18_.refs_26_ = bf16[144,1536]{1,0:T(8,128)(2,1)S(1)} collective-permute-done((bf16[144,1536]{1,0:T(8,128)(2,1)S(1)}, bf16[144,1536]{1,0:T(8,128)(2,1)S(1)}, u32[]{:S(2)}, u32[]{:S(2)}) %collective-permute-start.4) | collective-permute-done | bytes 442400 | tf_op jit(solution)/shard_map/ppermute | solution.py:725
  43.1 37.1 %collective-permute-done.6.refs_7_.refs_3_.refs_19_.refs_27_ = bf16[144,1536]{1,0:T(8,128)(2,1)} collective-permute-done((bf16[144,1536]{1,0:T(8,128)(2,1)S(1)}, bf16[144,1536]{1,0:T(8,128)(2,1)}, u32[]{:S(2)}, u32[]{:S(2)}) %collective-permute-start.6) | collective-permute-done | bytes 442400 | tf_op jit(solution)/shard_map/ppermute | solution.py:725
  84.9 6.6 %collective-permute-done.9.refs_11_.refs_7_.refs_23_.refs_31_ = bf16[144,1536]{1,0:T(8,128)(2,1)S(1)} collective-permute-done((bf16[144,1536]{1,0:T(8,128)(2,1)}, bf16[144,1536]{1,0:T(8,128)(2,1)S(1)}, u32[]{:S(2)}, u32[]{:S(2)}) %collective-permute-start.9) | collective-permute-done | bytes 442400 | tf_op jit(solution)/shard_map/ppermute | solution.py:725
  92.6 9.6 %shard_map.248 = (bf16[1024,1024]{1,0:T(8,128)(2,1)}, bf16[1024,1024]{1,0:T(8,128)(2,1)}, f32[1024,768]{1,0:T(8,128)}, f32[8,1024]{1,0:T(8,128)}) custom-call(s32[2]{0:T(128)} %pad_add_fusion.t, bf16[256,2048]{1,0:T(8,128)(2,1)} %shard_map.247.refs_0_.refs_3_.refs_4_.refs_12_, bf16[256,2048]{1,0:T(8,128)(2,1)} %copy-done.2, bf16[256,2048]{1,0:T(8,128)(2,1)} %copy-done.1, ...), custom_call_target="tpu_custom_call" | custom-call | flops 1 | bytes 1 | tf_op jit(solution)/shard_map/pallas_call | solution.py:210
  102.2 12.7 %shard_map.249 = (bf16[1024,512]{1,0:T(8,128)(2,1)}, f32[2,8,1024]{2,1,0:T(8,128)}, bf16[512,1024]{1,0:T(8,128)(2,1)}, bf16[512,1024]{1,0:T(8,128)(2,1)}) custom-call(s32[2]{0:T(128)} %pad_add_fusion.t, bf16[1024,1024]{1,0:T(8,128)(2,1)} %get-tuple-element.66.packed.refs_0_, s32[1024,1]{1,0:T(8,128)} %copy.30.seg_col.refs_1_, s32[1,1024]{1,0:T(1,128)} %refs_2_.1, ...), custom_call_target="tpu_custom_call" | custom-call | flops 1 | bytes 1 | tf_op jit(solution)/shard_map/pallas_call | solution.py:296
  120.9 12.5 %collective-permute-done.11.refs_2_ = bf16[256,1024]{1,0:T(8,128)(2,1)S(1)} collective-permute-done((bf16[256,1024]{1,0:T(8,128)(2,1)S(1)}, bf16[256,1024]{1,0:T(8,128)(2,1)S(1)}, u32[]{:S(2)}, u32[]{:S(2)}) %collective-permute-start.11) | collective-permute-done | bytes 524320 | tf_op jit(solution)/shard_map/ppermute | solution.py:728
  134.3 3.6 %shard_map.250 = (f32[256,1024]{1,0:T(8,128)}, bf16[256,1024]{1,0:T(8,128)(2,1)}) custom-call(s32[2]{0:T(128)} %pad_add_fusion.t, bf16[512,1024]{1,0:T(8,128)(2,1)} %get-tuple-element.67.refs_0_, bf16[512,1024]{1,0:T(8,128)(2,1)} %copy-done.14, bf16[256,1024]{1,0:T(8,128)(2,1)} %copy-done.27, bf16[256,2048]{1,0:T(8,128)(2,1)} %shard_map.247.refs_0_.refs_3_.refs_4_.refs_12_, ...), custom_call_target="tpu_custom_call" | custom-call | flops 1 | bytes 1 | tf_op jit(solution)/shard_map/pallas_call | solution.py:558
  139.4 11.9 %collective-permute-done.13.refs_2_ = bf16[256,1024]{1,0:T(8,128)(2,1)S(1)} collective-permute-done((bf16[256,1024]{1,0:T(8,128)(2,1)}, bf16[256,1024]{1,0:T(8,128)(2,1)S(1)}, u32[]{:S(2)}, u32[]{:S(2)}) %collective-permute-start.13) | collective-permute-done | bytes 524320 | tf_op jit(solution)/shard_map/ppermute | solution.py:728
  154.0 20.5 %shard_map.252 = (bf16[1024,768]{1,0:T(8,128)(2,1)}, bf16[1024,1536]{1,0:T(8,128)(2,1)}, bf16[1024,1024]{1,0:T(8,128)(2,1)}, bf16[1024,1024]{1,0:T(8,128)(2,1)},...) custom-call(s32[2]{0:T(128)} %pad_add_fusion.t, ...), custom_call_target="tpu_custom_call" | custom-call | flops 1 | bytes 1 | tf_op jit(solution)/shard_map/pallas_call | solution.py:516
  177.5 8.0 %convolution_convert_fusion = bf16[1024,1536]{1,0:T(8,128)(2,1)} fusion(bf16[1024,1024]{1,0:T(8,128)(2,1)} %get-tuple-element.77, bf16[1024,1536]{1,0:T(8,128)(2,1)} %get-tuple-element.79), kind=kOutput, calls=%fused_computation | convolution fusion | flops 3222798336 | bytes 8388608 | tf_op jit(solution)/shard_map/dot_general | solution.py:24
  188.4 12.5 %collective-permute-done.16.refs_2_ = bf16[256,1024]{1,0:T(8,128)(2,1)S(1)} collective-permute-done((bf16[256,1024]{1,0:T(8,128)(2,1)S(1)}, bf16[256,1024]{1,0:T(8,128)(2,1)S(1)}, u32[]{:S(2)}, u32[]{:S(2)}) %collective-permute-start.16) | collective-permute-done | bytes 524320 | tf_op jit(solution)/shard_map/ppermute | solution.py:728
  201.7 4.5 %shard_map.253 = (f32[256,1024]{1,0:T(8,128)}, bf16[256,1024]{1,0:T(8,128)(2,1)}, f32[8,1024]{1,0:T(8,128)}) custom-call(s32[2]{0:T(128)} %pad_add_fusion.t, bf16[512,1024]{1,0:T(8,128)(2,1)} %get-tuple-element.80.refs_0_, bf16[512,1024]{1,0:T(8,128)(2,1)} %copy-done.11, bf16[256,1024]{1,0:T(8,128)(2,1)} %copy-done.25, ...), custom_call_target="tpu_custom_call" | custom-call | flops 1 | bytes 1 | tf_op jit(solution)/shard_map/pallas_call | solution.py:587
  210.4 9.2 %collective-permute-done.18.refs_10_ = bf16[256,1024]{1,0:T(8,128)(2,1)S(1)} collective-permute-done((bf16[256,1024]{1,0:T(8,128)(2,1)}, bf16[256,1024]{1,0:T(8,128)(2,1)S(1)}, u32[]{:S(2)}, u32[]{:S(2)}) %collective-permute-start.18) | collective-permute-done | bytes 524320 | tf_op jit(solution)/shard_map/ppermute | solution.py:728
  230.1 25.8 %shard_map.255 = (bf16[1024,1024]{1,0:T(8,128)(2,1)}, f32[2,8,128]{2,1,0:T(8,128)}, bf16[512,1024]{1,0:T(8,128)(2,1)}, bf16[512,1024]{1,0:T(8,128)(2,1)}, f32[8,1024]{1,0:T(8,128)}) custom-call(s32[2]{0:T(128)} %pad_add_fusion.t, bf16[1024,1024]{1,0:T(8,128)(2,1)} %get-tuple-element.66.packed.refs_0_, s32[1024,1]{1,0:T(8,128)} %copy.30.seg_col.refs_1_, ...), custom_call_target="tpu_custom_call" | custom-call | flops 1 | bytes 1 | tf_op jit(solution)/shard_map/pallas_call | solution.py:416
  258.8 4.6 %collective-permute-done.22 = bf16[512,512]{1,0:T(8,128)(2,1)} collective-permute-done((bf16[512,512]{1,0:T(8,128)(2,1)}, bf16[512,512]{1,0:T(8,128)(2,1)}, u32[]{:S(2)}, u32[]{:S(2)}) %collective-permute-start.22) | collective-permute-done | bytes 524320 | tf_op jit(solution)/shard_map/ppermute | solution.py:725
  274.0 3.6 %shard_map.254 = bf16[256,1024]{1,0:T(8,128)(2,1)} custom-call(s32[2]{0:T(128)} %pad_add_fusion.t, bf16[512,1024]{1,0:T(8,128)(2,1)} %get-tuple-element.73.refs_0_, bf16[512,1024]{1,0:T(8,128)(2,1)} %copy-done.9, bf16[256,1024]{1,0:T(8,128)(2,1)} %collective-permute-done.21.refs_2_, f32[256,1024]{1,0:T(8,128)} %get-tuple-element.83.refs_3_), custom_call_target="tpu_custom_call" | custom-call | flops 1 | bytes 1 | tf_op jit(solution)/shard_map/pallas_call | solution.py:613
  289.2 4.5 %collective-permute-done.28 = bf16[128,512]{1,0:T(8,128)(2,1)S(1)} collective-permute-done((bf16[128,512]{1,0:T(8,128)(2,1)S(1)}, bf16[128,512]{1,0:T(8,128)(2,1)S(1)}, u32[]{:S(2)}, u32[]{:S(2)}) %collective-permute-start.28) | collective-permute-done | bytes 131104 | tf_op jit(solution)/shard_map/ppermute | solution.py:725
  293.7 3.4 collective-permute-start.31
  299.5 4.3 %collective-permute-done.32 = bf16[128,768]{1,0:T(8,128)(2,1)S(1)} collective-permute-done((bf16[128,768]{1,0:T(8,128)(2,1)S(1)}, bf16[128,768]{1,0:T(8,128)(2,1)S(1)}, u32[]{:S(2)}, u32[]{:S(2)}) %collective-permute-start.32) | collective-permute-done | bytes 196640 | tf_op jit(solution)/shard_map/ppermute | solution.py:725
  305.9 3.5 shard_map.258
  317.2 4.3 %shard_map.256 = f32[256,1024]{1,0:T(8,128)} custom-call(s32[2]{0:T(128)} %pad_add_fusion.t, bf16[512,1024]{1,0:T(8,128)(2,1)} %get-tuple-element.98.refs_0_, bf16[512,1024]{1,0:T(8,128)(2,1)} %copy-done.13, bf16[256,1024]{1,0:T(8,128)(2,1)} %copy-done.21, bf16[256,2048]{1,0:T(8,128)(2,1)} %shard_map.247.refs_0_.refs_3_.refs_4_.refs_12_, ...), custom_call_target="tpu_custom_call" | custom-call | flops 1 | bytes 1 | tf_op jit(solution)/shard_map/pallas_call | solution.py:632
  324.3 9.0 %collective-permute-done.34 = bf16[144,1024]{1,0:T(8,128)(2,1)S(1)} collective-permute-done((bf16[144,1024]{1,0:T(8,128)(2,1)}, bf16[144,1024]{1,0:T(8,128)(2,1)S(1)}, u32[]{:S(2)}, u32[]{:S(2)}) %collective-permute-start.34) | collective-permute-done | bytes 294944 | tf_op jit(solution)/shard_map/ppermute | solution.py:725
  333.3 6.7 %collective-permute-done.35 = bf16[144,1024]{1,0:T(8,128)(2,1)} collective-permute-done((bf16[144,1024]{1,0:T(8,128)(2,1)}, bf16[144,1024]{1,0:T(8,128)(2,1)}, u32[]{:S(2)}, u32[]{:S(2)}) %collective-permute-start.35) | collective-permute-done | bytes 294944 | tf_op jit(solution)/shard_map/ppermute | solution.py:725
  (190 shorter events, 103.6 us)
Async XLA Ops:
  7.2 146.0 %all-gather.2.cloned.1.call-start = ((), (), s32[]{:S(2)}) async-start(), calls=%async_computation.1 | async-start | bytes 5308416 | tf_op jit(solution)/shard_map/all_gather | solution.py:847
  13.7 25.1 %collective-permute-start.1 = (bf16[256,2048]{1,0:T(8,128)(2,1)}, bf16[256,2048]{1,0:T(8,128)(2,1)S(1)}, u32[]{:S(2)}, u32[]{:S(2)}) collective-permute-start(bf16[256,2048]{1,0:T(8,128)(2,1)} %shard_map.247.refs_0_.refs_3_.refs_4_.refs_12_), channel_id=1, source_target_pairs={{0,2},{1,3},{2,0},{3,1},{4,6},{5,7},{6,4},{7,5},{8,10},{9,11},{10,... | collective-permute-start | bytes 3145736 | tf_op jit(solution)/shard_map/ppermute | solution.py:728
  15.2 21.1 %collective-permute-start.4 = (bf16[144,1536]{1,0:T(8,128)(2,1)S(1)}, bf16[144,1536]{1,0:T(8,128)(2,1)S(1)}, u32[]{:S(2)}, u32[]{:S(2)}) collective-permute-start(bf16[144,1536]{1,0:T(8,128)(2,1)S(1)} %copy-done), channel_id=1, source_target_pairs={{0,16},{4,20},{8,24},{12,28},{16,0},{20,4},{24,8},{28,12},{1,17},{... | collective-permute-start | bytes 1327112 | tf_op jit(solution)/shard_map/ppermute | solution.py:725
  17.8 19.6 %collective-permute-start.3 = (bf16[144,1536]{1,0:T(8,128)(2,1)S(1)}, bf16[144,1536]{1,0:T(8,128)(2,1)S(1)}, u32[]{:S(2)}, u32[]{:S(2)}) collective-permute-start(bf16[144,1536]{1,0:T(8,128)(2,1)S(1)} %copy-done), channel_id=1, source_target_pairs={{0,8},{4,12},{8,0},{12,4},{16,24},{20,28},{24,16},{28,20},{1,9},{5... | collective-permute-start | bytes 1327112 | tf_op jit(solution)/shard_map/ppermute | solution.py:725
  18.2 19.1 %collective-permute-start.2 = (bf16[144,1536]{1,0:T(8,128)(2,1)S(1)}, bf16[144,1536]{1,0:T(8,128)(2,1)S(1)}, u32[]{:S(2)}, u32[]{:S(2)}) collective-permute-start(bf16[144,1536]{1,0:T(8,128)(2,1)S(1)} %copy-done), channel_id=1, source_target_pairs={{0,4},{4,0},{8,12},{12,8},{16,20},{20,16},{24,28},{28,24},{1,5},{5... | collective-permute-start | bytes 1327112 | tf_op jit(solution)/shard_map/ppermute | solution.py:725
  38.8 267.0 %reduce-scatter.2.cloned.1.call-start = ((), (), s32[]{:S(2)}) async-start(), calls=%async_computation.2 | async-start | bytes 3538944 | tf_op jit(solution)/shard_map/reduce_scatter | solution.py:884
  38.9 52.6 %collective-permute-start = (bf16[256,2048]{1,0:T(8,128)(2,1)}, bf16[256,2048]{1,0:T(8,128)(2,1)S(1)}, u32[]{:S(2)}, u32[]{:S(2)}) collective-permute-start(bf16[256,2048]{1,0:T(8,128)(2,1)} %shard_map.247.refs_0_.refs_3_.refs_4_.refs_12_), channel_id=1, source_target_pairs={{0,1},{1,0},{2,3},{3,2},{4,5},{5,4},{6,7},{7,6},{8,9},{9,8},{10,11... | collective-permute-start | bytes 3145736 | tf_op jit(solution)/shard_map/ppermute | solution.py:728
  39.0 52.6 %collective-permute-start.5 = (bf16[256,2048]{1,0:T(8,128)(2,1)S(1)}, bf16[256,2048]{1,0:T(8,128)(2,1)}, u32[]{:S(2)}, u32[]{:S(2)}) collective-permute-start(bf16[256,2048]{1,0:T(8,128)(2,1)S(1)} %collective-permute-done.1.refs_2_.refs_6_.refs_14_), channel_id=1, source_target_pairs={{0,1},{1,0},{2,3},{3,2},{4,5},{5,4},{6,7},{7,6},{8,9},{9,8},{10,11... | collective-permute-start | bytes 3145736 | tf_op jit(solution)/shard_map/ppermute | solution.py:728
  39.5 40.7 %collective-permute-start.6 = (bf16[144,1536]{1,0:T(8,128)(2,1)S(1)}, bf16[144,1536]{1,0:T(8,128)(2,1)}, u32[]{:S(2)}, u32[]{:S(2)}) collective-permute-start(bf16[144,1536]{1,0:T(8,128)(2,1)S(1)} %copy-done), channel_id=1, source_target_pairs={{0,24},{4,28},{8,16},{12,20},{16,8},{20,12},{24,0},{28,4},{1,25},{... | collective-permute-start | bytes 1327112 | tf_op jit(solution)/shard_map/ppermute | solution.py:725
  41.0 50.5 %collective-permute-start.8 = (bf16[144,1536]{1,0:T(8,128)(2,1)S(1)}, bf16[144,1536]{1,0:T(8,128)(2,1)}, u32[]{:S(2)}, u32[]{:S(2)}) collective-permute-start(bf16[144,1536]{1,0:T(8,128)(2,1)S(1)} %collective-permute-done.4.refs_6_.refs_2_.refs_18_.refs_26_), channel_id=1, source_target_pairs={{0,4},{4,0},{8,12},{12,8},{16,20},{20,16},{24,28},{28,24},{1,5},{5... | collective-permute-start | bytes 1327112 | tf_op jit(solution)/shard_map/ppermute | solution.py:725
  41.5 50.0 %collective-permute-start.7 = (bf16[144,1536]{1,0:T(8,128)(2,1)S(1)}, bf16[144,1536]{1,0:T(8,128)(2,1)}, u32[]{:S(2)}, u32[]{:S(2)}) collective-permute-start(bf16[144,1536]{1,0:T(8,128)(2,1)S(1)} %collective-permute-done.3.refs_5_.refs_1_.refs_17_.refs_25_), channel_id=1, source_target_pairs={{0,4},{4,0},{8,12},{12,8},{16,20},{20,16},{24,28},{28,24},{1,5},{5... | collective-permute-start | bytes 1327112 | tf_op jit(solution)/shard_map/ppermute | solution.py:725
  119.4 14.0 %collective-permute-start.11 = (bf16[256,1024]{1,0:T(8,128)(2,1)S(1)}, bf16[256,1024]{1,0:T(8,128)(2,1)S(1)}, u32[]{:S(2)}, u32[]{:S(2)}) collective-permute-start(bf16[256,1024]{1,0:T(8,128)(2,1)S(1)} %add_convert_fusion.3), channel_id=1, source_target_pairs={{0,2},{1,3},{2,0},{3,1},{4,6},{5,7},{6,4},{7,5},{8,10},{9,11},{10,... | collective-permute-start | bytes 1572872 | tf_op jit(solution)/shard_map/ppermute | solution.py:728
  186.9 14.0 %collective-permute-start.16 = (bf16[256,1024]{1,0:T(8,128)(2,1)S(1)}, bf16[256,1024]{1,0:T(8,128)(2,1)S(1)}, u32[]{:S(2)}, u32[]{:S(2)}) collective-permute-start(bf16[256,1024]{1,0:T(8,128)(2,1)S(1)} %add_convert_fusion.2), channel_id=1, source_target_pairs={{0,2},{1,3},{2,0},{3,1},{4,6},{5,7},{6,4},{7,5},{8,10},{9,11},{10,... | collective-permute-start | bytes 1572872 | tf_op jit(solution)/shard_map/ppermute | solution.py:728
  223.6 35.2 %collective-permute-start.23 = (bf16[512,768]{1,0:T(8,128)(2,1)}, bf16[512,768]{1,0:T(8,128)(2,1)}, u32[]{:S(2)}, u32[]{:S(2)}) collective-permute-start(bf16[512,768]{1,0:T(8,128)(2,1)} %convolution_convert_fusion.3), channel_id=1, source_target_pairs={{0,4},{4,0},{8,12},{12,8},{16,20},{20,16},{24,28},{28,24},{1,5},{5... | collective-permute-start | bytes 2359304 | tf_op jit(solution)/shard_map/ppermute | solution.py:725
  226.6 36.8 %collective-permute-start.22 = (bf16[512,512]{1,0:T(8,128)(2,1)}, bf16[512,512]{1,0:T(8,128)(2,1)}, u32[]{:S(2)}, u32[]{:S(2)}) collective-permute-start(bf16[512,512]{1,0:T(8,128)(2,1)} %convolution_convert_fusion.6), channel_id=1, source_target_pairs={{0,4},{4,0},{8,12},{12,8},{16,20},{20,16},{24,28},{28,24},{1,5},{5... | collective-permute-start | bytes 1572872 | tf_op jit(solution)/shard_map/ppermute | solution.py:725
  228.6 34.8 %collective-permute-start.21 = (bf16[256,1024]{1,0:T(8,128)(2,1)}, bf16[256,1024]{1,0:T(8,128)(2,1)}, u32[]{:S(2)}, u32[]{:S(2)}) collective-permute-start(bf16[256,1024]{1,0:T(8,128)(2,1)} %add_convert_fusion.1), channel_id=1, source_target_pairs={{0,2},{1,3},{2,0},{3,1},{4,6},{5,7},{6,4},{7,5},{8,10},{9,11},{10,... | collective-permute-start | bytes 1572872 | tf_op jit(solution)/shard_map/ppermute | solution.py:728
  263.4 14.2 %collective-permute-start.24 = (bf16[512,1024]{1,0:T(8,128)(2,1)}, bf16[512,1024]{1,0:T(8,128)(2,1)S(1)}, u32[]{:S(2)}, u32[]{:S(2)}) collective-permute-start(bf16[512,1024]{1,0:T(8,128)(2,1)} %get-tuple-element.99), channel_id=1, source_target_pairs={{0,1},{1,0},{2,3},{3,2},{4,5},{5,4},{6,7},{7,6},{8,9},{9,8},{10,11... | collective-permute-start | bytes 3145736 | tf_op jit(solution)/shard_map/ppermute | solution.py:728
  270.8 28.7 %collective-permute-start.26 = (bf16[576,1024]{1,0:T(8,128)(2,1)}, bf16[576,1024]{1,0:T(8,128)(2,1)}, u32[]{:S(2)}, u32[]{:S(2)}) collective-permute-start(bf16[576,1024]{1,0:T(8,128)(2,1)} %pad_maximum_fusion), channel_id=1, source_target_pairs={{0,4},{4,0},{8,12},{12,8},{16,20},{20,16},{24,28},{28,24},{1,5},{5... | collective-permute-start | bytes 3538952 | tf_op jit(solution)/shard_map/ppermute | solution.py:725
  280.0 17.1 %collective-permute-start.27 = (bf16[128,512]{1,0:T(8,128)(2,1)S(1)}, bf16[128,512]{1,0:T(8,128)(2,1)S(1)}, u32[]{:S(2)}, u32[]{:S(2)}) collective-permute-start(bf16[128,512]{1,0:T(8,128)(2,1)S(1)} %get-tuple-element.146), channel_id=1, source_target_pairs={{0,8},{4,12},{8,0},{12,4},{16,24},{20,28},{24,16},{28,20},{1,9},{5... | collective-permute-start | bytes 393224 | tf_op jit(solution)/shard_map/ppermute | solution.py:725
  282.9 33.5 %collective-permute-start.25 = (bf16[256,1024]{1,0:T(8,128)(2,1)S(1)}, bf16[256,1024]{1,0:T(8,128)(2,1)S(1)}, u32[]{:S(2)}, u32[]{:S(2)}) collective-permute-start(bf16[256,1024]{1,0:T(8,128)(2,1)S(1)} %add_convert_fusion), channel_id=1, source_target_pairs={{0,2},{1,3},{2,0},{3,1},{4,6},{5,7},{6,4},{7,5},{8,10},{9,11},{10,... | collective-permute-start | bytes 1572872 | tf_op jit(solution)/shard_map/ppermute | solution.py:728
  288.3 15.4 %collective-permute-start.32 = (bf16[128,768]{1,0:T(8,128)(2,1)S(1)}, bf16[128,768]{1,0:T(8,128)(2,1)S(1)}, u32[]{:S(2)}, u32[]{:S(2)}) collective-permute-start(bf16[128,768]{1,0:T(8,128)(2,1)S(1)} %get-tuple-element.141), channel_id=1, source_target_pairs={{0,24},{4,28},{8,16},{12,20},{16,8},{20,12},{24,0},{28,4},{1,25},{... | collective-permute-start | bytes 589832 | tf_op jit(solution)/shard_map/ppermute | solution.py:725
  309.4 14.9 %collective-permute-start.33 = (bf16[144,1024]{1,0:T(8,128)(2,1)}, bf16[144,1024]{1,0:T(8,128)(2,1)S(1)}, u32[]{:S(2)}, u32[]{:S(2)}) collective-permute-start(bf16[144,1024]{1,0:T(8,128)(2,1)} %get-tuple-element.112), channel_id=1, source_target_pairs={{0,8},{4,12},{8,0},{12,4},{16,24},{20,28},{24,16},{28,20},{1,9},{5... | collective-permute-start | bytes 884744 | tf_op jit(solution)/shard_map/ppermute | solution.py:725
  312.6 20.6 %collective-permute-start.34 = (bf16[144,1024]{1,0:T(8,128)(2,1)}, bf16[144,1024]{1,0:T(8,128)(2,1)S(1)}, u32[]{:S(2)}, u32[]{:S(2)}) collective-permute-start(bf16[144,1024]{1,0:T(8,128)(2,1)} %get-tuple-element.113), channel_id=1, source_target_pairs={{0,16},{4,20},{8,24},{12,28},{16,0},{20,4},{24,8},{28,12},{1,17},{... | collective-permute-start | bytes 884744 | tf_op jit(solution)/shard_map/ppermute | solution.py:725
  312.9 27.0 %collective-permute-start.35 = (bf16[144,1024]{1,0:T(8,128)(2,1)}, bf16[144,1024]{1,0:T(8,128)(2,1)}, u32[]{:S(2)}, u32[]{:S(2)}) collective-permute-start(bf16[144,1024]{1,0:T(8,128)(2,1)} %get-tuple-element.114), channel_id=1, source_target_pairs={{0,24},{4,28},{8,16},{12,20},{16,8},{20,12},{24,0},{28,4},{1,25},{... | collective-permute-start | bytes 884744 | tf_op jit(solution)/shard_map/ppermute | solution.py:725
  (54 other events, 602.1 us)
Sparse Core Ops, SparseCore 0:
  39.0 89.8 all-gather.1
  185.6 84.9 reduce-scatter.1

commit v3 on v2

--- a/solution.py
+++ b/solution.py
@@ -325,14 +325,28 @@
     return du, dgain
 
 
-def attn_backward_kernel(rows, blocks, group, kv_heads, nw, t, *refs):
-    packed, seg_col, seg_row, inv, raw, cos, sin, gains = refs[:8]
-    refs = refs[8:]
+def fill_gain_rows(d_attn, d_mlp, d_heads, outs):
+    n = outs[0].shape[0] // GAIN_ROWS
+    at = lax.broadcasted_iota(jnp.int32, (GAIN_ROWS, 4 * HEAD), 0)
+    for k, out in enumerate(outs):
+        out[...] = jnp.zeros_like(out)
+        for p in range(n):
+            here = slice((k * n + p) * HEAD, (k * n + p + 1) * HEAD)
+            row = jnp.concatenate(
+                [d_attn[0:1, here], d_mlp[0:1, here], d_heads[0:1], d_heads[1:2]], axis=1
+            )
+            rows = slice(p * GAIN_ROWS, (p + 1) * GAIN_ROWS)
+            out[rows, : 4 * HEAD] = jnp.where(at == 0, row, 0.0).astype(BF16)
+
+
+def attn_backward_kernel(rows, blocks, group, kv_heads, nw, packed_gains, t, *refs):
+    packed, seg_col, seg_row, inv, raw, cos, sin, gains, dgain_mlp = refs[:9]
+    refs = refs[9:]
     branch, refs = refs[:blocks], refs[blocks:]
     xs, refs = refs[:blocks], refs[blocks:]
     w_os, refs = refs[:nw], refs[nw:]
     w_qkvs, refs = refs[:nw], refs[nw:]
-    dpacked, dgain, keep, send, dgain_x, dk, dv, dmix, w_o, w_qkv, acc = refs
+    dpacked, dgain, keep, send, dgain_x, *tails, dk, dv, dmix, w_o, w_qkv, acc, heads = refs
     causal = lax.broadcasted_iota(jnp.int32, (rows, rows), 0) <= lax.broadcasted_iota(
         jnp.int32, (rows, rows), 1
     )
@@ -394,6 +408,7 @@
         dpacked[pl.ds(at, rows), kc : kc + HEAD] = du.astype(BF16)
         dpacked[pl.ds(at, rows), kc + HEAD : kc + 2 * HEAD] = dv[here, :].astype(BF16)
     accumulate(mm(dpacked[...], w_qkv[...], 1, 1), acc)
+    accumulate(dgain[0], heads)
 
     @pl.when(pl.program_id(0) == kv_heads - 1)
     def _():
@@ -403,18 +418,41 @@
             ur = u * lax.rsqrt(jnp.mean(u * u, axis=1, keepdims=True) + EPS)
             total = total + jnp.sum(acc[k * rows : (k + 1) * rows, :] * ur, axis=0, keepdims=True)
         dgain_x[...] = jnp.broadcast_to(total, dgain_x.shape)
+        if packed_gains:
+            fill_gain_rows(dgain_x, dgain_mlp, heads[...], tails)
         split_rows(rows, acc, keep, send)
 
 
 def attn_backward(
-    t, packed, seg_col, seg_row, inv, raw, cos, sin, gains, branch, xs, w_o, first, w_qkv, width, kv_heads, group
+    t,
+    packed_gains,
+    packed,
+    seg_col,
+    seg_row,
+    inv,
+    raw,
+    cos,
+    sin,
+    gains,
+    dgain_mlp,
+    branch,
+    xs,
+    w_o,
+    first,
+    w_qkv,
+    width,
+    kv_heads,
+    group,
 ):
     n = packed.shape[0]
     rows = xs[0].shape[0]
     q_cols = group * HEAD
     cols = q_cols + 2 * HEAD
-    return call(
-        functools.partial(attn_backward_kernel, rows, n // rows, group, kv_heads, len(w_o)),
+    tails = [(len(w_o) // 2 * GAIN_ROWS, kv_heads * cols)] * 2 if packed_gains else []
+    return call(
+        functools.partial(
+            attn_backward_kernel, rows, n // rows, group, kv_heads, len(w_o), packed_gains
+        ),
         (kv_heads,),
         [
             by_head(n, cols),
@@ -425,6 +463,7 @@
             whole(cos.shape),
             whole(sin.shape),
             whole(gains.shape),
+            whole(dgain_mlp.shape),
         ]
         + [whole(b.shape) for b in branch]
         + [part_at((rows, width), 0) for _ in xs]
@@ -436,14 +475,16 @@
             whole((n // 2, width)),
             whole((n // 2, width)),
             whole((8, width)),
-        ],
+        ]
+        + [whole(shape) for shape in tails],
         [
             shape_of(packed.shape),
             shape_of((kv_heads, 8, HEAD), F32),
             shape_of((n // 2, width)),
             shape_of((n // 2, width)),
             shape_of((8, width), F32),
-        ],
+        ]
+        + [shape_of(shape) for shape in tails],
         kv_heads * group * n * n * HEAD * 10,
         [
             pltpu.VMEM((n, HEAD), F32),
@@ -452,8 +493,9 @@
             pltpu.VMEM((width, q_cols), BF16),
             pltpu.VMEM((width, cols), BF16),
             pltpu.VMEM((n, width), F32),
+            pltpu.VMEM((8, HEAD), F32),
         ],
-    )(t, packed, seg_col, seg_row, inv, raw, cos, sin, gains, *branch, *xs, *w_o, *w_qkv)
+    )(t, packed, seg_col, seg_row, inv, raw, cos, sin, gains, dgain_mlp, *branch, *xs, *w_o, *w_qkv)
 
 
 def join_in_order(t, reorder, block, out):
@@ -663,30 +705,6 @@
     return join(q), join(k), join(v)
 
 
-def gain_rows_kernel(t, d_attn, d_mlp, d_heads, out):
-    heads = jnp.sum(d_heads[...], axis=0)
-    at = lax.broadcasted_iota(jnp.int32, (GAIN_ROWS, 4 * HEAD), 0)
-    for p in range(d_attn.shape[1] // HEAD):
-        here = slice(p * HEAD, (p + 1) * HEAD)
-        row = jnp.concatenate([d_attn[0:1, here], d_mlp[0:1, here], heads[0:1], heads[1:2]], axis=1)
-        rows = slice(p * GAIN_ROWS, (p + 1) * GAIN_ROWS)
-        out[rows, : 4 * HEAD] = jnp.where(at == 0, row, 0.0).astype(BF16)
-        out[rows, 4 * HEAD :] = jnp.zeros((GAIN_ROWS, out.shape[1] - 4 * HEAD), BF16)
-
-
-def gain_rows(t, d_attn, d_mlp, d_heads, cols):
-    args = (d_attn, d_mlp, d_heads)
-    rows = d_attn.shape[1] // HEAD * GAIN_ROWS
-    return call(
-        gain_rows_kernel,
-        (1,),
-        [whole(a.shape) for a in args],
-        whole((rows, cols)),
-        shape_of((rows, cols)),
-        rows * HEAD,
-    )(t, *args)
-
-
 def pair_sum_kernel(t, keep, rows, got, *outs):
     n = keep.shape[0] // len(outs)
     for z, out in enumerate(outs):
@@ -762,7 +780,7 @@
         far = self.over_tensor(x, 2)
         return [x, self.over_tensor(x, 1), far, self.over_tensor(tie(far, *after) if after else far, 1)]
 
-    def scatter_tensor(self, keep, send):
+    def scatter_tensor(self, keep, send, sent=False):
         rows = 2 * keep.shape[0] // self.tensor
         if not self.direct:
             blocks = []
@@ -770,9 +788,10 @@
                 blocks += [keep[k * rows : (k + 1) * rows], send[k * rows : (k + 1) * rows]]
             full = jnp.concatenate(blocks, axis=0)
             return [lax.psum_scatter(full, "tensor", scatter_dimension=0, tiled=True)]
-        got = self.over_tensor(send, 1)
+        got = send if sent else self.over_tensor(send, 1)
         far = keep[rows:].astype(F32) + got[rows:].astype(F32)
-        return [keep, got, self.over_tensor(far.astype(BF16), 2)]
+        far = far.astype(BF16)
+        return [keep, got, self.over_tensor(far, 2), far]
 
 
 def rope_tables(offsets):
@@ -841,8 +860,8 @@
         far = links.over_tensor(both, 2)
         across = tie(far, attn_far, attn_near[1], attn_near[2])
         rows_all = [both, beside, far, links.over_tensor(across, 1)]
-        w_mlp = tie(w_mlp, (far, attn_far, attn_near[1], attn_near[2]))
         w_attn = attn_near + [attn_far] + [links.over_dp(b, 1) for b in attn_near[1:]]
+        w_mlp = tie(w_mlp, (far, attn_far, attn_near[1], attn_near[2], w_attn[5]))
         w_qkv, w_o, o_index = w_attn, w_attn, kv_heads * (group + 2) * HEAD // q_cols
         w_gu = w_d = lax.all_gather(w_mlp, "dp", axis=0, tiled=True)
         d_index = 2
@@ -874,46 +893,44 @@
         t, packed, seg_col, seg_row, w_o, o_index, rows, width, kv_heads, group
     )
     parts = links.scatter_tensor(keep, send)
-    hidden, normed_mlp = hidden_call(t, parts, own, gains, rows, width)
+    hidden, normed_mlp = hidden_call(t, parts[:3], own, gains, rows, width)
     normed_mlp = links.gather_tensor(normed_mlp)
     act, d_gu, normed_mlp, cot, dx_keep, dx_send, out_keep, out_send = mlp_call(
         t, direct, normed_mlp, rows_all, 1, w_gu, w_d, d_index, ff, width
     )
     parts = links.scatter_tensor(dx_keep, dx_send)
-    gu_sum = mm(normed_mlp, tie(d_gu, parts[:2]), 0, 0).astype(BF16)
+    down = links.send_half(cot, tie(act, parts[1:2]))
+    d_hidden, branch, d_gain_mlp = d_hidden_call(t, parts[:3], hidden, own, 1, gains, rows, width)
+    gu_sum = mm(normed_mlp, tie(d_gu, branch), 0, 0).astype(BF16)
     gu = lax.psum_scatter(gu_sum, "dp", scatter_dimension=0, tiled=True)
-    d_hidden, branch, d_gain_mlp = d_hidden_call(
-        t, tie(parts, gu_sum), hidden, own, 1, gains, rows, width
-    )
-    down = links.send_half(cot, tie(act, branch))
-    branch = links.gather_tensor(branch, down[1])
-    out_parts = links.scatter_tensor(out_keep, tie(out_send, branch))
-    out = links.send_half(jnp.concatenate(branch, axis=0), mixed)
-    d_packed, d_gain_heads, keep, send, d_gain_attn = tie(
+    branch = links.gather_tensor(branch, gu_sum, down[0])
+    down = links.send_quarters(*down)
+    out_parts = links.scatter_tensor(out_keep, tie(out_send, branch))[:3]
+    branch_rows = jnp.concatenate(branch, axis=0)
+    out_sent = outer_half(branch_rows, mixed, 1)
+    if direct:
+        out_sent = links.over_dp(out_sent, 1)
+    d_packed, d_gain_heads, keep, send, d_gain_attn, *tails = tie(
         attn_backward(
-            t, packed, seg_col, seg_row, inv, raw, cos, sin, gains, branch, rows_all, w_o, o_index, w_qkv,
-            width, kv_heads, group,
+            t, direct, packed, seg_col, seg_row, inv, raw, cos, sin, gains, d_gain_mlp, branch, rows_all,
+            w_o, o_index, w_qkv, width, kv_heads, group,
         ),
-        out[0],
-        down[0],
+        out_sent,
+        down[1:],
         out_parts,
     )
     if direct:
-        tails = gain_rows(t, d_gain_attn, d_gain_mlp, d_gain_heads, d_packed.shape[1])
-        half = tails.shape[0] // 2
-        send_qkv = jnp.concatenate([outer_half(normed, d_packed, 1), tails[half:]], axis=0)
+        send_qkv = jnp.concatenate([outer_half(normed, d_packed, 1), tails[1]], axis=0)
         got = links.over_dp(send_qkv, 1)
-        parts = links.scatter_tensor(keep, send)
-        out, down = tie((out, down), parts[:2])
-        out = links.send_quarters(*out)
-        down = links.send_quarters(*down)
-        qkv = pair_sum(t, outer_half(normed, d_packed, 0), tails[:half], tie(got, out[1:], down[1:], gu), 4)
+    parts = links.scatter_tensor(keep, send)[:3]
+    out = (out_sent, outer_half(branch_rows, tie(mixed, parts[:2]), 0))
+    out = links.send_quarters(*tie(out, parts[:2]))
+    if direct:
+        keep_qkv = outer_half(normed, d_packed, 0)
+        qkv = pair_sum(t, keep_qkv, tails[0], tie(got, out[1:], parts[2]), 4)
         qkv = [qkv[0]] + [links.over_dp(qkv[z], 2 * z) for z in (1, 2, 3)]
     else:
         qkv = links.send_quarters(*links.send_half(normed, d_packed))
-        out = links.send_quarters(*out)
-        down = links.send_quarters(*down)
-        parts = links.scatter_tensor(keep, send)
     d_tokens = d_tokens_call(t, direct, parts, own, d_hidden, gains, rows, width)
     activations = activations_call(t, direct, out_parts, hidden, rows, width)
     grad_down = shard_of(down).T

time: 359 us -> 355 us (0.989)
    ppermute x19, starting transfers between devices: 21.1 us -> 28.1 us  [over_dp(): return lax.ppermute(x, 'dp', xor_pairs(self.dp, bits))]
    ppermute x19, waiting for transfers between devices: 96 us -> 102 us  [over_dp(): return lax.ppermute(x, 'dp', xor_pairs(self.dp, bits))]
    ppermute x19, starting transfers between devices: 12.9 us -> 7.26 us  [over_tensor(): return lax.ppermute(x, 'tensor', xor_pairs(self.tensor, bits))]
    ppermute x19, waiting for transfers between devices: 58.5 us -> 53.5 us  [over_tensor(): return lax.ppermute(x, 'tensor', xor_pairs(self.tensor, bits))]
    unnamed x81 -> x91, local copies, waits for them, and re-layouts: 8.61 us -> 8.42 us
  transfers between devices with their start and end apart: 40 -> 40, of which waited for: 23 -> 20; matrix products, arithmetic and copies ran while one was open for 10% -> 11% of each run, Pallas kernels for 20% -> 20%
where the time goes in v3:
time: 355 us; the launch traced here: 351 us
  waiting for transfers between devices  155 us (44%)
  Pallas kernels  96.5 us (27%)
  starting transfers between devices  35.4 us (10%)
  matrix products  20.9 us (6%)
  other arithmetic  16.1 us (5%)
  between operations  14.8 us (4%)
  local copies, waits for them, and re-layouts  11.9 us (3%)
    ppermute x19, waiting for transfers between devices, over_dp(): return lax.ppermute(x, 'dp', xor_pairs(self.dp, bits))  102 us
    ppermute x19, waiting for transfers between devices, over_tensor(): return lax.ppermute(x, 'tensor', xor_pairs(self.tensor, bits))  53.5 us
    ppermute x19, starting transfers between devices, over_dp(): return lax.ppermute(x, 'dp', xor_pairs(self.dp, bits))  28.1 us
    pallas_call x1, Pallas kernels, attn_backward(): call(functools.partial(attn_backward_kernel, rows, n // rows, group, kv_h...  25.9 us
    dot_general x7, matrix products, mm(): lax.dot_general(a, b, (((ca,), (cb,)), ((), ())), preferred_element_type=...  20.9 us
    pallas_call x1, Pallas kernels, mlp_call(): call(functools.partial(mlp_kernel, ff, len(xs), reorder), (len(xs),), [wh...  20.5 us
    pallas_call x1, Pallas kernels, attn_forward(): call(functools.partial(attn_forward_kernel, rows, n // rows, group, kv_he...  12.7 us
    pallas_call x1, Pallas kernels, qkv_call(): call(functools.partial(qkv_kernel, len(xs), len(ws), packed_gains, kv_hea...  9.58 us
  transfers between devices with their start and end apart: 40, of which 20 were waited for; matrix products, arithmetic and copies ran while one was open for 11% of the time, Pallas kernels for 20%

profile of v3, /device:TPU:12, one launch (start us, length us, event | category | flops | bytes accessed | tf_op | source)
XLA Modules:
  0.0 350.8 jit_solution(12054227378892244186)
XLA Ops:
  10.4 3.3 shard_map.247.refs_0_.refs_3_.refs_4_.refs_13_
  18.7 15.4 %collective-permute-done.3.refs_5_.refs_1_.refs_18_.refs_26_ = bf16[144,1536]{1,0:T(8,128)(2,1)S(1)} collective-permute-done((bf16[144,1536]{1,0:T(8,128)(2,1)S(1)}, bf16[144,1536]{1,0:T(8,128)(2,1)S(1)}, u32[]{:S(2)}, u32[]{:S(2)}) %collective-permute-start.3) | collective-permute-done | bytes 442400 | tf_op jit(solution)/shard_map/ppermute | solution.py:743
  37.4 7.5 %collective-permute-done.7.refs_9_.refs_5_.refs_22_.refs_30_ = bf16[144,1536]{1,0:T(8,128)(2,1)S(1)} collective-permute-done((bf16[144,1536]{1,0:T(8,128)(2,1)S(1)}, bf16[144,1536]{1,0:T(8,128)(2,1)S(1)}, u32[]{:S(2)}, u32[]{:S(2)}) %collective-permute-start.7) | collective-permute-done | bytes 442400 | tf_op jit(solution)/shard_map/ppermute | solution.py:743
  48.6 35.6 %collective-permute-done.6.refs_7_.refs_3_.refs_20_.refs_28_ = bf16[144,1536]{1,0:T(8,128)(2,1)} collective-permute-done((bf16[144,1536]{1,0:T(8,128)(2,1)S(1)}, bf16[144,1536]{1,0:T(8,128)(2,1)}, u32[]{:S(2)}, u32[]{:S(2)}) %collective-permute-start.6) | collective-permute-done | bytes 442400 | tf_op jit(solution)/shard_map/ppermute | solution.py:743
  89.1 3.6 %collective-permute-done.9.refs_11_.refs_7_.refs_24_.refs_32_ = bf16[144,1536]{1,0:T(8,128)(2,1)S(1)} collective-permute-done((bf16[144,1536]{1,0:T(8,128)(2,1)}, bf16[144,1536]{1,0:T(8,128)(2,1)S(1)}, u32[]{:S(2)}, u32[]{:S(2)}) %collective-permute-start.9) | collective-permute-done | bytes 442400 | tf_op jit(solution)/shard_map/ppermute | solution.py:743
  93.8 9.6 %shard_map.248 = (bf16[1024,1024]{1,0:T(8,128)(2,1)}, bf16[1024,1024]{1,0:T(8,128)(2,1)}, f32[1024,768]{1,0:T(8,128)}, f32[8,1024]{1,0:T(8,128)}) custom-call(s32[2]{0:T(128)} %pad_add_fusion.t, bf16[256,2048]{1,0:T(8,128)(2,1)} %shard_map.247.refs_0_.refs_3_.refs_4_.refs_13_, bf16[256,2048]{1,0:T(8,128)(2,1)} %copy-done.2, bf16[256,2048]{1,0:T(8,128)(2,1)} %copy-done.1, ...), custom_call_target="tpu_custom_call" | custom-call | flops 1 | bytes 1 | tf_op jit(solution)/shard_map/pallas_call | solution.py:210
  103.4 12.7 %shard_map.249 = (bf16[1024,512]{1,0:T(8,128)(2,1)}, f32[2,8,1024]{2,1,0:T(8,128)}, bf16[512,1024]{1,0:T(8,128)(2,1)}, bf16[512,1024]{1,0:T(8,128)(2,1)}) custom-call(s32[2]{0:T(128)} %pad_add_fusion.t, bf16[1024,1024]{1,0:T(8,128)(2,1)} %get-tuple-element.62.packed.refs_0_, s32[1024,1]{1,0:T(8,128)} %copy.30.seg_col.refs_1_, s32[1,1024]{1,0:T(1,128)} %refs_2_.1, ...), custom_call_target="tpu_custom_call" | custom-call | flops 1 | bytes 1 | tf_op jit(solution)/shard_map/pallas_call | solution.py:296
  121.1 13.6 %collective-permute-done.11.refs_2_ = bf16[256,1024]{1,0:T(8,128)(2,1)S(1)} collective-permute-done((bf16[256,1024]{1,0:T(8,128)(2,1)S(1)}, bf16[256,1024]{1,0:T(8,128)(2,1)S(1)}, u32[]{:S(2)}, u32[]{:S(2)}) %collective-permute-start.11) | collective-permute-done | bytes 524320 | tf_op jit(solution)/shard_map/ppermute | solution.py:746
  135.5 3.6 %shard_map.250 = (f32[256,1024]{1,0:T(8,128)}, bf16[256,1024]{1,0:T(8,128)(2,1)}) custom-call(s32[2]{0:T(128)} %pad_add_fusion.t, bf16[512,1024]{1,0:T(8,128)(2,1)} %get-tuple-element.63.refs_0_, bf16[512,1024]{1,0:T(8,128)(2,1)} %copy-done.14, bf16[256,1024]{1,0:T(8,128)(2,1)} %copy-done.35, bf16[256,2048]{1,0:T(8,128)(2,1)} %shard_map.247.refs_0_.refs_3_.refs_4_.refs_13_, ...), custom_call_target="tpu_custom_call" | custom-call | flops 1 | bytes 1 | tf_op jit(solution)/shard_map/pallas_call | solution.py:600
  139.5 13.0 %collective-permute-done.13.refs_2_ = bf16[256,1024]{1,0:T(8,128)(2,1)S(1)} collective-permute-done((bf16[256,1024]{1,0:T(8,128)(2,1)}, bf16[256,1024]{1,0:T(8,128)(2,1)S(1)}, u32[]{:S(2)}, u32[]{:S(2)}) %collective-permute-start.13) | collective-permute-done | bytes 524320 | tf_op jit(solution)/shard_map/ppermute | solution.py:746
  155.2 20.5 %shard_map.252 = (bf16[1024,768]{1,0:T(8,128)(2,1)}, bf16[1024,1536]{1,0:T(8,128)(2,1)}, bf16[1024,1024]{1,0:T(8,128)(2,1)}, bf16[1024,1024]{1,0:T(8,128)(2,1)},...) custom-call(s32[2]{0:T(128)} %pad_add_fusion.t, ...), custom_call_target="tpu_custom_call" | custom-call | flops 1 | bytes 1 | tf_op jit(solution)/shard_map/pallas_call | solution.py:558
  184.0 10.3 %collective-permute-done.16.refs_2_ = bf16[256,1024]{1,0:T(8,128)(2,1)S(1)} collective-permute-done((bf16[256,1024]{1,0:T(8,128)(2,1)S(1)}, bf16[256,1024]{1,0:T(8,128)(2,1)S(1)}, u32[]{:S(2)}, u32[]{:S(2)}) %collective-permute-start.16) | collective-permute-done | bytes 524320 | tf_op jit(solution)/shard_map/ppermute | solution.py:746
  195.1 4.4 %shard_map.253 = (f32[256,1024]{1,0:T(8,128)}, bf16[256,1024]{1,0:T(8,128)(2,1)}, f32[8,1024]{1,0:T(8,128)}) custom-call(s32[2]{0:T(128)} %pad_add_fusion.t, bf16[512,1024]{1,0:T(8,128)(2,1)} %get-tuple-element.71.refs_0_, bf16[512,1024]{1,0:T(8,128)(2,1)} %copy-done.11, bf16[256,1024]{1,0:T(8,128)(2,1)} %copy-done.31, ...), custom_call_target="tpu_custom_call" | custom-call | flops 1 | bytes 1 | tf_op jit(solution)/shard_map/pallas_call | solution.py:629
  199.8 7.6 %convolution_convert_fusion = bf16[1024,1536]{1,0:T(8,128)(2,1)} fusion(bf16[1024,1024]{1,0:T(8,128)(2,1)} %get-tuple-element.75, bf16[1024,1536]{1,0:T(8,128)(2,1)} %get-tuple-element.77), kind=kOutput, calls=%fused_computation | convolution fusion | flops 3222798336 | bytes 8388608 | tf_op jit(solution)/shard_map/dot_general | solution.py:24
  207.5 5.3 %collective-permute-done.18.refs_11_ = bf16[256,1024]{1,0:T(8,128)(2,1)S(1)} collective-permute-done((bf16[256,1024]{1,0:T(8,128)(2,1)}, bf16[256,1024]{1,0:T(8,128)(2,1)S(1)}, u32[]{:S(2)}, u32[]{:S(2)}) %collective-permute-start.18) | collective-permute-done | bytes 524320 | tf_op jit(solution)/shard_map/ppermute | solution.py:746
  225.0 25.9 %shard_map.255 = (bf16[1024,1024]{1,0:T(8,128)(2,1)}, f32[2,8,128]{2,1,0:T(8,128)}, bf16[512,1024]{1,0:T(8,128)(2,1)}, bf16[512,1024]{1,0:T(8,128)(2,1)}, f32[8,...) custom-call(s32[2]{0:T(128)} %pad_add_fusion.t, ...), custom_call_target="tpu_custom_call" | custom-call | flops 1 | bytes 1 | tf_op jit(solution)/shard_map/pallas_call | solution.py:452
  266.5 4.9 %collective-permute-start.31 = (bf16[128,512]{1,0:T(8,128)(2,1)S(1)}, bf16[128,512]{1,0:T(8,128)(2,1)S(1)}, u32[]{:S(2)}, u32[]{:S(2)}) collective-permute-start(bf16[128,512]{1,0:T(8,128)(2,1)S(1)} %get-tuple-element.137), channel_id=1, source_target_pairs={{0,16},{4,20},{8,24},{12,28},{16,0},{20,4},{24,8},{28,12},{1,17},{... | collective-permute-start | bytes 393224 | tf_op jit(solution)/shard_map/ppermute | solution.py:743
  274.2 4.4 %collective-permute-done.31 = bf16[128,512]{1,0:T(8,128)(2,1)S(1)} collective-permute-done((bf16[128,512]{1,0:T(8,128)(2,1)S(1)}, bf16[128,512]{1,0:T(8,128)(2,1)S(1)}, u32[]{:S(2)}, u32[]{:S(2)}) %collective-permute-start.31) | collective-permute-done | bytes 131104 | tf_op jit(solution)/shard_map/ppermute | solution.py:743
  278.6 15.7 %collective-permute-done.29.got = bf16[576,1024]{1,0:T(8,128)(2,1)S(1)} collective-permute-done((bf16[576,1024]{1,0:T(8,128)(2,1)}, bf16[576,1024]{1,0:T(8,128)(2,1)S(1)}, u32[]{:S(2)}, u32[]{:S(2)}) %collective-permute-start.29) | collective-permute-done | bytes 1179680 | tf_op jit(solution)/shard_map/ppermute | solution.py:743
  295.4 3.5 %shard_map.257 = (f32[144,1024]{1,0:T(8,128)}, bf16[144,1024]{1,0:T(8,128)(2,1)}, bf16[144,1024]{1,0:T(8,128)(2,1)}, bf16[144,1024]{1,0:T(8,128)(2,1)}) custom-call(s32[2]{0:T(128)} %pad_add_fusion.t, bf16[512,1024]{1,0:T(8,128)(2,1)} %convolution_convert_fusion.2.keep, bf16[64,1024]{1,0:T(8,128)(2,1)} %get-tuple-element.97.rows, bf16[576,1024]{1,0:T(8,128)(2,1)} %copy-done.21), custom_call_target="tpu_custom_call" | custom-call | flops 1 | bytes 1 | tf_op jit(solution)/shard_map/pallas_call | solution.py:721
  298.9 5.6 %collective-permute-start.33 = (bf16[144,1024]{1,0:T(8,128)(2,1)}, bf16[144,1024]{1,0:T(8,128)(2,1)S(1)}, u32[]{:S(2)}, u32[]{:S(2)}) collective-permute-start(bf16[144,1024]{1,0:T(8,128)(2,1)} %get-tuple-element.104), channel_id=1, source_target_pairs={{0,8},{4,12},{8,0},{12,4},{16,24},{20,28},{24,16},{28,20},{1,9},{5... | collective-permute-start | bytes 884744 | tf_op jit(solution)/shard_map/ppermute | solution.py:743
  308.3 3.5 shard_map.254
  313.6 4.3 %shard_map.256 = f32[256,1024]{1,0:T(8,128)} custom-call(s32[2]{0:T(128)} %pad_add_fusion.t, bf16[512,1024]{1,0:T(8,128)(2,1)} %get-tuple-element.92.refs_0_, bf16[512,1024]{1,0:T(8,128)(2,1)} %copy-done.13, bf16[256,1024]{1,0:T(8,128)(2,1)} %copy-done.27, bf16[256,2048]{1,0:T(8,128)(2,1)} %shard_map.247.refs_0_.refs_3_.refs_4_.refs_13_, ...), custom_call_target="tpu_custom_call" | custom-call | flops 1 | bytes 1 | tf_op jit(solution)/shard_map/pallas_call | solution.py:674
  322.2 12.5 %collective-permute-done.35 = bf16[144,1024]{1,0:T(8,128)(2,1)S(1)} collective-permute-done((bf16[144,1024]{1,0:T(8,128)(2,1)}, bf16[144,1024]{1,0:T(8,128)(2,1)S(1)}, u32[]{:S(2)}, u32[]{:S(2)}) %collective-permute-start.35) | collective-permute-done | bytes 294944 | tf_op jit(solution)/shard_map/ppermute | solution.py:743
  (198 shorter events, 89.7 us)
Async XLA Ops:
  7.2 147.3 %all-gather.2.cloned.1.call-start = ((), (), s32[]{:S(2)}) async-start(), calls=%async_computation.1 | async-start | bytes 5308416 | tf_op jit(solution)/shard_map/all_gather | solution.py:866
  13.7 31.2 %collective-permute-start.1 = (bf16[256,2048]{1,0:T(8,128)(2,1)}, bf16[256,2048]{1,0:T(8,128)(2,1)S(1)}, u32[]{:S(2)}, u32[]{:S(2)}) collective-permute-start(bf16[256,2048]{1,0:T(8,128)(2,1)} %shard_map.247.refs_0_.refs_3_.refs_4_.refs_13_), channel_id=1, source_target_pairs={{0,2},{1,3},{2,0},{3,1},{4,6},{5,7},{6,4},{7,5},{8,10},{9,11},{10,... | collective-permute-start | bytes 3145736 | tf_op jit(solution)/shard_map/ppermute | solution.py:746
  15.2 18.9 %collective-permute-start.3 = (bf16[144,1536]{1,0:T(8,128)(2,1)S(1)}, bf16[144,1536]{1,0:T(8,128)(2,1)S(1)}, u32[]{:S(2)}, u32[]{:S(2)}) collective-permute-start(bf16[144,1536]{1,0:T(8,128)(2,1)S(1)} %copy-done), channel_id=1, source_target_pairs={{0,8},{4,12},{8,0},{12,4},{16,24},{20,28},{24,16},{28,20},{1,9},{5... | collective-permute-start | bytes 1327112 | tf_op jit(solution)/shard_map/ppermute | solution.py:743
  15.6 21.8 %collective-permute-start.4 = (bf16[144,1536]{1,0:T(8,128)(2,1)S(1)}, bf16[144,1536]{1,0:T(8,128)(2,1)S(1)}, u32[]{:S(2)}, u32[]{:S(2)}) collective-permute-start(bf16[144,1536]{1,0:T(8,128)(2,1)S(1)} %copy-done), channel_id=1, source_target_pairs={{0,16},{4,20},{8,24},{12,28},{16,0},{20,4},{24,8},{28,12},{1,17},{... | collective-permute-start | bytes 1327112 | tf_op jit(solution)/shard_map/ppermute | solution.py:743
  18.2 19.2 %collective-permute-start.2 = (bf16[144,1536]{1,0:T(8,128)(2,1)S(1)}, bf16[144,1536]{1,0:T(8,128)(2,1)S(1)}, u32[]{:S(2)}, u32[]{:S(2)}) collective-permute-start(bf16[144,1536]{1,0:T(8,128)(2,1)S(1)} %copy-done), channel_id=1, source_target_pairs={{0,4},{4,0},{8,12},{12,8},{16,20},{20,16},{24,28},{28,24},{1,5},{5... | collective-permute-start | bytes 1327112 | tf_op jit(solution)/shard_map/ppermute | solution.py:743
  45.7 296.1 %reduce-scatter.2.cloned.1.call-start = ((), (), s32[]{:S(2)}) async-start(), calls=%async_computation.2 | async-start | bytes 3538944 | tf_op jit(solution)/shard_map/reduce_scatter | solution.py:905
  45.7 47.0 %collective-permute-start = (bf16[256,2048]{1,0:T(8,128)(2,1)}, bf16[256,2048]{1,0:T(8,128)(2,1)S(1)}, u32[]{:S(2)}, u32[]{:S(2)}) collective-permute-start(bf16[256,2048]{1,0:T(8,128)(2,1)} %shard_map.247.refs_0_.refs_3_.refs_4_.refs_13_), channel_id=1, source_target_pairs={{0,1},{1,0},{2,3},{3,2},{4,5},{5,4},{6,7},{7,6},{8,9},{9,8},{10,11... | collective-permute-start | bytes 3145736 | tf_op jit(solution)/shard_map/ppermute | solution.py:746
  45.7 47.0 %collective-permute-start.5 = (bf16[256,2048]{1,0:T(8,128)(2,1)S(1)}, bf16[256,2048]{1,0:T(8,128)(2,1)}, u32[]{:S(2)}, u32[]{:S(2)}) collective-permute-start(bf16[256,2048]{1,0:T(8,128)(2,1)S(1)} %collective-permute-done.1.refs_2_.refs_6_.refs_15_), channel_id=1, source_target_pairs={{0,1},{1,0},{2,3},{3,2},{4,5},{5,4},{6,7},{7,6},{8,9},{9,8},{10,11... | collective-permute-start | bytes 3145736 | tf_op jit(solution)/shard_map/ppermute | solution.py:746
  46.2 38.0 %collective-permute-start.6 = (bf16[144,1536]{1,0:T(8,128)(2,1)S(1)}, bf16[144,1536]{1,0:T(8,128)(2,1)}, u32[]{:S(2)}, u32[]{:S(2)}) collective-permute-start(bf16[144,1536]{1,0:T(8,128)(2,1)S(1)} %copy-done), channel_id=1, source_target_pairs={{0,24},{4,28},{8,16},{12,20},{16,8},{20,12},{24,0},{28,4},{1,25},{... | collective-permute-start | bytes 1327112 | tf_op jit(solution)/shard_map/ppermute | solution.py:743
  48.0 44.7 %collective-permute-start.8 = (bf16[144,1536]{1,0:T(8,128)(2,1)S(1)}, bf16[144,1536]{1,0:T(8,128)(2,1)}, u32[]{:S(2)}, u32[]{:S(2)}) collective-permute-start(bf16[144,1536]{1,0:T(8,128)(2,1)S(1)} %collective-permute-done.4.refs_6_.refs_2_.refs_19_.refs_27_), channel_id=1, source_target_pairs={{0,4},{4,0},{8,12},{12,8},{16,20},{20,16},{24,28},{28,24},{1,5},{5... | collective-permute-start | bytes 1327112 | tf_op jit(solution)/shard_map/ppermute | solution.py:743
  120.6 14.0 %collective-permute-start.11 = (bf16[256,1024]{1,0:T(8,128)(2,1)S(1)}, bf16[256,1024]{1,0:T(8,128)(2,1)S(1)}, u32[]{:S(2)}, u32[]{:S(2)}) collective-permute-start(bf16[256,1024]{1,0:T(8,128)(2,1)S(1)} %add_convert_fusion.3), channel_id=1, source_target_pairs={{0,2},{1,3},{2,0},{3,1},{4,6},{5,7},{6,4},{7,5},{8,10},{9,11},{10,... | collective-permute-start | bytes 1572872 | tf_op jit(solution)/shard_map/ppermute | solution.py:746
  139.1 13.4 %collective-permute-start.13 = (bf16[256,1024]{1,0:T(8,128)(2,1)}, bf16[256,1024]{1,0:T(8,128)(2,1)S(1)}, u32[]{:S(2)}, u32[]{:S(2)}) collective-permute-start(bf16[256,1024]{1,0:T(8,128)(2,1)} %get-tuple-element.66.refs_0_), channel_id=1, source_target_pairs={{0,2},{1,3},{2,0},{3,1},{4,6},{5,7},{6,4},{7,5},{8,10},{9,11},{10,... | collective-permute-start | bytes 1572872 | tf_op jit(solution)/shard_map/ppermute | solution.py:746
  180.2 14.0 %collective-permute-start.16 = (bf16[256,1024]{1,0:T(8,128)(2,1)S(1)}, bf16[256,1024]{1,0:T(8,128)(2,1)S(1)}, u32[]{:S(2)}, u32[]{:S(2)}) collective-permute-start(bf16[256,1024]{1,0:T(8,128)(2,1)S(1)} %add_convert_fusion.2), channel_id=1, source_target_pairs={{0,2},{1,3},{2,0},{3,1},{4,6},{5,7},{6,4},{7,5},{8,10},{9,11},{10,... | collective-permute-start | bytes 1572872 | tf_op jit(solution)/shard_map/ppermute | solution.py:746
  183.5 24.0 %collective-permute-start.19 = (bf16[512,768]{1,0:T(8,128)(2,1)S(1)}, bf16[512,768]{1,0:T(8,128)(2,1)S(1)}, u32[]{:S(2)}, u32[]{:S(2)}) collective-permute-start(bf16[512,768]{1,0:T(8,128)(2,1)S(1)} %convolution_convert_fusion.4), channel_id=1, source_target_pairs={{0,4},{4,0},{8,12},{12,8},{16,20},{20,16},{24,28},{28,24},{1,5},{5... | collective-permute-start | bytes 2359304 | tf_op jit(solution)/shard_map/ppermute | solution.py:743
  217.7 35.3 %collective-permute-start.23 = (bf16[512,512]{1,0:T(8,128)(2,1)}, bf16[512,512]{1,0:T(8,128)(2,1)S(1)}, u32[]{:S(2)}, u32[]{:S(2)}) collective-permute-start(bf16[512,512]{1,0:T(8,128)(2,1)} %convolution_convert_fusion.6), channel_id=1, source_target_pairs={{0,4},{4,0},{8,12},{12,8},{16,20},{20,16},{24,28},{28,24},{1,5},{5... | collective-permute-start | bytes 1572872 | tf_op jit(solution)/shard_map/ppermute | solution.py:743
  218.4 34.6 %collective-permute-start.22 = (bf16[256,1024]{1,0:T(8,128)(2,1)S(1)}, bf16[256,1024]{1,0:T(8,128)(2,1)S(1)}, u32[]{:S(2)}, u32[]{:S(2)}) collective-permute-start(bf16[256,1024]{1,0:T(8,128)(2,1)S(1)} %add_convert_fusion.1), channel_id=1, source_target_pairs={{0,2},{1,3},{2,0},{3,1},{4,6},{5,7},{6,4},{7,5},{8,10},{9,11},{10,... | collective-permute-start | bytes 1572872 | tf_op jit(solution)/shard_map/ppermute | solution.py:746
  220.8 30.1 %collective-permute-start.26 = (bf16[128,768]{1,0:T(8,128)(2,1)}, bf16[128,768]{1,0:T(8,128)(2,1)}, u32[]{:S(2)}, u32[]{:S(2)}) collective-permute-start(bf16[128,768]{1,0:T(8,128)(2,1)} %get-tuple-element.133), channel_id=1, source_target_pairs={{0,24},{4,28},{8,16},{12,20},{16,8},{20,12},{24,0},{28,4},{1,25},{... | collective-permute-start | bytes 589832 | tf_op jit(solution)/shard_map/ppermute | solution.py:743
  223.6 29.4 %collective-permute-start.25 = (bf16[128,768]{1,0:T(8,128)(2,1)S(1)}, bf16[128,768]{1,0:T(8,128)(2,1)}, u32[]{:S(2)}, u32[]{:S(2)}) collective-permute-start(bf16[128,768]{1,0:T(8,128)(2,1)S(1)} %get-tuple-element.134), channel_id=1, source_target_pairs={{0,16},{4,20},{8,24},{12,28},{16,0},{20,4},{24,8},{28,12},{1,17},{... | collective-permute-start | bytes 589832 | tf_op jit(solution)/shard_map/ppermute | solution.py:743
  223.6 29.4 %collective-permute-start.24 = (bf16[128,768]{1,0:T(8,128)(2,1)S(1)}, bf16[128,768]{1,0:T(8,128)(2,1)}, u32[]{:S(2)}, u32[]{:S(2)}) collective-permute-start(bf16[128,768]{1,0:T(8,128)(2,1)S(1)} %get-tuple-element.135), channel_id=1, source_target_pairs={{0,8},{4,12},{8,0},{12,4},{16,24},{20,28},{24,16},{28,20},{1,9},{5... | collective-permute-start | bytes 589832 | tf_op jit(solution)/shard_map/ppermute | solution.py:743
  257.9 36.5 %collective-permute-start.29 = (bf16[576,1024]{1,0:T(8,128)(2,1)}, bf16[576,1024]{1,0:T(8,128)(2,1)S(1)}, u32[]{:S(2)}, u32[]{:S(2)}) collective-permute-start(bf16[576,1024]{1,0:T(8,128)(2,1)} %pad_maximum_fusion), channel_id=1, source_target_pairs={{0,4},{4,0},{8,12},{12,8},{16,20},{20,16},{24,28},{28,24},{1,5},{5... | collective-permute-start | bytes 3538952 | tf_op jit(solution)/shard_map/ppermute | solution.py:743
  262.3 32.1 %collective-permute-start.28 = (bf16[256,1024]{1,0:T(8,128)(2,1)S(1)}, bf16[256,1024]{1,0:T(8,128)(2,1)S(1)}, u32[]{:S(2)}, u32[]{:S(2)}) collective-permute-start(bf16[256,1024]{1,0:T(8,128)(2,1)S(1)} %add_convert_fusion), channel_id=1, source_target_pairs={{0,2},{1,3},{2,0},{3,1},{4,6},{5,7},{6,4},{7,5},{8,10},{9,11},{10,... | collective-permute-start | bytes 1572872 | tf_op jit(solution)/shard_map/ppermute | solution.py:746
  298.9 20.2 %collective-permute-start.33 = (bf16[144,1024]{1,0:T(8,128)(2,1)}, bf16[144,1024]{1,0:T(8,128)(2,1)S(1)}, u32[]{:S(2)}, u32[]{:S(2)}) collective-permute-start(bf16[144,1024]{1,0:T(8,128)(2,1)} %get-tuple-element.104), channel_id=1, source_target_pairs={{0,8},{4,12},{8,0},{12,4},{16,24},{20,28},{24,16},{28,20},{1,9},{5... | collective-permute-start | bytes 884744 | tf_op jit(solution)/shard_map/ppermute | solution.py:743
  304.5 17.7 %collective-permute-start.34 = (bf16[144,1024]{1,0:T(8,128)(2,1)}, bf16[144,1024]{1,0:T(8,128)(2,1)S(1)}, u32[]{:S(2)}, u32[]{:S(2)}) collective-permute-start(bf16[144,1024]{1,0:T(8,128)(2,1)} %get-tuple-element.105), channel_id=1, source_target_pairs={{0,16},{4,20},{8,24},{12,28},{16,0},{20,4},{24,8},{28,12},{1,17},{... | collective-permute-start | bytes 884744 | tf_op jit(solution)/shard_map/ppermute | solution.py:743
  304.5 30.3 %collective-permute-start.35 = (bf16[144,1024]{1,0:T(8,128)(2,1)}, bf16[144,1024]{1,0:T(8,128)(2,1)S(1)}, u32[]{:S(2)}, u32[]{:S(2)}) collective-permute-start(bf16[144,1024]{1,0:T(8,128)(2,1)} %get-tuple-element.106), channel_id=1, source_target_pairs={{0,24},{4,28},{8,16},{12,20},{16,8},{20,12},{24,0},{28,4},{1,25},{... | collective-permute-start | bytes 884744 | tf_op jit(solution)/shard_map/ppermute | solution.py:743
  (59 other events, 599.7 us)
Sparse Core Ops, SparseCore 0:
  45.0 89.6 all-gather.1
  215.0 100.5 reduce-scatter.1

commit v4 on v3

--- a/solution.py
+++ b/solution.py
@@ -861,7 +861,7 @@
         across = tie(far, attn_far, attn_near[1], attn_near[2])
         rows_all = [both, beside, far, links.over_tensor(across, 1)]
         w_attn = attn_near + [attn_far] + [links.over_dp(b, 1) for b in attn_near[1:]]
-        w_mlp = tie(w_mlp, (far, attn_far, attn_near[1], attn_near[2], w_attn[5]))
+        w_mlp = tie(w_mlp, (far, attn_far, attn_near[1:], w_attn[5], w_attn[6]))
         w_qkv, w_o, o_index = w_attn, w_attn, kv_heads * (group + 2) * HEAD // q_cols
         w_gu = w_d = lax.all_gather(w_mlp, "dp", axis=0, tiled=True)
         d_index = 2

time: 355 us -> 343 us (0.966)
  waiting for transfers between devices: 155 us -> 145 us
    ppermute x19, waiting for transfers between devices: 102 us -> 91 us  [over_dp(): return lax.ppermute(x, 'dp', xor_pairs(self.dp, bits))]
    unnamed x91 -> x89, local copies, waits for them, and re-layouts: 8.42 us -> 6.78 us
  transfers between devices with their start and end apart: 40 -> 40, of which waited for: 20 -> 23; matrix products, arithmetic and copies ran while one was open for 11% -> 11% of each run, Pallas kernels for 20% -> 21%
where the time goes in v4:
time: 343 us; the launch traced here: 339 us
  waiting for transfers between devices  145 us (42%)
  Pallas kernels  96.6 us (28%)
  starting transfers between devices  35.6 us (10%)
  matrix products  20.9 us (6%)
  other arithmetic  16.1 us (5%)
  between operations  14.8 us (4%)
  local copies, waits for them, and re-layouts  10.2 us (3%)
    ppermute x19, waiting for transfers between devices, over_dp(): return lax.ppermute(x, 'dp', xor_pairs(self.dp, bits))  91 us
    ppermute x19, waiting for transfers between devices, over_tensor(): return lax.ppermute(x, 'tensor', xor_pairs(self.tensor, bits))  50.9 us
    ppermute x19, starting transfers between devices, over_dp(): return lax.ppermute(x, 'dp', xor_pairs(self.dp, bits))  26.2 us
    pallas_call x1, Pallas kernels, attn_backward(): call(functools.partial(attn_backward_kernel, rows, n // rows, group, kv_h...  25.9 us
    dot_general x7, matrix products, mm(): lax.dot_general(a, b, (((ca,), (cb,)), ((), ())), preferred_element_type=...  20.9 us
    pallas_call x1, Pallas kernels, mlp_call(): call(functools.partial(mlp_kernel, ff, len(xs), reorder), (len(xs),), [wh...  20.5 us
    pallas_call x1, Pallas kernels, attn_forward(): call(functools.partial(attn_forward_kernel, rows, n // rows, group, kv_he...  12.7 us
    pallas_call x1, Pallas kernels, qkv_call(): call(functools.partial(qkv_kernel, len(xs), len(ws), packed_gains, kv_hea...  9.61 us
  transfers between devices with their start and end apart: 40, of which 23 were waited for; matrix products, arithmetic and copies ran while one was open for 11% of the time, Pallas kernels for 21%

profile of v4, /device:TPU:12, one launch (start us, length us, event | category | flops | bytes accessed | tf_op | source)
XLA Modules:
  0.0 339.0 jit_solution(11420843755295560619)
XLA Ops:
  10.4 3.3 shard_map.247.refs_0_.refs_3_.refs_4_.refs_13_
  19.2 18.4 %collective-permute-done.4.refs_6_.refs_2_.refs_19_.refs_27_ = bf16[144,1536]{1,0:T(8,128)(2,1)S(1)} collective-permute-done((bf16[144,1536]{1,0:T(8,128)(2,1)S(1)}, bf16[144,1536]{1,0:T(8,128)(2,1)S(1)}, u32[]{:S(2)}, u32[]{:S(2)}) %collective-permute-start.4) | collective-permute-done | bytes 442400 | tf_op jit(solution)/shard_map/ppermute | solution.py:743
  42.3 13.0 %collective-permute-done.6.refs_7_.refs_3_.refs_20_.refs_28_ = bf16[144,1536]{1,0:T(8,128)(2,1)S(1)} collective-permute-done((bf16[144,1536]{1,0:T(8,128)(2,1)S(1)}, bf16[144,1536]{1,0:T(8,128)(2,1)S(1)}, u32[]{:S(2)}, u32[]{:S(2)}) %collective-permute-start.6) | collective-permute-done | bytes 442400 | tf_op jit(solution)/shard_map/ppermute | solution.py:743
  55.3 3.5 %collective-permute-done.7.refs_9_.refs_5_.refs_22_.refs_30_ = bf16[144,1536]{1,0:T(8,128)(2,1)} collective-permute-done((bf16[144,1536]{1,0:T(8,128)(2,1)S(1)}, bf16[144,1536]{1,0:T(8,128)(2,1)}, u32[]{:S(2)}, u32[]{:S(2)}) %collective-permute-start.7) | collective-permute-done | bytes 442400 | tf_op jit(solution)/shard_map/ppermute | solution.py:743
  64.2 9.6 %collective-permute-done.9.refs_11_.refs_7_.refs_24_.refs_32_ = bf16[144,1536]{1,0:T(8,128)(2,1)} collective-permute-done((bf16[144,1536]{1,0:T(8,128)(2,1)S(1)}, bf16[144,1536]{1,0:T(8,128)(2,1)}, u32[]{:S(2)}, u32[]{:S(2)}) %collective-permute-start.9) | collective-permute-done | bytes 442400 | tf_op jit(solution)/shard_map/ppermute | solution.py:743
  74.8 9.6 %shard_map.248 = (bf16[1024,1024]{1,0:T(8,128)(2,1)}, bf16[1024,1024]{1,0:T(8,128)(2,1)}, f32[1024,768]{1,0:T(8,128)}, f32[8,1024]{1,0:T(8,128)}) custom-call(s32[2]{0:T(128)} %pad_add_fusion.t, bf16[256,2048]{1,0:T(8,128)(2,1)} %shard_map.247.refs_0_.refs_3_.refs_4_.refs_13_, bf16[256,2048]{1,0:T(8,128)(2,1)} %copy-done.2, bf16[256,2048]{1,0:T(8,128)(2,1)} %copy-done.1, ...), custom_call_target="tpu_custom_call" | custom-call | flops 1 | bytes 1 | tf_op jit(solution)/shard_map/pallas_call | solution.py:210
  84.4 12.7 %shard_map.249 = (bf16[1024,512]{1,0:T(8,128)(2,1)}, f32[2,8,1024]{2,1,0:T(8,128)}, bf16[512,1024]{1,0:T(8,128)(2,1)}, bf16[512,1024]{1,0:T(8,128)(2,1)}) custom-call(s32[2]{0:T(128)} %pad_add_fusion.t, bf16[1024,1024]{1,0:T(8,128)(2,1)} %get-tuple-element.62.packed.refs_0_, s32[1024,1]{1,0:T(8,128)} %copy.30.seg_col.refs_1_, s32[1,1024]{1,0:T(1,128)} %refs_2_.1, ...), custom_call_target="tpu_custom_call" | custom-call | flops 1 | bytes 1 | tf_op jit(solution)/shard_map/pallas_call | solution.py:296
  101.8 14.0 %collective-permute-done.11.refs_2_ = bf16[256,1024]{1,0:T(8,128)(2,1)S(1)} collective-permute-done((bf16[256,1024]{1,0:T(8,128)(2,1)S(1)}, bf16[256,1024]{1,0:T(8,128)(2,1)S(1)}, u32[]{:S(2)}, u32[]{:S(2)}) %collective-permute-start.11) | collective-permute-done | bytes 524320 | tf_op jit(solution)/shard_map/ppermute | solution.py:746
  116.5 3.7 %shard_map.250 = (f32[256,1024]{1,0:T(8,128)}, bf16[256,1024]{1,0:T(8,128)(2,1)}) custom-call(s32[2]{0:T(128)} %pad_add_fusion.t, bf16[512,1024]{1,0:T(8,128)(2,1)} %get-tuple-element.63.refs_0_, bf16[512,1024]{1,0:T(8,128)(2,1)} %copy-done.13, bf16[256,1024]{1,0:T(8,128)(2,1)} %copy-done.34, bf16[256,2048]{1,0:T(8,128)(2,1)} %shard_map.247.refs_0_.refs_3_.refs_4_.refs_13_, ...), custom_call_target="tpu_custom_call" | custom-call | flops 1 | bytes 1 | tf_op jit(solution)/shard_map/pallas_call | solution.py:600
  120.4 13.2 %collective-permute-done.13.refs_2_ = bf16[256,1024]{1,0:T(8,128)(2,1)S(1)} collective-permute-done((bf16[256,1024]{1,0:T(8,128)(2,1)}, bf16[256,1024]{1,0:T(8,128)(2,1)S(1)}, u32[]{:S(2)}, u32[]{:S(2)}) %collective-permute-start.13) | collective-permute-done | bytes 524320 | tf_op jit(solution)/shard_map/ppermute | solution.py:746
  138.3 20.5 %shard_map.252 = (bf16[1024,768]{1,0:T(8,128)(2,1)}, bf16[1024,1536]{1,0:T(8,128)(2,1)}, bf16[1024,1024]{1,0:T(8,128)(2,1)}, bf16[1024,1024]{1,0:T(8,128)(2,1)},...) custom-call(s32[2]{0:T(128)} %pad_add_fusion.t, ...), custom_call_target="tpu_custom_call" | custom-call | flops 1 | bytes 1 | tf_op jit(solution)/shard_map/pallas_call | solution.py:558
  169.3 8.0 %collective-permute-done.16.refs_2_ = bf16[256,1024]{1,0:T(8,128)(2,1)S(1)} collective-permute-done((bf16[256,1024]{1,0:T(8,128)(2,1)S(1)}, bf16[256,1024]{1,0:T(8,128)(2,1)S(1)}, u32[]{:S(2)}, u32[]{:S(2)}) %collective-permute-start.16) | collective-permute-done | bytes 524320 | tf_op jit(solution)/shard_map/ppermute | solution.py:746
  178.1 4.4 %shard_map.253 = (f32[256,1024]{1,0:T(8,128)}, bf16[256,1024]{1,0:T(8,128)(2,1)}, f32[8,1024]{1,0:T(8,128)}) custom-call(s32[2]{0:T(128)} %pad_add_fusion.t, bf16[512,1024]{1,0:T(8,128)(2,1)} %get-tuple-element.71.refs_0_, bf16[512,1024]{1,0:T(8,128)(2,1)} %copy-done.10, bf16[256,1024]{1,0:T(8,128)(2,1)} %copy-done.30, ...), custom_call_target="tpu_custom_call" | custom-call | flops 1 | bytes 1 | tf_op jit(solution)/shard_map/pallas_call | solution.py:629
  183.9 7.6 %convolution_convert_fusion = bf16[1024,1536]{1,0:T(8,128)(2,1)} fusion(bf16[1024,1024]{1,0:T(8,128)(2,1)} %get-tuple-element.75, bf16[1024,1536]{1,0:T(8,128)(2,1)} %get-tuple-element.77), kind=kOutput, calls=%fused_computation | convolution fusion | flops 3222798336 | bytes 8388608 | tf_op jit(solution)/shard_map/dot_general | solution.py:24
  191.6 4.2 %collective-permute-done.18.refs_11_ = bf16[256,1024]{1,0:T(8,128)(2,1)S(1)} collective-permute-done((bf16[256,1024]{1,0:T(8,128)(2,1)}, bf16[256,1024]{1,0:T(8,128)(2,1)S(1)}, u32[]{:S(2)}, u32[]{:S(2)}) %collective-permute-start.18) | collective-permute-done | bytes 524320 | tf_op jit(solution)/shard_map/ppermute | solution.py:746
  209.6 25.9 %shard_map.255 = (bf16[1024,1024]{1,0:T(8,128)(2,1)}, f32[2,8,128]{2,1,0:T(8,128)}, bf16[512,1024]{1,0:T(8,128)(2,1)}, bf16[512,1024]{1,0:T(8,128)(2,1)}, f32[8,...) custom-call(s32[2]{0:T(128)} %pad_add_fusion.t, ...), custom_call_target="tpu_custom_call" | custom-call | flops 1 | bytes 1 | tf_op jit(solution)/shard_map/pallas_call | solution.py:452
  235.5 5.7 %collective-permute-done.25 = bf16[128,768]{1,0:T(8,128)(2,1)} collective-permute-done((bf16[128,768]{1,0:T(8,128)(2,1)S(1)}, bf16[128,768]{1,0:T(8,128)(2,1)}, u32[]{:S(2)}, u32[]{:S(2)}) %collective-permute-start.25) | collective-permute-done | bytes 196640 | tf_op jit(solution)/shard_map/ppermute | solution.py:743
  252.8 4.8 %collective-permute-start.31 = (bf16[128,512]{1,0:T(8,128)(2,1)S(1)}, bf16[128,512]{1,0:T(8,128)(2,1)S(1)}, u32[]{:S(2)}, u32[]{:S(2)}) collective-permute-start(bf16[128,512]{1,0:T(8,128)(2,1)S(1)} %get-tuple-element.137), channel_id=1, source_target_pairs={{0,16},{4,20},{8,24},{12,28},{16,0},{20,4},{24,8},{28,12},{1,17},{... | collective-permute-start | bytes 393224 | tf_op jit(solution)/shard_map/ppermute | solution.py:743
  264.9 17.7 %collective-permute-done.29.got = bf16[576,1024]{1,0:T(8,128)(2,1)S(1)} collective-permute-done((bf16[576,1024]{1,0:T(8,128)(2,1)}, bf16[576,1024]{1,0:T(8,128)(2,1)S(1)}, u32[]{:S(2)}, u32[]{:S(2)}) %collective-permute-start.29) | collective-permute-done | bytes 1179680 | tf_op jit(solution)/shard_map/ppermute | solution.py:743
  283.6 3.5 %shard_map.257 = (f32[144,1024]{1,0:T(8,128)}, bf16[144,1024]{1,0:T(8,128)(2,1)}, bf16[144,1024]{1,0:T(8,128)(2,1)}, bf16[144,1024]{1,0:T(8,128)(2,1)}) custom-call(s32[2]{0:T(128)} %pad_add_fusion.t, bf16[512,1024]{1,0:T(8,128)(2,1)} %convolution_convert_fusion.2.keep, bf16[64,1024]{1,0:T(8,128)(2,1)} %get-tuple-element.97.rows, bf16[576,1024]{1,0:T(8,128)(2,1)} %copy-done.20), custom_call_target="tpu_custom_call" | custom-call | flops 1 | bytes 1 | tf_op jit(solution)/shard_map/pallas_call | solution.py:721
  287.1 5.0 %collective-permute-start.33 = (bf16[144,1024]{1,0:T(8,128)(2,1)}, bf16[144,1024]{1,0:T(8,128)(2,1)S(1)}, u32[]{:S(2)}, u32[]{:S(2)}) collective-permute-start(bf16[144,1024]{1,0:T(8,128)(2,1)} %get-tuple-element.104), channel_id=1, source_target_pairs={{0,8},{4,12},{8,0},{12,4},{16,24},{20,28},{24,16},{28,20},{1,9},{5... | collective-permute-start | bytes 884744 | tf_op jit(solution)/shard_map/ppermute | solution.py:743
  295.9 3.5 %shard_map.254 = bf16[256,1024]{1,0:T(8,128)(2,1)} custom-call(s32[2]{0:T(128)} %pad_add_fusion.t, bf16[512,1024]{1,0:T(8,128)(2,1)} %get-tuple-element.69.refs_0_, bf16[512,1024]{1,0:T(8,128)(2,1)} %copy-done.9, bf16[256,1024]{1,0:T(8,128)(2,1)} %copy-done.25, f32[256,1024]{1,0:T(8,128)} %get-tuple-element.73.refs_3_), custom_call_target="tpu_custom_call" | custom-call | flops 1 | bytes 1 | tf_op jit(solution)/shard_map/pallas_call | solution.py:655
  301.2 4.3 %shard_map.256 = f32[256,1024]{1,0:T(8,128)} custom-call(s32[2]{0:T(128)} %pad_add_fusion.t, bf16[512,1024]{1,0:T(8,128)(2,1)} %get-tuple-element.92.refs_0_, bf16[512,1024]{1,0:T(8,128)(2,1)} %copy-done.12, bf16[256,1024]{1,0:T(8,128)(2,1)} %copy-done.26, bf16[256,2048]{1,0:T(8,128)(2,1)} %shard_map.247.refs_0_.refs_3_.refs_4_.refs_13_, ...), custom_call_target="tpu_custom_call" | custom-call | flops 1 | bytes 1 | tf_op jit(solution)/shard_map/pallas_call | solution.py:674
  310.6 12.4 %collective-permute-done.35 = bf16[144,1024]{1,0:T(8,128)(2,1)S(1)} collective-permute-done((bf16[144,1024]{1,0:T(8,128)(2,1)}, bf16[144,1024]{1,0:T(8,128)(2,1)S(1)}, u32[]{:S(2)}, u32[]{:S(2)}) %collective-permute-start.35) | collective-permute-done | bytes 294944 | tf_op jit(solution)/shard_map/ppermute | solution.py:743
  (196 shorter events, 96.1 us)
Async XLA Ops:
  7.2 131.1 %all-gather.2.cloned.1.call-start = ((), (), s32[]{:S(2)}) async-start(), calls=%async_computation.1 | async-start | bytes 5308416 | tf_op jit(solution)/shard_map/all_gather | solution.py:866
  13.7 45.1 %collective-permute-start.1 = (bf16[256,2048]{1,0:T(8,128)(2,1)}, bf16[256,2048]{1,0:T(8,128)(2,1)S(1)}, u32[]{:S(2)}, u32[]{:S(2)}) collective-permute-start(bf16[256,2048]{1,0:T(8,128)(2,1)} %shard_map.247.refs_0_.refs_3_.refs_4_.refs_13_), channel_id=1, source_target_pairs={{0,2},{1,3},{2,0},{3,1},{4,6},{5,7},{6,4},{7,5},{8,10},{9,11},{10,... | collective-permute-start | bytes 3145736 | tf_op jit(solution)/shard_map/ppermute | solution.py:746
  15.2 22.3 %collective-permute-start.4 = (bf16[144,1536]{1,0:T(8,128)(2,1)S(1)}, bf16[144,1536]{1,0:T(8,128)(2,1)S(1)}, u32[]{:S(2)}, u32[]{:S(2)}) collective-permute-start(bf16[144,1536]{1,0:T(8,128)(2,1)S(1)} %copy-done), channel_id=1, source_target_pairs={{0,16},{4,20},{8,24},{12,28},{16,0},{20,4},{24,8},{28,12},{1,17},{... | collective-permute-start | bytes 1327112 | tf_op jit(solution)/shard_map/ppermute | solution.py:743
  17.8 21.0 %collective-permute-start.3 = (bf16[144,1536]{1,0:T(8,128)(2,1)S(1)}, bf16[144,1536]{1,0:T(8,128)(2,1)S(1)}, u32[]{:S(2)}, u32[]{:S(2)}) collective-permute-start(bf16[144,1536]{1,0:T(8,128)(2,1)S(1)} %copy-done), channel_id=1, source_target_pairs={{0,8},{4,12},{8,0},{12,4},{16,24},{20,28},{24,16},{28,20},{1,9},{5... | collective-permute-start | bytes 1327112 | tf_op jit(solution)/shard_map/ppermute | solution.py:743
  18.2 37.0 %collective-permute-start.6 = (bf16[144,1536]{1,0:T(8,128)(2,1)S(1)}, bf16[144,1536]{1,0:T(8,128)(2,1)S(1)}, u32[]{:S(2)}, u32[]{:S(2)}) collective-permute-start(bf16[144,1536]{1,0:T(8,128)(2,1)S(1)} %copy-done), channel_id=1, source_target_pairs={{0,24},{4,28},{8,16},{12,20},{16,8},{20,12},{24,0},{28,4},{1,25},{... | collective-permute-start | bytes 1327112 | tf_op jit(solution)/shard_map/ppermute | solution.py:743
  18.7 36.6 %collective-permute-start.2 = (bf16[144,1536]{1,0:T(8,128)(2,1)S(1)}, bf16[144,1536]{1,0:T(8,128)(2,1)S(1)}, u32[]{:S(2)}, u32[]{:S(2)}) collective-permute-start(bf16[144,1536]{1,0:T(8,128)(2,1)S(1)} %copy-done), channel_id=1, source_target_pairs={{0,4},{4,0},{8,12},{12,8},{16,20},{20,16},{24,28},{28,24},{1,5},{5... | collective-permute-start | bytes 1327112 | tf_op jit(solution)/shard_map/ppermute | solution.py:743
  37.5 17.7 %collective-permute-start.8 = (bf16[144,1536]{1,0:T(8,128)(2,1)S(1)}, bf16[144,1536]{1,0:T(8,128)(2,1)}, u32[]{:S(2)}, u32[]{:S(2)}) collective-permute-start(bf16[144,1536]{1,0:T(8,128)(2,1)S(1)} %collective-permute-done.4.refs_6_.refs_2_.refs_19_.refs_27_), channel_id=1, source_target_pairs={{0,4},{4,0},{8,12},{12,8},{16,20},{20,16},{24,28},{28,24},{1,5},{5... | collective-permute-start | bytes 1327112 | tf_op jit(solution)/shard_map/ppermute | solution.py:743
  38.8 20.0 %collective-permute-start.7 = (bf16[144,1536]{1,0:T(8,128)(2,1)S(1)}, bf16[144,1536]{1,0:T(8,128)(2,1)}, u32[]{:S(2)}, u32[]{:S(2)}) collective-permute-start(bf16[144,1536]{1,0:T(8,128)(2,1)S(1)} %collective-permute-done.3.refs_5_.refs_1_.refs_18_.refs_26_), channel_id=1, source_target_pairs={{0,4},{4,0},{8,12},{12,8},{16,20},{20,16},{24,28},{28,24},{1,5},{5... | collective-permute-start | bytes 1327112 | tf_op jit(solution)/shard_map/ppermute | solution.py:743
  58.8 271.2 %reduce-scatter.2.cloned.1.call-start = ((), (), s32[]{:S(2)}) async-start(), calls=%async_computation.2 | async-start | bytes 3538944 | tf_op jit(solution)/shard_map/reduce_scatter | solution.py:905
  58.8 15.0 %collective-permute-start = (bf16[256,2048]{1,0:T(8,128)(2,1)}, bf16[256,2048]{1,0:T(8,128)(2,1)S(1)}, u32[]{:S(2)}, u32[]{:S(2)}) collective-permute-start(bf16[256,2048]{1,0:T(8,128)(2,1)} %shard_map.247.refs_0_.refs_3_.refs_4_.refs_13_), channel_id=1, source_target_pairs={{0,1},{1,0},{2,3},{3,2},{4,5},{5,4},{6,7},{7,6},{8,9},{9,8},{10,11... | collective-permute-start | bytes 3145736 | tf_op jit(solution)/shard_map/ppermute | solution.py:746
  58.9 14.9 %collective-permute-start.5 = (bf16[256,2048]{1,0:T(8,128)(2,1)S(1)}, bf16[256,2048]{1,0:T(8,128)(2,1)}, u32[]{:S(2)}, u32[]{:S(2)}) collective-permute-start(bf16[256,2048]{1,0:T(8,128)(2,1)S(1)} %collective-permute-done.1.refs_2_.refs_6_.refs_15_), channel_id=1, source_target_pairs={{0,1},{1,0},{2,3},{3,2},{4,5},{5,4},{6,7},{7,6},{8,9},{9,8},{10,11... | collective-permute-start | bytes 3145736 | tf_op jit(solution)/shard_map/ppermute | solution.py:746
  59.4 14.4 %collective-permute-start.9 = (bf16[144,1536]{1,0:T(8,128)(2,1)S(1)}, bf16[144,1536]{1,0:T(8,128)(2,1)}, u32[]{:S(2)}, u32[]{:S(2)}) collective-permute-start(bf16[144,1536]{1,0:T(8,128)(2,1)S(1)} %collective-permute-done.6.refs_7_.refs_3_.refs_20_.refs_28_), channel_id=1, source_target_pairs={{0,4},{4,0},{8,12},{12,8},{16,20},{20,16},{24,28},{28,24},{1,5},{5... | collective-permute-start | bytes 1327112 | tf_op jit(solution)/shard_map/ppermute | solution.py:743
  101.7 14.0 %collective-permute-start.11 = (bf16[256,1024]{1,0:T(8,128)(2,1)S(1)}, bf16[256,1024]{1,0:T(8,128)(2,1)S(1)}, u32[]{:S(2)}, u32[]{:S(2)}) collective-permute-start(bf16[256,1024]{1,0:T(8,128)(2,1)S(1)} %add_convert_fusion.3), channel_id=1, source_target_pairs={{0,2},{1,3},{2,0},{3,1},{4,6},{5,7},{6,4},{7,5},{8,10},{9,11},{10,... | collective-permute-start | bytes 1572872 | tf_op jit(solution)/shard_map/ppermute | solution.py:746
  167.6 24.0 %collective-permute-start.19 = (bf16[512,768]{1,0:T(8,128)(2,1)S(1)}, bf16[512,768]{1,0:T(8,128)(2,1)S(1)}, u32[]{:S(2)}, u32[]{:S(2)}) collective-permute-start(bf16[512,768]{1,0:T(8,128)(2,1)S(1)} %convolution_convert_fusion.4), channel_id=1, source_target_pairs={{0,4},{4,0},{8,12},{12,8},{16,20},{20,16},{24,28},{28,24},{1,5},{5... | collective-permute-start | bytes 2359304 | tf_op jit(solution)/shard_map/ppermute | solution.py:743
  200.7 40.5 %collective-permute-start.23 = (bf16[512,512]{1,0:T(8,128)(2,1)}, bf16[512,512]{1,0:T(8,128)(2,1)S(1)}, u32[]{:S(2)}, u32[]{:S(2)}) collective-permute-start(bf16[512,512]{1,0:T(8,128)(2,1)} %convolution_convert_fusion.6), channel_id=1, source_target_pairs={{0,4},{4,0},{8,12},{12,8},{16,20},{20,16},{24,28},{28,24},{1,5},{5... | collective-permute-start | bytes 1572872 | tf_op jit(solution)/shard_map/ppermute | solution.py:743
  202.4 38.8 %collective-permute-start.22 = (bf16[256,1024]{1,0:T(8,128)(2,1)S(1)}, bf16[256,1024]{1,0:T(8,128)(2,1)S(1)}, u32[]{:S(2)}, u32[]{:S(2)}) collective-permute-start(bf16[256,1024]{1,0:T(8,128)(2,1)S(1)} %add_convert_fusion.1), channel_id=1, source_target_pairs={{0,2},{1,3},{2,0},{3,1},{4,6},{5,7},{6,4},{7,5},{8,10},{9,11},{10,... | collective-permute-start | bytes 1572872 | tf_op jit(solution)/shard_map/ppermute | solution.py:746
  206.1 29.4 %collective-permute-start.26 = (bf16[128,768]{1,0:T(8,128)(2,1)}, bf16[128,768]{1,0:T(8,128)(2,1)}, u32[]{:S(2)}, u32[]{:S(2)}) collective-permute-start(bf16[128,768]{1,0:T(8,128)(2,1)} %get-tuple-element.133), channel_id=1, source_target_pairs={{0,24},{4,28},{8,16},{12,20},{16,8},{20,12},{24,0},{28,4},{1,25},{... | collective-permute-start | bytes 589832 | tf_op jit(solution)/shard_map/ppermute | solution.py:743
  207.4 33.8 %collective-permute-start.25 = (bf16[128,768]{1,0:T(8,128)(2,1)S(1)}, bf16[128,768]{1,0:T(8,128)(2,1)}, u32[]{:S(2)}, u32[]{:S(2)}) collective-permute-start(bf16[128,768]{1,0:T(8,128)(2,1)S(1)} %get-tuple-element.134), channel_id=1, source_target_pairs={{0,16},{4,20},{8,24},{12,28},{16,0},{20,4},{24,8},{28,12},{1,17},{... | collective-permute-start | bytes 589832 | tf_op jit(solution)/shard_map/ppermute | solution.py:743
  209.4 31.7 %collective-permute-start.24 = (bf16[128,768]{1,0:T(8,128)(2,1)S(1)}, bf16[128,768]{1,0:T(8,128)(2,1)}, u32[]{:S(2)}, u32[]{:S(2)}) collective-permute-start(bf16[128,768]{1,0:T(8,128)(2,1)S(1)} %get-tuple-element.135), channel_id=1, source_target_pairs={{0,8},{4,12},{8,0},{12,4},{16,24},{20,28},{24,16},{28,20},{1,9},{5... | collective-permute-start | bytes 589832 | tf_op jit(solution)/shard_map/ppermute | solution.py:743
  246.0 36.5 %collective-permute-start.29 = (bf16[576,1024]{1,0:T(8,128)(2,1)}, bf16[576,1024]{1,0:T(8,128)(2,1)S(1)}, u32[]{:S(2)}, u32[]{:S(2)}) collective-permute-start(bf16[576,1024]{1,0:T(8,128)(2,1)} %pad_maximum_fusion), channel_id=1, source_target_pairs={{0,4},{4,0},{8,12},{12,8},{16,20},{20,16},{24,28},{28,24},{1,5},{5... | collective-permute-start | bytes 3538952 | tf_op jit(solution)/shard_map/ppermute | solution.py:743
  249.2 33.4 %collective-permute-start.28 = (bf16[256,1024]{1,0:T(8,128)(2,1)S(1)}, bf16[256,1024]{1,0:T(8,128)(2,1)S(1)}, u32[]{:S(2)}, u32[]{:S(2)}) collective-permute-start(bf16[256,1024]{1,0:T(8,128)(2,1)S(1)} %add_convert_fusion), channel_id=1, source_target_pairs={{0,2},{1,3},{2,0},{3,1},{4,6},{5,7},{6,4},{7,5},{8,10},{9,11},{10,... | collective-permute-start | bytes 1572872 | tf_op jit(solution)/shard_map/ppermute | solution.py:746
  287.1 20.6 %collective-permute-start.33 = (bf16[144,1024]{1,0:T(8,128)(2,1)}, bf16[144,1024]{1,0:T(8,128)(2,1)S(1)}, u32[]{:S(2)}, u32[]{:S(2)}) collective-permute-start(bf16[144,1024]{1,0:T(8,128)(2,1)} %get-tuple-element.104), channel_id=1, source_target_pairs={{0,8},{4,12},{8,0},{12,4},{16,24},{20,28},{24,16},{28,20},{1,9},{5... | collective-permute-start | bytes 884744 | tf_op jit(solution)/shard_map/ppermute | solution.py:743
  292.1 18.5 %collective-permute-start.34 = (bf16[144,1024]{1,0:T(8,128)(2,1)}, bf16[144,1024]{1,0:T(8,128)(2,1)S(1)}, u32[]{:S(2)}, u32[]{:S(2)}) collective-permute-start(bf16[144,1024]{1,0:T(8,128)(2,1)} %get-tuple-element.105), channel_id=1, source_target_pairs={{0,16},{4,20},{8,24},{12,28},{16,0},{20,4},{24,8},{28,12},{1,17},{... | collective-permute-start | bytes 884744 | tf_op jit(solution)/shard_map/ppermute | solution.py:743
  292.1 30.9 %collective-permute-start.35 = (bf16[144,1024]{1,0:T(8,128)(2,1)}, bf16[144,1024]{1,0:T(8,128)(2,1)S(1)}, u32[]{:S(2)}, u32[]{:S(2)}) collective-permute-start(bf16[144,1024]{1,0:T(8,128)(2,1)} %get-tuple-element.106), channel_id=1, source_target_pairs={{0,24},{4,28},{8,16},{12,20},{16,8},{20,12},{24,0},{28,4},{1,25},{... | collective-permute-start | bytes 884744 | tf_op jit(solution)/shard_map/ppermute | solution.py:743
  (58 other events, 482.3 us)
Sparse Core Ops, SparseCore 0:
  58.9 79.2 all-gather.1
  198.0 106.2 reduce-scatter.1

commit v5 on v4

--- a/solution.py
+++ b/solution.py
@@ -861,7 +861,7 @@
         across = tie(far, attn_far, attn_near[1], attn_near[2])
         rows_all = [both, beside, far, links.over_tensor(across, 1)]
         w_attn = attn_near + [attn_far] + [links.over_dp(b, 1) for b in attn_near[1:]]
-        w_mlp = tie(w_mlp, (far, attn_far, attn_near[1:], w_attn[5], w_attn[6]))
+        w_mlp = tie(w_mlp, (far, attn_far, attn_near[1:], w_attn[5]))
         w_qkv, w_o, o_index = w_attn, w_attn, kv_heads * (group + 2) * HEAD // q_cols
         w_gu = w_d = lax.all_gather(w_mlp, "dp", axis=0, tiled=True)
         d_index = 2

time: 343 us -> 352 us (1.026)
  starting transfers between devices: 35.6 us -> 40.4 us
    ppermute x19, starting transfers between devices: 26.2 us -> 31.3 us  [over_dp(): return lax.ppermute(x, 'dp', xor_pairs(self.dp, bits))]
    ppermute x19, waiting for transfers between devices: 91 us -> 94.8 us  [over_dp(): return lax.ppermute(x, 'dp', xor_pairs(self.dp, bits))]
  transfers between devices with their start and end apart: 40 -> 40, of which waited for: 23 -> 20; matrix products, arithmetic and copies ran while one was open for 11% -> 11% of each run, Pallas kernels for 21% -> 20%
where the time goes in v5:
time: 352 us; the launch traced here: 348 us
  waiting for transfers between devices  147 us (42%)
  Pallas kernels  96.7 us (27%)
  starting transfers between devices  40.4 us (11%)
  matrix products  20.9 us (6%)
  other arithmetic  16.1 us (5%)
  between operations  14.8 us (4%)
  local copies, waits for them, and re-layouts  11.8 us (3%)
    ppermute x19, waiting for transfers between devices, over_dp(): return lax.ppermute(x, 'dp', xor_pairs(self.dp, bits))  94.8 us
    ppermute x19, waiting for transfers between devices, over_tensor(): return lax.ppermute(x, 'tensor', xor_pairs(self.tensor, bits))  51.9 us
    ppermute x19, starting transfers between devices, over_dp(): return lax.ppermute(x, 'dp', xor_pairs(self.dp, bits))  31.3 us
    pallas_call x1, Pallas kernels, attn_backward(): call(functools.partial(attn_backward_kernel, rows, n // rows, group, kv_h...  25.9 us
    dot_general x7, matrix products, mm(): lax.dot_general(a, b, (((ca,), (cb,)), ((), ())), preferred_element_type=...  20.9 us
    pallas_call x1, Pallas kernels, mlp_call(): call(functools.partial(mlp_kernel, ff, len(xs), reorder), (len(xs),), [wh...  20.5 us
    pallas_call x1, Pallas kernels, attn_forward(): call(functools.partial(attn_forward_kernel, rows, n // rows, group, kv_he...  12.9 us
    pallas_call x1, Pallas kernels, qkv_call(): call(functools.partial(qkv_kernel, len(xs), len(ws), packed_gains, kv_hea...  9.59 us
  transfers between devices with their start and end apart: 40, of which 20 were waited for; matrix products, arithmetic and copies ran while one was open for 11% of the time, Pallas kernels for 20%

profile of v5, /device:TPU:12, one launch (start us, length us, event | category | flops | bytes accessed | tf_op | source)
XLA Modules:
  0.0 347.6 jit_solution(7537054847388121635)
XLA Ops:
  20.1 8.2 %collective-permute-done.3.refs_5_.refs_1_.refs_18_.refs_26_ = bf16[144,1536]{1,0:T(8,128)(2,1)S(1)} collective-permute-done((bf16[144,1536]{1,0:T(8,128)(2,1)S(1)}, bf16[144,1536]{1,0:T(8,128)(2,1)S(1)}, u32[]{:S(2)}, u32[]{:S(2)}) %collective-permute-start.3) | collective-permute-done | bytes 442400 | tf_op jit(solution)/shard_map/ppermute | solution.py:743
  31.5 16.9 %collective-permute-done.6.refs_7_.refs_3_.refs_20_.refs_28_ = bf16[144,1536]{1,0:T(8,128)(2,1)S(1)} collective-permute-done((bf16[144,1536]{1,0:T(8,128)(2,1)S(1)}, bf16[144,1536]{1,0:T(8,128)(2,1)S(1)}, u32[]{:S(2)}, u32[]{:S(2)}) %collective-permute-start.6) | collective-permute-done | bytes 442400 | tf_op jit(solution)/shard_map/ppermute | solution.py:743
  48.3 7.3 %collective-permute-done.4.refs_6_.refs_2_.refs_19_.refs_27_ = bf16[144,1536]{1,0:T(8,128)(2,1)S(1)} collective-permute-done((bf16[144,1536]{1,0:T(8,128)(2,1)S(1)}, bf16[144,1536]{1,0:T(8,128)(2,1)S(1)}, u32[]{:S(2)}, u32[]{:S(2)}) %collective-permute-start.4) | collective-permute-done | bytes 442400 | tf_op jit(solution)/shard_map/ppermute | solution.py:743
  63.3 10.1 %collective-permute-done.9.refs_11_.refs_7_.refs_24_.refs_32_ = bf16[144,1536]{1,0:T(8,128)(2,1)} collective-permute-done((bf16[144,1536]{1,0:T(8,128)(2,1)S(1)}, bf16[144,1536]{1,0:T(8,128)(2,1)}, u32[]{:S(2)}, u32[]{:S(2)}) %collective-permute-start.9) | collective-permute-done | bytes 442400 | tf_op jit(solution)/shard_map/ppermute | solution.py:743
  73.4 11.6 %collective-permute-done.8.refs_10_.refs_6_.refs_23_.refs_31_ = bf16[144,1536]{1,0:T(8,128)(2,1)} collective-permute-done((bf16[144,1536]{1,0:T(8,128)(2,1)S(1)}, bf16[144,1536]{1,0:T(8,128)(2,1)}, u32[]{:S(2)}, u32[]{:S(2)}) %collective-permute-start.8) | collective-permute-done | bytes 442400 | tf_op jit(solution)/shard_map/ppermute | solution.py:743
  85.9 9.6 %shard_map.248 = (bf16[1024,1024]{1,0:T(8,128)(2,1)}, bf16[1024,1024]{1,0:T(8,128)(2,1)}, f32[1024,768]{1,0:T(8,128)}, f32[8,1024]{1,0:T(8,128)}) custom-call(s32[2]{0:T(128)} %pad_add_fusion.t, bf16[256,2048]{1,0:T(8,128)(2,1)} %shard_map.247.refs_0_.refs_3_.refs_4_.refs_13_, bf16[256,2048]{1,0:T(8,128)(2,1)} %copy-done.2, bf16[256,2048]{1,0:T(8,128)(2,1)} %copy-done.1, ...), custom_call_target="tpu_custom_call" | custom-call | flops 1 | bytes 1 | tf_op jit(solution)/shard_map/pallas_call | solution.py:210
  95.5 12.9 %shard_map.249 = (bf16[1024,512]{1,0:T(8,128)(2,1)}, f32[2,8,1024]{2,1,0:T(8,128)}, bf16[512,1024]{1,0:T(8,128)(2,1)}, bf16[512,1024]{1,0:T(8,128)(2,1)}) custom-call(s32[2]{0:T(128)} %pad_add_fusion.t, bf16[1024,1024]{1,0:T(8,128)(2,1)} %get-tuple-element.62.packed.refs_0_, s32[1024,1]{1,0:T(8,128)} %copy.30.seg_col.refs_1_, s32[1,1024]{1,0:T(1,128)} %refs_2_.1, ...), custom_call_target="tpu_custom_call" | custom-call | flops 1 | bytes 1 | tf_op jit(solution)/shard_map/pallas_call | solution.py:296
  113.7 13.2 %collective-permute-done.11.refs_2_ = bf16[256,1024]{1,0:T(8,128)(2,1)S(1)} collective-permute-done((bf16[256,1024]{1,0:T(8,128)(2,1)S(1)}, bf16[256,1024]{1,0:T(8,128)(2,1)S(1)}, u32[]{:S(2)}, u32[]{:S(2)}) %collective-permute-start.11) | collective-permute-done | bytes 524320 | tf_op jit(solution)/shard_map/ppermute | solution.py:746
  127.7 3.6 %shard_map.250 = (f32[256,1024]{1,0:T(8,128)}, bf16[256,1024]{1,0:T(8,128)(2,1)}) custom-call(s32[2]{0:T(128)} %pad_add_fusion.t, bf16[512,1024]{1,0:T(8,128)(2,1)} %get-tuple-element.63.refs_0_, bf16[512,1024]{1,0:T(8,128)(2,1)} %copy-done.13, bf16[256,1024]{1,0:T(8,128)(2,1)} %copy-done.34, bf16[256,2048]{1,0:T(8,128)(2,1)} %shard_map.247.refs_0_.refs_3_.refs_4_.refs_13_, ...), custom_call_target="tpu_custom_call" | custom-call | flops 1 | bytes 1 | tf_op jit(solution)/shard_map/pallas_call | solution.py:600
  132.1 12.7 %collective-permute-done.13.refs_2_ = bf16[256,1024]{1,0:T(8,128)(2,1)S(1)} collective-permute-done((bf16[256,1024]{1,0:T(8,128)(2,1)}, bf16[256,1024]{1,0:T(8,128)(2,1)S(1)}, u32[]{:S(2)}, u32[]{:S(2)}) %collective-permute-start.13) | collective-permute-done | bytes 524320 | tf_op jit(solution)/shard_map/ppermute | solution.py:746
  147.5 20.5 %shard_map.252 = (bf16[1024,768]{1,0:T(8,128)(2,1)}, bf16[1024,1536]{1,0:T(8,128)(2,1)}, bf16[1024,1024]{1,0:T(8,128)(2,1)}, bf16[1024,1024]{1,0:T(8,128)(2,1)},...) custom-call(s32[2]{0:T(128)} %pad_add_fusion.t, ...), custom_call_target="tpu_custom_call" | custom-call | flops 1 | bytes 1 | tf_op jit(solution)/shard_map/pallas_call | solution.py:558
  176.6 9.9 %collective-permute-done.16.refs_2_ = bf16[256,1024]{1,0:T(8,128)(2,1)S(1)} collective-permute-done((bf16[256,1024]{1,0:T(8,128)(2,1)S(1)}, bf16[256,1024]{1,0:T(8,128)(2,1)S(1)}, u32[]{:S(2)}, u32[]{:S(2)}) %collective-permute-start.16) | collective-permute-done | bytes 524320 | tf_op jit(solution)/shard_map/ppermute | solution.py:746
  187.4 4.4 %shard_map.253 = (f32[256,1024]{1,0:T(8,128)}, bf16[256,1024]{1,0:T(8,128)(2,1)}, f32[8,1024]{1,0:T(8,128)}) custom-call(s32[2]{0:T(128)} %pad_add_fusion.t, bf16[512,1024]{1,0:T(8,128)(2,1)} %get-tuple-element.71.refs_0_, bf16[512,1024]{1,0:T(8,128)(2,1)} %copy-done.10, bf16[256,1024]{1,0:T(8,128)(2,1)} %copy-done.30, ...), custom_call_target="tpu_custom_call" | custom-call | flops 1 | bytes 1 | tf_op jit(solution)/shard_map/pallas_call | solution.py:629
  192.4 7.6 %convolution_convert_fusion = bf16[1024,1536]{1,0:T(8,128)(2,1)} fusion(bf16[1024,1024]{1,0:T(8,128)(2,1)} %get-tuple-element.75, bf16[1024,1536]{1,0:T(8,128)(2,1)} %get-tuple-element.77), kind=kOutput, calls=%fused_computation | convolution fusion | flops 3222798336 | bytes 8388608 | tf_op jit(solution)/shard_map/dot_general | solution.py:24
  200.0 5.1 %collective-permute-done.18.refs_11_ = bf16[256,1024]{1,0:T(8,128)(2,1)S(1)} collective-permute-done((bf16[256,1024]{1,0:T(8,128)(2,1)}, bf16[256,1024]{1,0:T(8,128)(2,1)S(1)}, u32[]{:S(2)}, u32[]{:S(2)}) %collective-permute-start.18) | collective-permute-done | bytes 524320 | tf_op jit(solution)/shard_map/ppermute | solution.py:746
  213.8 3.8 %collective-permute-start.25 = (bf16[128,768]{1,0:T(8,128)(2,1)S(1)}, bf16[128,768]{1,0:T(8,128)(2,1)}, u32[]{:S(2)}, u32[]{:S(2)}) collective-permute-start(bf16[128,768]{1,0:T(8,128)(2,1)S(1)} %get-tuple-element.134), channel_id=1, source_target_pairs={{0,16},{4,20},{8,24},{12,28},{16,0},{20,4},{24,8},{28,12},{1,17},{... | collective-permute-start | bytes 589832 | tf_op jit(solution)/shard_map/ppermute | solution.py:743
  218.0 25.9 %shard_map.255 = (bf16[1024,1024]{1,0:T(8,128)(2,1)}, f32[2,8,128]{2,1,0:T(8,128)}, bf16[512,1024]{1,0:T(8,128)(2,1)}, bf16[512,1024]{1,0:T(8,128)(2,1)}, f32[8,...) custom-call(s32[2]{0:T(128)} %pad_add_fusion.t, ...), custom_call_target="tpu_custom_call" | custom-call | flops 1 | bytes 1 | tf_op jit(solution)/shard_map/pallas_call | solution.py:452
  260.8 5.3 %collective-permute-start.31 = (bf16[128,512]{1,0:T(8,128)(2,1)S(1)}, bf16[128,512]{1,0:T(8,128)(2,1)S(1)}, u32[]{:S(2)}, u32[]{:S(2)}) collective-permute-start(bf16[128,512]{1,0:T(8,128)(2,1)S(1)} %get-tuple-element.137), channel_id=1, source_target_pairs={{0,16},{4,20},{8,24},{12,28},{16,0},{20,4},{24,8},{28,12},{1,17},{... | collective-permute-start | bytes 393224 | tf_op jit(solution)/shard_map/ppermute | solution.py:743
  268.4 4.9 %collective-permute-done.31 = bf16[128,512]{1,0:T(8,128)(2,1)S(1)} collective-permute-done((bf16[128,512]{1,0:T(8,128)(2,1)S(1)}, bf16[128,512]{1,0:T(8,128)(2,1)S(1)}, u32[]{:S(2)}, u32[]{:S(2)}) %collective-permute-start.31) | collective-permute-done | bytes 131104 | tf_op jit(solution)/shard_map/ppermute | solution.py:743
  273.3 15.5 %collective-permute-done.29.got = bf16[576,1024]{1,0:T(8,128)(2,1)S(1)} collective-permute-done((bf16[576,1024]{1,0:T(8,128)(2,1)}, bf16[576,1024]{1,0:T(8,128)(2,1)S(1)}, u32[]{:S(2)}, u32[]{:S(2)}) %collective-permute-start.29) | collective-permute-done | bytes 1179680 | tf_op jit(solution)/shard_map/ppermute | solution.py:743
  289.8 3.6 %shard_map.257 = (f32[144,1024]{1,0:T(8,128)}, bf16[144,1024]{1,0:T(8,128)(2,1)}, bf16[144,1024]{1,0:T(8,128)(2,1)}, bf16[144,1024]{1,0:T(8,128)(2,1)}) custom-call(s32[2]{0:T(128)} %pad_add_fusion.t, bf16[512,1024]{1,0:T(8,128)(2,1)} %convolution_convert_fusion.2.keep, bf16[64,1024]{1,0:T(8,128)(2,1)} %get-tuple-element.97.rows, bf16[576,1024]{1,0:T(8,128)(2,1)} %copy-done.20), custom_call_target="tpu_custom_call" | custom-call | flops 1 | bytes 1 | tf_op jit(solution)/shard_map/pallas_call | solution.py:721
  293.4 6.9 %collective-permute-start.33 = (bf16[144,1024]{1,0:T(8,128)(2,1)}, bf16[144,1024]{1,0:T(8,128)(2,1)S(1)}, u32[]{:S(2)}, u32[]{:S(2)}) collective-permute-start(bf16[144,1024]{1,0:T(8,128)(2,1)} %get-tuple-element.104), channel_id=1, source_target_pairs={{0,8},{4,12},{8,0},{12,4},{16,24},{20,28},{24,16},{28,20},{1,9},{5... | collective-permute-start | bytes 884744 | tf_op jit(solution)/shard_map/ppermute | solution.py:743
  309.4 4.3 %shard_map.256 = f32[256,1024]{1,0:T(8,128)} custom-call(s32[2]{0:T(128)} %pad_add_fusion.t, bf16[512,1024]{1,0:T(8,128)(2,1)} %get-tuple-element.92.refs_0_, bf16[512,1024]{1,0:T(8,128)(2,1)} %copy-done.12, bf16[256,1024]{1,0:T(8,128)(2,1)} %copy-done.26, bf16[256,2048]{1,0:T(8,128)(2,1)} %shard_map.247.refs_0_.refs_3_.refs_4_.refs_13_, ...), custom_call_target="tpu_custom_call" | custom-call | flops 1 | bytes 1 | tf_op jit(solution)/shard_map/pallas_call | solution.py:674
  318.7 12.8 %collective-permute-done.35 = bf16[144,1024]{1,0:T(8,128)(2,1)S(1)} collective-permute-done((bf16[144,1024]{1,0:T(8,128)(2,1)}, bf16[144,1024]{1,0:T(8,128)(2,1)S(1)}, u32[]{:S(2)}, u32[]{:S(2)}) %collective-permute-start.35) | collective-permute-done | bytes 294944 | tf_op jit(solution)/shard_map/ppermute | solution.py:743
  (196 shorter events, 96.5 us)
Async XLA Ops:
  7.2 139.5 %all-gather.2.cloned.1.call-start = ((), (), s32[]{:S(2)}) async-start(), calls=%async_computation.1 | async-start | bytes 5308416 | tf_op jit(solution)/shard_map/all_gather | solution.py:866
  13.7 41.9 %collective-permute-start.1 = (bf16[256,2048]{1,0:T(8,128)(2,1)}, bf16[256,2048]{1,0:T(8,128)(2,1)S(1)}, u32[]{:S(2)}, u32[]{:S(2)}) collective-permute-start(bf16[256,2048]{1,0:T(8,128)(2,1)} %shard_map.247.refs_0_.refs_3_.refs_4_.refs_13_), channel_id=1, source_target_pairs={{0,2},{1,3},{2,0},{3,1},{4,6},{5,7},{6,4},{7,5},{8,10},{9,11},{10,... | collective-permute-start | bytes 3145736 | tf_op jit(solution)/shard_map/ppermute | solution.py:746
  15.6 32.7 %collective-permute-start.6 = (bf16[144,1536]{1,0:T(8,128)(2,1)S(1)}, bf16[144,1536]{1,0:T(8,128)(2,1)S(1)}, u32[]{:S(2)}, u32[]{:S(2)}) collective-permute-start(bf16[144,1536]{1,0:T(8,128)(2,1)S(1)} %copy-done), channel_id=1, source_target_pairs={{0,24},{4,28},{8,16},{12,20},{16,8},{20,12},{24,0},{28,4},{1,25},{... | collective-permute-start | bytes 1327112 | tf_op jit(solution)/shard_map/ppermute | solution.py:743
  18.3 37.3 %collective-permute-start.4 = (bf16[144,1536]{1,0:T(8,128)(2,1)S(1)}, bf16[144,1536]{1,0:T(8,128)(2,1)S(1)}, u32[]{:S(2)}, u32[]{:S(2)}) collective-permute-start(bf16[144,1536]{1,0:T(8,128)(2,1)S(1)} %copy-done), channel_id=1, source_target_pairs={{0,16},{4,20},{8,24},{12,28},{16,0},{20,4},{24,8},{28,12},{1,17},{... | collective-permute-start | bytes 1327112 | tf_op jit(solution)/shard_map/ppermute | solution.py:743
  19.6 36.0 %collective-permute-start.2 = (bf16[144,1536]{1,0:T(8,128)(2,1)S(1)}, bf16[144,1536]{1,0:T(8,128)(2,1)S(1)}, u32[]{:S(2)}, u32[]{:S(2)}) collective-permute-start(bf16[144,1536]{1,0:T(8,128)(2,1)S(1)} %copy-done), channel_id=1, source_target_pairs={{0,4},{4,0},{8,12},{12,8},{16,20},{20,16},{24,28},{28,24},{1,5},{5... | collective-permute-start | bytes 1327112 | tf_op jit(solution)/shard_map/ppermute | solution.py:743
  28.2 27.4 %collective-permute-start.7 = (bf16[144,1536]{1,0:T(8,128)(2,1)S(1)}, bf16[144,1536]{1,0:T(8,128)(2,1)}, u32[]{:S(2)}, u32[]{:S(2)}) collective-permute-start(bf16[144,1536]{1,0:T(8,128)(2,1)S(1)} %collective-permute-done.3.refs_5_.refs_1_.refs_18_.refs_26_), channel_id=1, source_target_pairs={{0,4},{4,0},{8,12},{12,8},{16,20},{20,16},{24,28},{28,24},{1,5},{5... | collective-permute-start | bytes 1327112 | tf_op jit(solution)/shard_map/ppermute | solution.py:743
  56.4 282.1 %reduce-scatter.2.cloned.1.call-start = ((), (), s32[]{:S(2)}) async-start(), calls=%async_computation.2 | async-start | bytes 3538944 | tf_op jit(solution)/shard_map/reduce_scatter | solution.py:905
  56.4 28.5 %collective-permute-start = (bf16[256,2048]{1,0:T(8,128)(2,1)}, bf16[256,2048]{1,0:T(8,128)(2,1)S(1)}, u32[]{:S(2)}, u32[]{:S(2)}) collective-permute-start(bf16[256,2048]{1,0:T(8,128)(2,1)} %shard_map.247.refs_0_.refs_3_.refs_4_.refs_13_), channel_id=1, source_target_pairs={{0,1},{1,0},{2,3},{3,2},{4,5},{5,4},{6,7},{7,6},{8,9},{9,8},{10,11... | collective-permute-start | bytes 3145736 | tf_op jit(solution)/shard_map/ppermute | solution.py:746
  56.4 28.5 %collective-permute-start.5 = (bf16[256,2048]{1,0:T(8,128)(2,1)S(1)}, bf16[256,2048]{1,0:T(8,128)(2,1)}, u32[]{:S(2)}, u32[]{:S(2)}) collective-permute-start(bf16[256,2048]{1,0:T(8,128)(2,1)S(1)} %collective-permute-done.1.refs_2_.refs_6_.refs_15_), channel_id=1, source_target_pairs={{0,1},{1,0},{2,3},{3,2},{4,5},{5,4},{6,7},{7,6},{8,9},{9,8},{10,11... | collective-permute-start | bytes 3145736 | tf_op jit(solution)/shard_map/ppermute | solution.py:746
  57.0 16.4 %collective-permute-start.9 = (bf16[144,1536]{1,0:T(8,128)(2,1)S(1)}, bf16[144,1536]{1,0:T(8,128)(2,1)}, u32[]{:S(2)}, u32[]{:S(2)}) collective-permute-start(bf16[144,1536]{1,0:T(8,128)(2,1)S(1)} %collective-permute-done.6.refs_7_.refs_3_.refs_20_.refs_28_), channel_id=1, source_target_pairs={{0,4},{4,0},{8,12},{12,8},{16,20},{20,16},{24,28},{28,24},{1,5},{5... | collective-permute-start | bytes 1327112 | tf_op jit(solution)/shard_map/ppermute | solution.py:743
  57.5 27.4 %collective-permute-start.8 = (bf16[144,1536]{1,0:T(8,128)(2,1)S(1)}, bf16[144,1536]{1,0:T(8,128)(2,1)}, u32[]{:S(2)}, u32[]{:S(2)}) collective-permute-start(bf16[144,1536]{1,0:T(8,128)(2,1)S(1)} %collective-permute-done.4.refs_6_.refs_2_.refs_19_.refs_27_), channel_id=1, source_target_pairs={{0,4},{4,0},{8,12},{12,8},{16,20},{20,16},{24,28},{28,24},{1,5},{5... | collective-permute-start | bytes 1327112 | tf_op jit(solution)/shard_map/ppermute | solution.py:743
  112.9 14.0 %collective-permute-start.11 = (bf16[256,1024]{1,0:T(8,128)(2,1)S(1)}, bf16[256,1024]{1,0:T(8,128)(2,1)S(1)}, u32[]{:S(2)}, u32[]{:S(2)}) collective-permute-start(bf16[256,1024]{1,0:T(8,128)(2,1)S(1)} %add_convert_fusion.3), channel_id=1, source_target_pairs={{0,2},{1,3},{2,0},{3,1},{4,6},{5,7},{6,4},{7,5},{8,10},{9,11},{10,... | collective-permute-start | bytes 1572872 | tf_op jit(solution)/shard_map/ppermute | solution.py:746
  172.5 14.1 %collective-permute-start.16 = (bf16[256,1024]{1,0:T(8,128)(2,1)S(1)}, bf16[256,1024]{1,0:T(8,128)(2,1)S(1)}, u32[]{:S(2)}, u32[]{:S(2)}) collective-permute-start(bf16[256,1024]{1,0:T(8,128)(2,1)S(1)} %add_convert_fusion.2), channel_id=1, source_target_pairs={{0,2},{1,3},{2,0},{3,1},{4,6},{5,7},{6,4},{7,5},{8,10},{9,11},{10,... | collective-permute-start | bytes 1572872 | tf_op jit(solution)/shard_map/ppermute | solution.py:746
  176.0 24.0 %collective-permute-start.19 = (bf16[512,768]{1,0:T(8,128)(2,1)S(1)}, bf16[512,768]{1,0:T(8,128)(2,1)S(1)}, u32[]{:S(2)}, u32[]{:S(2)}) collective-permute-start(bf16[512,768]{1,0:T(8,128)(2,1)S(1)} %convolution_convert_fusion.4), channel_id=1, source_target_pairs={{0,4},{4,0},{8,12},{12,8},{16,20},{20,16},{24,28},{28,24},{1,5},{5... | collective-permute-start | bytes 2359304 | tf_op jit(solution)/shard_map/ppermute | solution.py:743
  210.0 36.5 %collective-permute-start.23 = (bf16[512,512]{1,0:T(8,128)(2,1)}, bf16[512,512]{1,0:T(8,128)(2,1)S(1)}, u32[]{:S(2)}, u32[]{:S(2)}) collective-permute-start(bf16[512,512]{1,0:T(8,128)(2,1)} %convolution_convert_fusion.6), channel_id=1, source_target_pairs={{0,4},{4,0},{8,12},{12,8},{16,20},{20,16},{24,28},{28,24},{1,5},{5... | collective-permute-start | bytes 1572872 | tf_op jit(solution)/shard_map/ppermute | solution.py:743
  210.6 35.9 %collective-permute-start.22 = (bf16[256,1024]{1,0:T(8,128)(2,1)S(1)}, bf16[256,1024]{1,0:T(8,128)(2,1)S(1)}, u32[]{:S(2)}, u32[]{:S(2)}) collective-permute-start(bf16[256,1024]{1,0:T(8,128)(2,1)S(1)} %add_convert_fusion.1), channel_id=1, source_target_pairs={{0,2},{1,3},{2,0},{3,1},{4,6},{5,7},{6,4},{7,5},{8,10},{9,11},{10,... | collective-permute-start | bytes 1572872 | tf_op jit(solution)/shard_map/ppermute | solution.py:746
  213.4 30.5 %collective-permute-start.26 = (bf16[128,768]{1,0:T(8,128)(2,1)}, bf16[128,768]{1,0:T(8,128)(2,1)}, u32[]{:S(2)}, u32[]{:S(2)}) collective-permute-start(bf16[128,768]{1,0:T(8,128)(2,1)} %get-tuple-element.133), channel_id=1, source_target_pairs={{0,24},{4,28},{8,16},{12,20},{16,8},{20,12},{24,0},{28,4},{1,25},{... | collective-permute-start | bytes 589832 | tf_op jit(solution)/shard_map/ppermute | solution.py:743
  213.8 32.7 %collective-permute-start.25 = (bf16[128,768]{1,0:T(8,128)(2,1)S(1)}, bf16[128,768]{1,0:T(8,128)(2,1)}, u32[]{:S(2)}, u32[]{:S(2)}) collective-permute-start(bf16[128,768]{1,0:T(8,128)(2,1)S(1)} %get-tuple-element.134), channel_id=1, source_target_pairs={{0,16},{4,20},{8,24},{12,28},{16,0},{20,4},{24,8},{28,12},{1,17},{... | collective-permute-start | bytes 589832 | tf_op jit(solution)/shard_map/ppermute | solution.py:743
  217.6 28.9 %collective-permute-start.24 = (bf16[128,768]{1,0:T(8,128)(2,1)S(1)}, bf16[128,768]{1,0:T(8,128)(2,1)}, u32[]{:S(2)}, u32[]{:S(2)}) collective-permute-start(bf16[128,768]{1,0:T(8,128)(2,1)S(1)} %get-tuple-element.135), channel_id=1, source_target_pairs={{0,8},{4,12},{8,0},{12,4},{16,24},{20,28},{24,16},{28,20},{1,9},{5... | collective-permute-start | bytes 589832 | tf_op jit(solution)/shard_map/ppermute | solution.py:743
  251.4 37.4 %collective-permute-start.29 = (bf16[576,1024]{1,0:T(8,128)(2,1)}, bf16[576,1024]{1,0:T(8,128)(2,1)S(1)}, u32[]{:S(2)}, u32[]{:S(2)}) collective-permute-start(bf16[576,1024]{1,0:T(8,128)(2,1)} %pad_maximum_fusion), channel_id=1, source_target_pairs={{0,4},{4,0},{8,12},{12,8},{16,20},{20,16},{24,28},{28,24},{1,5},{5... | collective-permute-start | bytes 3538952 | tf_op jit(solution)/shard_map/ppermute | solution.py:743
  256.5 32.3 %collective-permute-start.28 = (bf16[256,1024]{1,0:T(8,128)(2,1)S(1)}, bf16[256,1024]{1,0:T(8,128)(2,1)S(1)}, u32[]{:S(2)}, u32[]{:S(2)}) collective-permute-start(bf16[256,1024]{1,0:T(8,128)(2,1)S(1)} %add_convert_fusion), channel_id=1, source_target_pairs={{0,2},{1,3},{2,0},{3,1},{4,6},{5,7},{6,4},{7,5},{8,10},{9,11},{10,... | collective-permute-start | bytes 1572872 | tf_op jit(solution)/shard_map/ppermute | solution.py:746
  293.4 22.3 %collective-permute-start.33 = (bf16[144,1024]{1,0:T(8,128)(2,1)}, bf16[144,1024]{1,0:T(8,128)(2,1)S(1)}, u32[]{:S(2)}, u32[]{:S(2)}) collective-permute-start(bf16[144,1024]{1,0:T(8,128)(2,1)} %get-tuple-element.104), channel_id=1, source_target_pairs={{0,8},{4,12},{8,0},{12,4},{16,24},{20,28},{24,16},{28,20},{1,9},{5... | collective-permute-start | bytes 884744 | tf_op jit(solution)/shard_map/ppermute | solution.py:743
  300.2 18.5 %collective-permute-start.34 = (bf16[144,1024]{1,0:T(8,128)(2,1)}, bf16[144,1024]{1,0:T(8,128)(2,1)S(1)}, u32[]{:S(2)}, u32[]{:S(2)}) collective-permute-start(bf16[144,1024]{1,0:T(8,128)(2,1)} %get-tuple-element.105), channel_id=1, source_target_pairs={{0,16},{4,20},{8,24},{12,28},{16,0},{20,4},{24,8},{28,12},{1,17},{... | collective-permute-start | bytes 884744 | tf_op jit(solution)/shard_map/ppermute | solution.py:743
  300.2 31.3 %collective-permute-start.35 = (bf16[144,1024]{1,0:T(8,128)(2,1)}, bf16[144,1024]{1,0:T(8,128)(2,1)S(1)}, u32[]{:S(2)}, u32[]{:S(2)}) collective-permute-start(bf16[144,1024]{1,0:T(8,128)(2,1)} %get-tuple-element.106), channel_id=1, source_target_pairs={{0,24},{4,28},{8,16},{12,20},{16,8},{20,12},{24,0},{28,4},{1,25},{... | collective-permute-start | bytes 884744 | tf_op jit(solution)/shard_map/ppermute | solution.py:743
  (58 other events, 489.8 us)
Sparse Core Ops, SparseCore 0:
  55.8 81.8 all-gather.1
  207.3 105.8 reduce-scatter.1
